TPU v7x, 32 devices: a whole 2x2x4 slice. The times are simulated.
32 devices in a mesh: frame: 8 (over y, x, core), space: 4 (over z).
Axes of the slice: x: 2, y: 2, z: 4, core: 2. Of those that a mesh axis runs over, the one named last changes fastest.
Arguments:
- grad_out: bfloat16 [16, 880, 2240], P('frame', 'space'), may hold values from -6 to 6
- conv_taps: float32 [3, 2240], replicated, may hold values from -3 to 3
- saved_queries: bfloat16 [16, 880, 2240], P('frame', 'space'), may hold values from -6 to 6
- saved_keys: bfloat16 [16, 880, 2240], P('frame', 'space'), may hold values from -30 to 30
- saved_values: bfloat16 [16, 880, 2240], P('frame', 'space'), may hold values from -8 to 8
Outputs:
- grad_queries: bfloat16 [16, 880, 2240], P('frame', 'space')
- grad_keys: bfloat16 [16, 880, 2240], P('frame', 'space')
- grad_values: bfloat16 [16, 880, 2240], P('frame', 'space')
All inputs are finite; a program needn't handle non-finite values.
Results may differ from a plain program's by a relative error of at most 0.015.
Values may be sent and summed in bfloat16 or wider, within the bound.
No kernel may reach another device: no remote copies, remote signals or barrier semaphores. Data moves between devices by JAX's collectives and lax.ppermute only.
A program may use at most 128 MiB of HBM per device.

v0:
```python
import functools
import math

import jax
import jax.numpy as jnp
from jax import lax
from jax.experimental import pallas as pl
from jax.experimental.pallas import tpu as pltpu
from jax.sharding import PartitionSpec as P

H = 20
E = 112
EPSILON = 1e-06
LANES = 128
SPAN = 256
ROWS = 14
PARTS = E // ROWS
COPY = 32
F32, BF16 = jnp.float32, jnp.bfloat16
PARAMS = pltpu.CompilerParams(vmem_limit_bytes=48 << 20)


def spans(width):
    blocks = []
    for start in range(0, width, SPAN):
        stop = min(start + SPAN, width)
        first, last = start // E, (stop - 1) // E
        low = first * E // LANES * LANES
        high = min(-(-(last + 1) * E // LANES) * LANES, width)
        blocks.append((start, stop, low, high, range(first, last + 1)))
    return blocks


def dot(a, b, contract):
    return lax.dot_general(a, b, ((contract[:1], contract[1:]), ((), ())), preferred_element_type=F32)


def head_of_lane(rows, start, stop):
    return (lax.broadcasted_iota(jnp.int32, (rows, stop - start), 1) + start) // E


def picks(start, stop):
    row = lax.broadcasted_iota(jnp.int32, (LANES, stop - start), 0)
    return (row % COPY == head_of_lane(LANES, start, stop)) & (row < 3 * COPY)


def split(x):
    high = x.astype(BF16)
    return high, (x - high.astype(F32)).astype(BF16)


def add_outer(state, left, right):
    for start, stop, low, high, heads in spans(left.shape[1]):
        product = dot(left[:, low:high], right[:, start:stop], (0, 0))
        owner = head_of_lane(E, start, stop)
        part = jnp.zeros((E, stop - start), F32)
        for h in heads:
            part = jnp.where(owner == h, product[h * E - low : (h + 1) * E - low], part)
        state[:, start:stop] += part


def write_messages(rank, state, total, sorted_ref, out_refs):
    high, low = split(total)
    for part in range(PARTS):
        rows = state[part * ROWS : (part + 1) * ROWS, :]
        sorted_ref[part] = jnp.concatenate([rows, high.astype(F32), low.astype(F32)], 0)
    for d, out in enumerate(out_refs):
        out[...] = sorted_ref[rank ^ d].astype(BF16)


def load_state(messages, state):
    for part in range(PARTS):
        state[part * ROWS : (part + 1) * ROWS, :] = messages[part].astype(F32)[:ROWS]


def read_totals(messages):
    rows = messages[0].astype(F32)
    return rows[ROWS : ROWS + 1], rows[ROWS + 1 : ROWS + 2]


def columns_of(state, block):
    start, stop, low, high, heads = block
    owner = head_of_lane(E, start, stop)
    rows = [jnp.where(owner == h, state[:, start:stop], 0.0) for h in heads]
    before, after = heads[0] * E - low, high - (heads[-1] + 1) * E
    if before > 0:
        rows = [jnp.zeros((before, stop - start), F32)] + rows
    if after > 0:
        rows = rows + [jnp.zeros((after, stop - start), F32)]
    return jnp.concatenate(rows, 0).astype(BF16)


def rows_of(state, block):
    start, stop, low, high, heads = block
    owner = head_of_lane(E, low, high)
    rows = []
    for h in heads:
        first, last = max(start - h * E, 0), min(stop - h * E, E)
        rows.append(jnp.where(owner[first:last] == h, state[first:last, low:high], 0.0))
    return jnp.concatenate(rows, 0).astype(BF16)


def key_kernel(rank_ref, keys_ref, values_ref, *refs):
    out_refs, (state, total, sorted_ref) = refs[:PARTS], refs[PARTS:]
    frame = pl.program_id(0)

    @pl.when(frame == 0)
    def _():
        state[...] = jnp.zeros_like(state)
        total[...] = jnp.zeros_like(total)

    feat = jnp.maximum(keys_ref[0], 0)
    add_outer(state, feat, values_ref[0])
    total[...] += dot(jnp.ones((8, feat.shape[0]), BF16), feat, (1, 0))

    @pl.when(frame == pl.num_programs(0) - 1)
    def _():
        write_messages(rank_ref[0], state[...], total[:1], sorted_ref, out_refs)


def sum_kernel(*refs):
    in_refs, out_ref = refs[:-1], refs[-1]
    added = in_refs[0][...].astype(F32)
    for ref in in_refs[1:]:
        added = added + ref[...].astype(F32)
    high, low = split(added[ROWS : ROWS + 1] + added[ROWS + 1 : ROWS + 2])
    row = lax.broadcasted_iota(jnp.int32, added.shape, 0)
    added = jnp.where(row == ROWS, high.astype(F32), added)
    added = jnp.where(row == ROWS + 1, low.astype(F32), added)
    out_ref[...] = added.astype(BF16)


def query_kernel(rank_ref, queries_ref, grad_ref, next_ref, taps_ref, messages_ref, *refs):
    numer_ref, denom_ref, *refs = refs
    out_refs, (state, total, sorted_ref, wide) = refs[:PARTS], refs[PARTS:]
    frames, tokens, width = queries_ref.shape
    load_state(messages_ref, state)
    tot_high, tot_low = read_totals(messages_ref)
    blocks = spans(width)
    taps = taps_ref[...]
    taps = [taps[0:1] + 1.0, taps[1:2], taps[2:3]]
    for i, block in enumerate(blocks):
        wide[i, : block[3] - block[2], : block[1] - block[0]] = columns_of(state, block)
    state[...] = jnp.zeros_like(state)
    total[...] = jnp.zeros_like(total)
    lane = lax.broadcasted_iota(jnp.int32, (tokens, LANES), 1)

    def frame_step(frame, following):
        feat = jnp.maximum(queries_ref[frame], 0)
        denominator = jnp.full((tokens, LANES), EPSILON, F32)
        for start, stop, *_ in blocks:
            pick = picks(start, stop)
            for tot in (tot_high, tot_low):
                weights = jnp.where(pick, tot[:, start:stop], 0.0).astype(BF16)
                denominator += dot(feat[:, start:stop], weights, (1, 1))
        inverse = jnp.where(lane % COPY < H, 1.0 / denominator, 0.0)
        high, rest = split(inverse)
        middle, low = split(inverse - high.astype(F32))
        spread = jnp.where(lane < COPY, high.astype(F32), jnp.where(lane < 2 * COPY, middle.astype(F32), low_part(inverse, high, middle)))
        spread = jnp.where(lane < 3 * COPY, spread, 0.0).astype(BF16)
        summed = jnp.zeros((tokens, LANES), F32)
        for i, (start, stop, low_lane, high_lane, _) in enumerate(blocks):
            pick = jnp.where(picks(start, stop), 1.0, 0.0).astype(BF16)
            upstream = grad_ref[frame, :, start:stop].astype(F32) * taps[0][:, start:stop]
            for tap, source in zip(taps[1:], following):
                upstream += source[:, start:stop].astype(F32) * tap[:, start:stop]
            upstream = upstream.astype(BF16).astype(F32)
            scaled = upstream * dot(spread, pick, (1, 0))
            numer_ref[frame, :, start:stop] = scaled.astype(BF16)
            attended = dot(feat[:, low_lane:high_lane], wide[i, : high_lane - low_lane, : stop - start], (1, 0))
            for part in split(scaled * attended):
                summed += dot(part, pick, (1, 1))
        grad_denom = -summed * inverse
        high, low = split(grad_denom)
        high, low = high.astype(F32), low.astype(F32)
        sides = jnp.where((lane >= COPY) & (lane < 2 * COPY), low, high)
        sides = jnp.where(lane < 3 * COPY, sides, 0.0)
        denom_ref[frame] = sides.astype(BF16)
        numer = numer_ref[frame]
        add_outer(state, feat, numer)
        pairs = jnp.where(lane < 2 * COPY, sides, 0.0).astype(BF16)
        for start, stop, *_ in blocks:
            terms = dot(pairs, feat[:, start:stop], (0, 0))
            total[:, start:stop] += jnp.sum(jnp.where(picks(start, stop), terms, 0.0), 0, keepdims=True)

    for frame in range(frames):
        following = [
            grad_ref.at[i] if i < frames else next_ref.at[i - frames] for i in (frame + 1, frame + 2)
        ]
        frame_step(frame, following)
    write_messages(rank_ref[0], state[...], total[...], sorted_ref, out_refs)


def low_part(whole, high, middle):
    return whole - high.astype(F32) - middle.astype(F32)


def query_grad_kernel(scale, queries_ref, numer_ref, denom_ref, messages_ref, out_ref, state, across):
    blocks = spans(queries_ref.shape[2])
    tot_high, tot_low = read_totals(messages_ref)

    @pl.when(pl.program_id(0) == 0)
    def _():
        load_state(messages_ref, state)
        for i, block in enumerate(blocks):
            across[i, : block[1] - block[0], : block[3] - block[2]] = rows_of(state, block)

    denom = denom_ref[0]
    for i, (start, stop, low, high, _) in enumerate(blocks):
        row = lax.broadcasted_iota(jnp.int32, (LANES, stop - start), 0)
        tot = jnp.where(row < 2 * COPY, tot_high[:, start:stop], tot_low[:, start:stop])
        tot = jnp.where(picks(start, stop), tot, 0.0).astype(BF16)
        grad = dot(numer_ref[0, :, low:high], across[i, : stop - start, : high - low], (1, 1)) + dot(denom, tot, (1, 0))
        alive = queries_ref[0, :, start:stop].astype(F32) > 0
        out_ref[0, :, start:stop] = jnp.where(alive, grad * scale, 0.0).astype(BF16)


def key_grad_kernel(scale, keys_ref, values_ref, messages_ref, key_out, value_out, state, across, wide):
    blocks = spans(keys_ref.shape[2])
    rows = messages_ref[0].astype(F32)
    row = lax.broadcasted_iota(jnp.int32, rows.shape, 0)
    total = jnp.sum(jnp.where(row >= ROWS, rows, 0.0), 0, keepdims=True)

    @pl.when(pl.program_id(0) == 0)
    def _():
        load_state(messages_ref, state)
        for i, block in enumerate(blocks):
            across[i, : block[1] - block[0], : block[3] - block[2]] = rows_of(state, block)
            wide[i, : block[3] - block[2], : block[1] - block[0]] = columns_of(state, block)

    feat = jnp.maximum(keys_ref[0], 0)
    for i, (start, stop, low, high, _) in enumerate(blocks):
        grad = dot(values_ref[0, :, low:high], across[i, : stop - start, : high - low], (1, 1)) + total[:, start:stop]
        alive = keys_ref[0, :, start:stop].astype(F32) > 0
        key_out[0, :, start:stop] = jnp.where(alive, grad * scale, 0.0).astype(BF16)
        grad = dot(feat[:, low:high], wide[i, : high - low, : stop - start], (1, 0))
        value_out[0, :, start:stop] = (grad * scale).astype(BF16)


def cost(flops, size):
    return pl.CostEstimate(flops=flops, bytes_accessed=size, transcendentals=0)


def exchange(block, axis, distance):
    devices = range(lax.axis_size(axis))
    return lax.ppermute(block, axis, [(i, i ^ distance) for i in devices])


def total_of(messages):
    width = messages[0].shape[1]

    def added(parts):
        return pl.pallas_call(
            sum_kernel,
            out_shape=jax.ShapeDtypeStruct(parts[0].shape, BF16),
            compiler_params=pltpu.CompilerParams(vmem_limit_bytes=8 << 20),
            cost_estimate=cost(0, 9 * 32 * width),
        )(*parts)

    frames = lax.axis_size("frame")
    with jax.named_scope("spread"):
        got = [exchange(messages[d], "frame", d) for d in range(1, PARTS)]
    part = added([messages[0], *got])
    steps = [("frame", PARTS * d) for d in range(1, frames // PARTS)]
    if steps:
        part = added([part] + [exchange(part, *step) for step in steps])
    steps = [("space", d) for d in range(1, lax.axis_size("space"))]
    if steps:
        part = added([part] + [exchange(part, *step) for step in steps])
    groups = [list(range(i, i + PARTS)) for i in range(0, frames, PARTS)]
    return lax.all_gather(part, "frame", axis_index_groups=groups if len(groups) > 1 else None)


def shards(grad_out, conv_taps, saved_queries, saved_keys, saved_values):
    frames, tokens, width = grad_out.shape
    devices = lax.axis_size("frame")
    rank = (lax.axis_index("frame") % PARTS).astype(jnp.int32).reshape(1)
    scale = 2.0 * math.sqrt(frames * devices * tokens * lax.axis_size("space"))
    array = jax.ShapeDtypeStruct(grad_out.shape, BF16)
    message = jax.ShapeDtypeStruct((ROWS + 2, width), BF16)
    smem = pl.BlockSpec(memory_space=pltpu.SMEM)
    per_frame = pl.BlockSpec((1, tokens, width), lambda i: (i, 0, 0))
    scratch = [
        pltpu.VMEM((E, width), F32),
        pltpu.VMEM((8, width), F32),
        pltpu.VMEM((PARTS, ROWS + 2, width), F32),
    ]

    window = max(block[3] - block[2] for block in spans(width))
    across = pltpu.VMEM((len(spans(width)), SPAN, window), BF16)
    wide = pltpu.VMEM((len(spans(width)), window, SPAN), BF16)

    def whole(shape):
        return pl.BlockSpec(shape, lambda i: (0,) * len(shape))

    size = 2 * frames * tokens * width
    state_messages = pl.pallas_call(
        key_kernel,
        grid=(frames,),
        in_specs=[smem, per_frame, per_frame],
        out_specs=[whole(message.shape)] * PARTS,
        out_shape=[message] * PARTS,
        scratch_shapes=scratch,
        compiler_params=PARAMS,
        cost_estimate=cost(size * 512, 2 * size),
    )(rank, saved_keys, saved_values)
    with jax.named_scope("halo"):
        source, state_messages = lax.optimization_barrier((grad_out, state_messages))
        following = lax.ppermute(source, "frame", [(i + 1, i) for i in range(devices - 1)])
    states = total_of(state_messages)
    numer, denom, *grad_messages = pl.pallas_call(
        query_kernel,
        in_specs=[smem] + [pl.BlockSpec(memory_space=pltpu.VMEM)] * 5,
        out_shape=[array, jax.ShapeDtypeStruct((frames, tokens, LANES), BF16)] + [message] * PARTS,
        scratch_shapes=[scratch[0], pltpu.VMEM((1, width), F32), scratch[2], wide],
        compiler_params=PARAMS,
        cost_estimate=cost(size * 2048, 4 * size),
    )(rank, saved_queries, grad_out, following, conv_taps, states)
    per_denom = pl.BlockSpec((1, tokens, LANES), lambda i: (i, 0, 0))
    grad_queries = pl.pallas_call(
        functools.partial(query_grad_kernel, scale),
        grid=(frames,),
        in_specs=[per_frame, per_frame, per_denom, whole(states.shape)],
        out_specs=per_frame,
        out_shape=array,
        scratch_shapes=[scratch[0], across],
        compiler_params=PARAMS,
        cost_estimate=cost(size * 512, 3 * size),
    )(saved_queries, numer, denom, states)
    grads = total_of(grad_messages)
    grad_keys, grad_values = pl.pallas_call(
        functools.partial(key_grad_kernel, scale),
        grid=(frames,),
        in_specs=[per_frame, per_frame, whole(grads.shape)],
        out_specs=[per_frame, per_frame],
        out_shape=[array, array],
        scratch_shapes=[scratch[0], across, wide],
        compiler_params=PARAMS,
        cost_estimate=cost(size * 1024, 4 * size),
    )(saved_keys, saved_values, grads)
    return grad_queries, grad_keys, grad_values


def solution(mesh):
    block = P("frame", "space", None)
    return jax.shard_map(
        shards,
        mesh=mesh,
        in_specs=(block, P(), block, block, block),
        out_specs=(block, block, block),
        check_vma=False,
    )
```

profile of v0, /device:TPU:0, one launch (start us, length us, event | category | flops | bytes accessed | tf_op | source)
XLA Modules:
  0.0 124.5 jit_solution(17855955252794820971)
XLA Ops:
  0.7 1.9 %copy.19.keys_ref = bf16[2,220,2240]{2,1,0:T(8,128)(2,1)S(1)} copy(bf16[2,220,2240]{2,0,1:T(2,128)(2,1)} %param.8) | data formatting | bytes 3942400 | tf_op args[3]
  2.8 1.7 %copy.20.values_ref = bf16[2,220,2240]{2,1,0:T(8,128)(2,1)} copy(bf16[2,220,2240]{2,0,1:T(2,128)(2,1)S(1)} %copy-done.4) | data formatting | bytes 3942400 | tf_op args[4]
  4.5 1.6 %copy-done.1 = bf16[2,220,2240]{2,1,0:T(8,128)(2,1)S(1)} copy-done((bf16[2,220,2240]{2,1,0:T(8,128)(2,1)S(1)}, bf16[2,220,2240]{2,1,0:T(8,128)(2,1)}, u32[]{:S(2)}) %copy-start.1) | copy-done | bytes 1971224
  6.1 2.0 %shard_map.76 = (bf16[16,2240]{1,0:T(8,128)(2,1)S(1)}, bf16[16,2240]{1,0:T(8,128)(2,1)S(1)}, bf16[16,2240]{1,0:T(8,128)(2,1)S(1)}, bf16[16,2240]{1,0:T(8,128)(2,...) custom-call(s32[1]{0:T(128)} %bitcast.rank_ref, ...), custom_call_target="tpu_custom_call" | custom-call | flops 1009254400 | bytes 3942400 | tf_op jit(solution)/shard_map/pallas_call | solution.py:297
  8.1 1.3 %collective-permute-start = (bf16[2,220,2240]{2,0,1:T(2,128)(2,1)S(1)}, bf16[2,220,2240]{2,0,1:T(2,128)(2,1)S(1)}, u32[]{:S(2)}, u32[]{:S(2)}) collective-permute-start(bf16[2,220,2240]{2,0,1:T(2,128)(2,1)S(1)} %copy-done.6), channel_id=1, source_target_pairs={{4,0},{8,4},{12,8},{16,12},{20,16},{24,20},{28,24},{5,1},{9,5},{13... | collective-permute-start | bytes 5913608 | tf_op jit(solution)/shard_map/halo/ppermute | solution.py:309
  9.4 1.2 collective-permute-start.1
  10.6 3.0 %collective-permute-start.2 = (bf16[16,2240]{1,0:T(8,128)(2,1)S(1)}, bf16[16,2240]{1,0:T(8,128)(2,1)S(1)}, u32[]{:S(2)}, u32[]{:S(2)}) collective-permute-start(bf16[16,2240]{1,0:T(8,128)(2,1)S(1)} %get-tuple-element.43), channel_id=1, source_target_pairs={{0,8},{4,12},{8,0},{12,4},{16,24},{20,28},{24,16},{28,20},{1,9},{5... | collective-permute-start | bytes 215048 | tf_op jit(solution)/shard_map/spread/ppermute | solution.py:246
  13.5 2.3 %collective-permute-start.4 = (bf16[16,2240]{1,0:T(8,128)(2,1)S(1)}, bf16[16,2240]{1,0:T(8,128)(2,1)S(1)}, u32[]{:S(2)}, u32[]{:S(2)}) collective-permute-start(bf16[16,2240]{1,0:T(8,128)(2,1)S(1)} %get-tuple-element.45), channel_id=1, source_target_pairs={{0,16},{4,20},{8,24},{12,28},{16,0},{20,4},{24,8},{28,12},{1,17},{... | collective-permute-start | bytes 215048 | tf_op jit(solution)/shard_map/spread/ppermute | solution.py:246
  16.9 22.5 %collective-permute-done.2.refs_2_ = bf16[16,2240]{1,0:T(8,128)(2,1)S(1)} collective-permute-done((bf16[16,2240]{1,0:T(8,128)(2,1)S(1)}, bf16[16,2240]{1,0:T(8,128)(2,1)S(1)}, u32[]{:S(2)}, u32[]{:S(2)}) %collective-permute-start.2) | collective-permute-done | bytes 71712 | tf_op jit(solution)/shard_map/spread/ppermute | solution.py:246
  39.4 2.4 %collective-permute-start.6 = (bf16[16,2240]{1,0:T(8,128)(2,1)S(1)}, bf16[16,2240]{1,0:T(8,128)(2,1)S(1)}, u32[]{:S(2)}, u32[]{:S(2)}) collective-permute-start(bf16[16,2240]{1,0:T(8,128)(2,1)S(1)} %get-tuple-element.47), channel_id=1, source_target_pairs={{0,24},{4,28},{8,16},{12,20},{16,8},{20,12},{24,0},{28,4},{1,25},{... | collective-permute-start | bytes 215048 | tf_op jit(solution)/shard_map/spread/ppermute | solution.py:246
  42.0 2.6 %collective-permute-done.6.refs_6_ = bf16[16,2240]{1,0:T(8,128)(2,1)S(1)} collective-permute-done((bf16[16,2240]{1,0:T(8,128)(2,1)S(1)}, bf16[16,2240]{1,0:T(8,128)(2,1)S(1)}, u32[]{:S(2)}, u32[]{:S(2)}) %collective-permute-start.6) | collective-permute-done | bytes 71712 | tf_op jit(solution)/shard_map/spread/ppermute | solution.py:246
  44.6 1.8 %collective-permute-done.7.refs_7_ = bf16[16,2240]{1,0:T(8,128)(2,1)S(1)} collective-permute-done((bf16[16,2240]{1,0:T(8,128)(2,1)S(1)}, bf16[16,2240]{1,0:T(8,128)(2,1)S(1)}, u32[]{:S(2)}, u32[]{:S(2)}) %collective-permute-start.7) | collective-permute-done | bytes 71712 | tf_op jit(solution)/shard_map/spread/ppermute | solution.py:246
  46.6 3.7 %collective-permute-start.10 = (bf16[16,2240]{1,0:T(8,128)(2,1)S(1)}, bf16[16,2240]{1,0:T(8,128)(2,1)S(1)}, u32[]{:S(2)}, u32[]{:S(2)}) collective-permute-start(bf16[16,2240]{1,0:T(8,128)(2,1)S(1)} %shard_map.77.refs_0_), channel_id=1, source_target_pairs={{0,3},{1,2},{2,1},{3,0},{4,7},{5,6},{6,5},{7,4},{8,11},{9,10},{10,... | collective-permute-start | bytes 215048 | tf_op jit(solution)/shard_map/ppermute | solution.py:246
  51.0 1.5 %copy.22.grad_ref = bf16[2,220,2240]{2,1,0:T(8,128)(2,1)} copy(bf16[2,220,2240]{2,0,1:T(2,128)(2,1)S(1)} %copy-done.6) | data formatting | bytes 3942400 | tf_op args[0]
  52.9 3.0 %collective-permute-done.9.refs_2_ = bf16[16,2240]{1,0:T(8,128)(2,1)S(1)} collective-permute-done((bf16[16,2240]{1,0:T(8,128)(2,1)S(1)}, bf16[16,2240]{1,0:T(8,128)(2,1)S(1)}, u32[]{:S(2)}, u32[]{:S(2)}) %collective-permute-start.9) | collective-permute-done | bytes 71712 | tf_op jit(solution)/shard_map/ppermute | solution.py:246
  56.0 9.9 %all-gather = bf16[128,2240]{1,0:T(8,128)(2,1)S(1)} all-gather(bf16[16,2240]{1,0:T(8,128)(2,1)S(1)} %shard_map.78), channel_id=2, replica_groups=mesh['frame'=8,'space'=4] {'frame'}, dimensions={0}, use_global_device_ids=true | all-gather | bytes 645120 | tf_op jit(solution)/shard_map/all_gather | solution.py:271
  66.0 1.6 %copy.23.next_ref = bf16[2,220,2240]{2,1,0:T(8,128)(2,1)} copy(bf16[2,220,2240]{2,0,1:T(2,128)(2,1)S(1)} %collective-permute-done) | data formatting | bytes 3942400 | tf_op jit(solution)/shard_map/halo/ppermute | solution.py:309
  67.5 10.6 %shard_map.79 = (bf16[2,220,2240]{2,1,0:T(8,128)(2,1)S(1)}, bf16[2,220,128]{2,1,0:T(8,128)(2,1)S(1)}, bf16[16,2240]{1,0:T(8,128)(2,1)S(1)}, bf16[16,2240]{1,0:T(...) custom-call(s32[1]{0:T(128)} %bitcast.rank_ref, ...), custom_call_target="tpu_custom_call" | custom-call | flops 4037017600 | bytes 7884800 | tf_op jit(solution)/shard_map/pallas_call | solution.py:311
  78.2 1.3 %copy-done.2 = bf16[2,220,2240]{2,1,0:T(8,128)(2,1)} copy-done((bf16[2,220,2240]{2,1,0:T(8,128)(2,1)}, bf16[2,220,2240]{2,1,0:T(8,128)(2,1)S(1)}, u32[]{:S(2)}) %copy-start.2) | copy-done | bytes 1971224
  79.8 1.8 %collective-permute-start.12 = (bf16[16,2240]{1,0:T(8,128)(2,1)S(1)}, bf16[16,2240]{1,0:T(8,128)(2,1)S(1)}, u32[]{:S(2)}, u32[]{:S(2)}) collective-permute-start(bf16[16,2240]{1,0:T(8,128)(2,1)S(1)} %get-tuple-element.53), channel_id=1, source_target_pairs={{0,8},{4,12},{8,0},{12,4},{16,24},{20,28},{24,16},{28,20},{1,9},{5... | collective-permute-start | bytes 215048 | tf_op jit(solution)/shard_map/spread/ppermute | solution.py:246
  81.7 1.5 %collective-permute-start.14 = (bf16[16,2240]{1,0:T(8,128)(2,1)S(1)}, bf16[16,2240]{1,0:T(8,128)(2,1)S(1)}, u32[]{:S(2)}, u32[]{:S(2)}) collective-permute-start(bf16[16,2240]{1,0:T(8,128)(2,1)S(1)} %get-tuple-element.55), channel_id=1, source_target_pairs={{0,16},{4,20},{8,24},{12,28},{16,0},{20,4},{24,8},{28,12},{1,17},{... | collective-permute-start | bytes 215048 | tf_op jit(solution)/shard_map/spread/ppermute | solution.py:246
  83.4 1.5 %collective-permute-start.16 = (bf16[16,2240]{1,0:T(8,128)(2,1)S(1)}, bf16[16,2240]{1,0:T(8,128)(2,1)S(1)}, u32[]{:S(2)}, u32[]{:S(2)}) collective-permute-start(bf16[16,2240]{1,0:T(8,128)(2,1)S(1)} %get-tuple-element.57), channel_id=1, source_target_pairs={{0,24},{4,28},{8,16},{12,20},{16,8},{20,12},{24,0},{28,4},{1,25},{... | collective-permute-start | bytes 215048 | tf_op jit(solution)/shard_map/spread/ppermute | solution.py:246
  84.9 1.2 collective-permute-start.17
  86.3 4.0 %collective-permute-done.15.refs_5_ = bf16[16,2240]{1,0:T(8,128)(2,1)S(1)} collective-permute-done((bf16[16,2240]{1,0:T(8,128)(2,1)S(1)}, bf16[16,2240]{1,0:T(8,128)(2,1)S(1)}, u32[]{:S(2)}, u32[]{:S(2)}) %collective-permute-start.15) | collective-permute-done | bytes 71712 | tf_op jit(solution)/shard_map/spread/ppermute | solution.py:246
  90.5 2.5 %collective-permute-start.20 = (bf16[16,2240]{1,0:T(8,128)(2,1)S(1)}, bf16[16,2240]{1,0:T(8,128)(2,1)S(1)}, u32[]{:S(2)}, u32[]{:S(2)}) collective-permute-start(bf16[16,2240]{1,0:T(8,128)(2,1)S(1)} %shard_map.81.refs_0_), channel_id=1, source_target_pairs={{0,3},{1,2},{2,1},{3,0},{4,7},{5,6},{6,5},{7,4},{8,11},{9,10},{10,... | collective-permute-start | bytes 215048 | tf_op jit(solution)/shard_map/ppermute | solution.py:246
  93.1 1.9 %collective-permute-start.18 = (bf16[16,2240]{1,0:T(8,128)(2,1)S(1)}, bf16[16,2240]{1,0:T(8,128)(2,1)S(1)}, u32[]{:S(2)}, u32[]{:S(2)}) collective-permute-start(bf16[16,2240]{1,0:T(8,128)(2,1)S(1)} %shard_map.81.refs_0_), channel_id=1, source_target_pairs={{0,1},{1,0},{2,3},{3,2},{4,5},{5,4},{6,7},{7,6},{8,9},{9,8},{10,11... | collective-permute-start | bytes 215048 | tf_op jit(solution)/shard_map/ppermute | solution.py:246
  95.0 3.8 %shard_map.80 = bf16[2,220,2240]{2,1,0:T(8,128)(2,1)S(1)} custom-call(bf16[2,220,2240]{2,1,0:T(8,128)(2,1)S(1)} %copy.24.queries_ref, bf16[2,220,2240]{2,1,0:T(8,128)(2,1)} %copy-done.2, bf16[2,220,128]{2,1,0:T(8,128)(2,1)S(1)} %get-tuple-element.50.denom_ref, bf16[8,16,2240]{2,1,0:T(8,128)(2,1)S(1)} %bitcast.4), custom_call_target="tpu_custom_call" | custom-call | flops 1009254400 | bytes 5913600 | tf_op jit(solution)/shard_map/pallas_call | solution.py:320
  98.8 3.4 %copy.27 = bf16[2,220,2240]{2,0,1:T(2,128)(2,1)} copy(bf16[2,220,2240]{2,1,0:T(8,128)(2,1)S(1)} %shard_map.80) | data formatting | bytes 3942400
  102.3 10.5 %all-gather.1 = bf16[128,2240]{1,0:T(8,128)(2,1)S(1)} all-gather(bf16[16,2240]{1,0:T(8,128)(2,1)S(1)} %shard_map.82), channel_id=3, replica_groups=mesh['frame'=8,'space'=4] {'frame'}, dimensions={0}, use_global_device_ids=true | all-gather | bytes 645120 | tf_op jit(solution)/shard_map/all_gather | solution.py:271
  112.8 5.0 %shard_map.83 = (bf16[2,220,2240]{2,1,0:T(8,128)(2,1)S(1)}, bf16[2,220,2240]{2,1,0:T(8,128)(2,1)S(1)}) custom-call(bf16[2,220,2240]{2,1,0:T(8,128)(2,1)} %copy-done, bf16[2,220,2240]{2,1,0:T(8,128)(2,1)} %copy.20.values_ref, bf16[8,16,2240]{2,1,0:T(8,128)(2,1)S(1)} %bitcast.5), custom_call_target="tpu_custom_call" | custom-call | flops 2018508800 | bytes 7884800 | tf_op jit(solution)/shard_map/pallas_call | solution.py:331
  117.8 3.4 %copy.28 = bf16[2,220,2240]{2,0,1:T(2,128)(2,1)} copy(bf16[2,220,2240]{2,1,0:T(8,128)(2,1)S(1)} %get-tuple-element.65) | data formatting | bytes 3942400
  121.1 3.4 %copy.29 = bf16[2,220,2240]{2,0,1:T(2,128)(2,1)} copy(bf16[2,220,2240]{2,1,0:T(8,128)(2,1)S(1)} %get-tuple-element.66) | data formatting | bytes 3942400
  (42 shorter events, 4.1 us)
Async XLA Ops:
  0.6 2.2 %copy-start.4 = (bf16[2,220,2240]{2,0,1:T(2,128)(2,1)S(1)}, bf16[2,220,2240]{2,0,1:T(2,128)(2,1)}, u32[]{:S(2)}) copy-start(bf16[2,220,2240]{2,0,1:T(2,128)(2,1)} %param.9) | copy-start | bytes 5913604
  2.8 5.3 %copy-start = (bf16[2,220,2240]{2,1,0:T(8,128)(2,1)}, bf16[2,220,2240]{2,1,0:T(8,128)(2,1)S(1)}, u32[]{:S(2)}) copy-start(bf16[2,220,2240]{2,1,0:T(8,128)(2,1)S(1)} %copy.19.keys_ref) | copy-start | bytes 5913604
  4.5 1.6 %copy-start.1 = (bf16[2,220,2240]{2,1,0:T(8,128)(2,1)S(1)}, bf16[2,220,2240]{2,1,0:T(8,128)(2,1)}, u32[]{:S(2)}) copy-start(bf16[2,220,2240]{2,1,0:T(8,128)(2,1)} %copy.20.values_ref) | copy-start | bytes 5913604
  6.1 2.0 %copy-start.6 = (bf16[2,220,2240]{2,0,1:T(2,128)(2,1)S(1)}, bf16[2,220,2240]{2,0,1:T(2,128)(2,1)}, u32[]{:S(2)}) copy-start(bf16[2,220,2240]{2,0,1:T(2,128)(2,1)} %param.5) | copy-start | bytes 5913604
  8.1 57.9 %collective-permute-start = (bf16[2,220,2240]{2,0,1:T(2,128)(2,1)S(1)}, bf16[2,220,2240]{2,0,1:T(2,128)(2,1)S(1)}, u32[]{:S(2)}, u32[]{:S(2)}) collective-permute-start(bf16[2,220,2240]{2,0,1:T(2,128)(2,1)S(1)} %copy-done.6), channel_id=1, source_target_pairs={{4,0},{8,4},{12,8},{16,12},{20,16},{24,20},{28,24},{5,1},{9,5},{13... | collective-permute-start | bytes 5913608 | tf_op jit(solution)/shard_map/halo/ppermute | solution.py:309
  9.4 6.4 %collective-permute-start.1 = (bf16[16,2240]{1,0:T(8,128)(2,1)S(1)}, bf16[16,2240]{1,0:T(8,128)(2,1)S(1)}, u32[]{:S(2)}, u32[]{:S(2)}) collective-permute-start(bf16[16,2240]{1,0:T(8,128)(2,1)S(1)} %get-tuple-element.42), channel_id=1, source_target_pairs={{0,4},{4,0},{8,12},{12,8},{16,20},{20,16},{24,28},{28,24},{1,5},{5... | collective-permute-start | bytes 215048 | tf_op jit(solution)/shard_map/spread/ppermute | solution.py:246
  10.6 28.8 %collective-permute-start.2 = (bf16[16,2240]{1,0:T(8,128)(2,1)S(1)}, bf16[16,2240]{1,0:T(8,128)(2,1)S(1)}, u32[]{:S(2)}, u32[]{:S(2)}) collective-permute-start(bf16[16,2240]{1,0:T(8,128)(2,1)S(1)} %get-tuple-element.43), channel_id=1, source_target_pairs={{0,8},{4,12},{8,0},{12,4},{16,24},{20,28},{24,16},{28,20},{1,9},{5... | collective-permute-start | bytes 215048 | tf_op jit(solution)/shard_map/spread/ppermute | solution.py:246
  13.5 28.2 %collective-permute-start.3 = (bf16[16,2240]{1,0:T(8,128)(2,1)S(1)}, bf16[16,2240]{1,0:T(8,128)(2,1)S(1)}, u32[]{:S(2)}, u32[]{:S(2)}) collective-permute-start(bf16[16,2240]{1,0:T(8,128)(2,1)S(1)} %get-tuple-element.44), channel_id=1, source_target_pairs={{0,12},{4,8},{8,4},{12,0},{16,28},{20,24},{24,20},{28,16},{1,13},{... | collective-permute-start | bytes 215048 | tf_op jit(solution)/shard_map/spread/ppermute | solution.py:246
  13.5 28.4 %collective-permute-start.4 = (bf16[16,2240]{1,0:T(8,128)(2,1)S(1)}, bf16[16,2240]{1,0:T(8,128)(2,1)S(1)}, u32[]{:S(2)}, u32[]{:S(2)}) collective-permute-start(bf16[16,2240]{1,0:T(8,128)(2,1)S(1)} %get-tuple-element.45), channel_id=1, source_target_pairs={{0,16},{4,20},{8,24},{12,28},{16,0},{20,4},{24,8},{28,12},{1,17},{... | collective-permute-start | bytes 215048 | tf_op jit(solution)/shard_map/spread/ppermute | solution.py:246
  15.8 26.2 %collective-permute-start.5 = (bf16[16,2240]{1,0:T(8,128)(2,1)S(1)}, bf16[16,2240]{1,0:T(8,128)(2,1)S(1)}, u32[]{:S(2)}, u32[]{:S(2)}) collective-permute-start(bf16[16,2240]{1,0:T(8,128)(2,1)S(1)} %get-tuple-element.46), channel_id=1, source_target_pairs={{0,20},{4,16},{8,28},{12,24},{16,4},{20,0},{24,12},{28,8},{1,21},{... | collective-permute-start | bytes 215048 | tf_op jit(solution)/shard_map/spread/ppermute | solution.py:246
  39.4 5.3 %collective-permute-start.6 = (bf16[16,2240]{1,0:T(8,128)(2,1)S(1)}, bf16[16,2240]{1,0:T(8,128)(2,1)S(1)}, u32[]{:S(2)}, u32[]{:S(2)}) collective-permute-start(bf16[16,2240]{1,0:T(8,128)(2,1)S(1)} %get-tuple-element.47), channel_id=1, source_target_pairs={{0,24},{4,28},{8,16},{12,20},{16,8},{20,12},{24,0},{28,4},{1,25},{... | collective-permute-start | bytes 215048 | tf_op jit(solution)/shard_map/spread/ppermute | solution.py:246
  41.8 4.7 %collective-permute-start.7 = (bf16[16,2240]{1,0:T(8,128)(2,1)S(1)}, bf16[16,2240]{1,0:T(8,128)(2,1)S(1)}, u32[]{:S(2)}, u32[]{:S(2)}) collective-permute-start(bf16[16,2240]{1,0:T(8,128)(2,1)S(1)} %get-tuple-element.48), channel_id=1, source_target_pairs={{0,28},{4,24},{8,20},{12,16},{16,12},{20,8},{24,4},{28,0},{1,29},{... | collective-permute-start | bytes 215048 | tf_op jit(solution)/shard_map/spread/ppermute | solution.py:246
  46.6 6.0 %copy-start.5 = (bf16[2,220,2240]{2,0,1:T(2,128)(2,1)S(1)}, bf16[2,220,2240]{2,0,1:T(2,128)(2,1)}, u32[]{:S(2)}) copy-start(bf16[2,220,2240]{2,0,1:T(2,128)(2,1)} %param.7) | copy-start | bytes 5913604
  46.6 6.3 %collective-permute-start.10 = (bf16[16,2240]{1,0:T(8,128)(2,1)S(1)}, bf16[16,2240]{1,0:T(8,128)(2,1)S(1)}, u32[]{:S(2)}, u32[]{:S(2)}) collective-permute-start(bf16[16,2240]{1,0:T(8,128)(2,1)S(1)} %shard_map.77.refs_0_), channel_id=1, source_target_pairs={{0,3},{1,2},{2,1},{3,0},{4,7},{5,6},{6,5},{7,4},{8,11},{9,10},{10,... | collective-permute-start | bytes 215048 | tf_op jit(solution)/shard_map/ppermute | solution.py:246
  50.3 5.7 %collective-permute-start.9 = (bf16[16,2240]{1,0:T(8,128)(2,1)S(1)}, bf16[16,2240]{1,0:T(8,128)(2,1)S(1)}, u32[]{:S(2)}, u32[]{:S(2)}) collective-permute-start(bf16[16,2240]{1,0:T(8,128)(2,1)S(1)} %shard_map.77.refs_0_), channel_id=1, source_target_pairs={{0,2},{1,3},{2,0},{3,1},{4,6},{5,7},{6,4},{7,5},{8,10},{9,11},{10,... | collective-permute-start | bytes 215048 | tf_op jit(solution)/shard_map/ppermute | solution.py:246
  50.3 5.7 %collective-permute-start.8 = (bf16[16,2240]{1,0:T(8,128)(2,1)S(1)}, bf16[16,2240]{1,0:T(8,128)(2,1)S(1)}, u32[]{:S(2)}, u32[]{:S(2)}) collective-permute-start(bf16[16,2240]{1,0:T(8,128)(2,1)S(1)} %shard_map.77.refs_0_), channel_id=1, source_target_pairs={{0,1},{1,0},{2,3},{3,2},{4,5},{5,4},{6,7},{7,6},{8,9},{9,8},{10,11... | collective-permute-start | bytes 215048 | tf_op jit(solution)/shard_map/ppermute | solution.py:246
  66.0 1.6 %copy-start.3 = (f32[3,2240]{1,0:T(4,128)S(1)}, f32[3,2240]{1,0:T(4,128)}, u32[]{:S(2)}) copy-start(f32[3,2240]{1,0:T(4,128)} %taps_ref.1) | copy-start | bytes 80644
  78.2 1.3 %copy-start.2 = (bf16[2,220,2240]{2,1,0:T(8,128)(2,1)}, bf16[2,220,2240]{2,1,0:T(8,128)(2,1)S(1)}, u32[]{:S(2)}) copy-start(bf16[2,220,2240]{2,1,0:T(8,128)(2,1)S(1)} %get-tuple-element.49.numer_ref) | copy-start | bytes 5913604
  79.5 3.9 %collective-permute-start.11 = (bf16[16,2240]{1,0:T(8,128)(2,1)S(1)}, bf16[16,2240]{1,0:T(8,128)(2,1)S(1)}, u32[]{:S(2)}, u32[]{:S(2)}) collective-permute-start(bf16[16,2240]{1,0:T(8,128)(2,1)S(1)} %get-tuple-element.52), channel_id=1, source_target_pairs={{0,4},{4,0},{8,12},{12,8},{16,20},{20,16},{24,28},{28,24},{1,5},{5... | collective-permute-start | bytes 215048 | tf_op jit(solution)/shard_map/spread/ppermute | solution.py:246
  79.8 5.1 %collective-permute-start.12 = (bf16[16,2240]{1,0:T(8,128)(2,1)S(1)}, bf16[16,2240]{1,0:T(8,128)(2,1)S(1)}, u32[]{:S(2)}, u32[]{:S(2)}) collective-permute-start(bf16[16,2240]{1,0:T(8,128)(2,1)S(1)} %get-tuple-element.53), channel_id=1, source_target_pairs={{0,8},{4,12},{8,0},{12,4},{16,24},{20,28},{24,16},{28,20},{1,9},{5... | collective-permute-start | bytes 215048 | tf_op jit(solution)/shard_map/spread/ppermute | solution.py:246
  81.7 4.5 %collective-permute-start.13 = (bf16[16,2240]{1,0:T(8,128)(2,1)S(1)}, bf16[16,2240]{1,0:T(8,128)(2,1)S(1)}, u32[]{:S(2)}, u32[]{:S(2)}) collective-permute-start(bf16[16,2240]{1,0:T(8,128)(2,1)S(1)} %get-tuple-element.54), channel_id=1, source_target_pairs={{0,12},{4,8},{8,4},{12,0},{16,28},{20,24},{24,20},{28,16},{1,13},{... | collective-permute-start | bytes 215048 | tf_op jit(solution)/shard_map/spread/ppermute | solution.py:246
  81.7 4.7 %collective-permute-start.14 = (bf16[16,2240]{1,0:T(8,128)(2,1)S(1)}, bf16[16,2240]{1,0:T(8,128)(2,1)S(1)}, u32[]{:S(2)}, u32[]{:S(2)}) collective-permute-start(bf16[16,2240]{1,0:T(8,128)(2,1)S(1)} %get-tuple-element.55), channel_id=1, source_target_pairs={{0,16},{4,20},{8,24},{12,28},{16,0},{20,4},{24,8},{28,12},{1,17},{... | collective-permute-start | bytes 215048 | tf_op jit(solution)/shard_map/spread/ppermute | solution.py:246
  83.2 7.1 %collective-permute-start.15 = (bf16[16,2240]{1,0:T(8,128)(2,1)S(1)}, bf16[16,2240]{1,0:T(8,128)(2,1)S(1)}, u32[]{:S(2)}, u32[]{:S(2)}) collective-permute-start(bf16[16,2240]{1,0:T(8,128)(2,1)S(1)} %get-tuple-element.56), channel_id=1, source_target_pairs={{0,20},{4,16},{8,28},{12,24},{16,4},{20,0},{24,12},{28,8},{1,21},{... | collective-permute-start | bytes 215048 | tf_op jit(solution)/shard_map/spread/ppermute | solution.py:246
  83.4 6.9 %collective-permute-start.16 = (bf16[16,2240]{1,0:T(8,128)(2,1)S(1)}, bf16[16,2240]{1,0:T(8,128)(2,1)S(1)}, u32[]{:S(2)}, u32[]{:S(2)}) collective-permute-start(bf16[16,2240]{1,0:T(8,128)(2,1)S(1)} %get-tuple-element.57), channel_id=1, source_target_pairs={{0,24},{4,28},{8,16},{12,20},{16,8},{20,12},{24,0},{28,4},{1,25},{... | collective-permute-start | bytes 215048 | tf_op jit(solution)/shard_map/spread/ppermute | solution.py:246
  84.9 5.5 %collective-permute-start.17 = (bf16[16,2240]{1,0:T(8,128)(2,1)S(1)}, bf16[16,2240]{1,0:T(8,128)(2,1)S(1)}, u32[]{:S(2)}, u32[]{:S(2)}) collective-permute-start(bf16[16,2240]{1,0:T(8,128)(2,1)S(1)} %get-tuple-element.58), channel_id=1, source_target_pairs={{0,28},{4,24},{8,20},{12,16},{16,12},{20,8},{24,4},{28,0},{1,29},{... | collective-permute-start | bytes 215048 | tf_op jit(solution)/shard_map/spread/ppermute | solution.py:246
  90.5 11.7 %collective-permute-start.20 = (bf16[16,2240]{1,0:T(8,128)(2,1)S(1)}, bf16[16,2240]{1,0:T(8,128)(2,1)S(1)}, u32[]{:S(2)}, u32[]{:S(2)}) collective-permute-start(bf16[16,2240]{1,0:T(8,128)(2,1)S(1)} %shard_map.81.refs_0_), channel_id=1, source_target_pairs={{0,3},{1,2},{2,1},{3,0},{4,7},{5,6},{6,5},{7,4},{8,11},{9,10},{10,... | collective-permute-start | bytes 215048 | tf_op jit(solution)/shard_map/ppermute | solution.py:246
  93.1 9.1 %collective-permute-start.19 = (bf16[16,2240]{1,0:T(8,128)(2,1)S(1)}, bf16[16,2240]{1,0:T(8,128)(2,1)S(1)}, u32[]{:S(2)}, u32[]{:S(2)}) collective-permute-start(bf16[16,2240]{1,0:T(8,128)(2,1)S(1)} %shard_map.81.refs_0_), channel_id=1, source_target_pairs={{0,2},{1,3},{2,0},{3,1},{4,6},{5,7},{6,4},{7,5},{8,10},{9,11},{10,... | collective-permute-start | bytes 215048 | tf_op jit(solution)/shard_map/ppermute | solution.py:246
  93.1 9.1 %collective-permute-start.18 = (bf16[16,2240]{1,0:T(8,128)(2,1)S(1)}, bf16[16,2240]{1,0:T(8,128)(2,1)S(1)}, u32[]{:S(2)}, u32[]{:S(2)}) collective-permute-start(bf16[16,2240]{1,0:T(8,128)(2,1)S(1)} %shard_map.81.refs_0_), channel_id=1, source_target_pairs={{0,1},{1,0},{2,3},{3,2},{4,5},{5,4},{6,7},{7,6},{8,9},{9,8},{10,11... | collective-permute-start | bytes 215048 | tf_op jit(solution)/shard_map/ppermute | solution.py:246
where the time goes:
time: 125 us
  waiting for transfers between devices  34.5 us (28%)
  starting transfers between devices  26.9 us (22%)
  Pallas kernels  21.8 us (17%)
  blocking collectives  20.4 us (16%)
  local copies, waits for them, and re-layouts  20.2 us (16%)
    ppermute x20, waiting for transfers between devices, exchange(): return lax.ppermute(block, axis, [(i, i ^ distance) for i in devices])  34.5 us
    ppermute x20, starting transfers between devices, exchange(): return lax.ppermute(block, axis, [(i, i ^ distance) for i in devices])  25.6 us
    all_gather x2, blocking collectives, total_of(): lax.all_gather(part, 'frame', axis_index_groups=groups if len(groups) > 1...  20.4 us
    unnamed x21, local copies, waits for them, and re-layouts  18.6 us
    pallas_call x1, Pallas kernels, shards(): pl.pallas_call(query_kernel, in_specs=[smem] + [pl.BlockSpec(memory_space...  10.6 us
    pallas_call x1, Pallas kernels, shards(): pl.pallas_call(functools.partial(key_grad_kernel, scale), grid=(frames,),...  4.98 us
    pallas_call x1, Pallas kernels, shards(): pl.pallas_call(functools.partial(query_grad_kernel, scale), grid=(frames,...  3.84 us
  transfers between devices with their start and end apart: 21, of which 9 were waited for; matrix products, arithmetic and copies ran while one was open for 4% of the time, Pallas kernels for 3%

commit v1 on v0

v1 whole, which is shorter than its diff:
```python
import functools
import math

import jax
import jax.numpy as jnp
from jax import lax
from jax.experimental import pallas as pl
from jax.experimental.pallas import tpu as pltpu
from jax.sharding import PartitionSpec as P


H = 20
E = 112
EPSILON = 1e-06
LANES = 128
SPAN = 256
ROWS = 14
PARTS = E // ROWS
COPY = 32
F32, BF16 = jnp.float32, jnp.bfloat16
PARAMS = pltpu.CompilerParams(vmem_limit_bytes=48 << 20)


def spans(width):
    blocks = []
    for start in range(0, width, SPAN):
        stop = min(start + SPAN, width)
        first, last = start // E, (stop - 1) // E
        low = first * E // LANES * LANES
        high = min(-(-(last + 1) * E // LANES) * LANES, width)
        blocks.append((start, stop, low, high, range(first, last + 1)))
    return blocks


def dot(a, b, contract):
    return lax.dot_general(a, b, ((contract[:1], contract[1:]), ((), ())), preferred_element_type=F32)


def head_of_lane(rows, start, stop):
    return (lax.broadcasted_iota(jnp.int32, (rows, stop - start), 1) + start) // E


def picks(start, stop):
    row = lax.broadcasted_iota(jnp.int32, (LANES, stop - start), 0)
    return (row % COPY == head_of_lane(LANES, start, stop)) & (row < 3 * COPY)


def split(x):
    high = x.astype(BF16)
    return high, (x - high.astype(F32)).astype(BF16)


def add_outer(state, left, right):
    for start, stop, low, high, heads in spans(left.shape[1]):
        product = dot(left[:, low:high], right[:, start:stop], (0, 0))
        owner = head_of_lane(E, start, stop)
        part = jnp.zeros((E, stop - start), F32)
        for h in heads:
            part = jnp.where(owner == h, product[h * E - low : (h + 1) * E - low], part)
        state[:, start:stop] += part


def take(ref, start, stop):
    block = ref[:, :, start:stop]
    return block.reshape(block.shape[0] * block.shape[1], stop - start)


def put(ref, start, stop, rows):
    ref[:, :, start:stop] = rows.reshape(ref.shape[0], ref.shape[1], stop - start)


def write_messages(rank, state, total, sorted_ref, out_refs):
    high, low = split(total)
    for part in range(PARTS):
        rows = state[part * ROWS : (part + 1) * ROWS, :]
        sorted_ref[part] = jnp.concatenate([rows, high.astype(F32), low.astype(F32)], 0)
    for d, out in enumerate(out_refs):
        out[...] = sorted_ref[rank ^ d].astype(BF16)


def load_state(messages, state):
    for part in range(PARTS):
        state[part * ROWS : (part + 1) * ROWS, :] = messages[part].astype(F32)[:ROWS]


def read_totals(message):
    rows = message[...].astype(F32)
    return rows[ROWS : ROWS + 1], rows[ROWS + 1 : ROWS + 2]


def columns_of(state, block):
    start, stop, low, high, heads = block
    owner = head_of_lane(E, start, stop)
    rows = [jnp.where(owner == h, state[:, start:stop], 0.0) for h in heads]
    before, after = heads[0] * E - low, high - (heads[-1] + 1) * E
    if before > 0:
        rows = [jnp.zeros((before, stop - start), F32)] + rows
    if after > 0:
        rows = rows + [jnp.zeros((after, stop - start), F32)]
    return jnp.concatenate(rows, 0).astype(BF16)


def rows_of(state, block):
    start, stop, low, high, heads = block
    owner = head_of_lane(E, low, high)
    rows = []
    for h in heads:
        first, last = max(start - h * E, 0), min(stop - h * E, E)
        rows.append(jnp.where(owner[first:last] == h, state[first:last, low:high], 0.0))
    return jnp.concatenate(rows, 0).astype(BF16)


def key_kernel(rank_ref, keys_ref, values_ref, *refs):
    out_refs, (state, total, sorted_ref) = refs[:PARTS], refs[PARTS:]
    step = pl.program_id(0)

    @pl.when(step == 0)
    def _():
        state[...] = jnp.zeros_like(state)
        total[...] = jnp.zeros_like(total)

    width = keys_ref.shape[2]
    feat = jnp.maximum(take(keys_ref, 0, width), 0)
    add_outer(state, feat, take(values_ref, 0, width))
    total[...] += dot(jnp.ones((8, feat.shape[0]), BF16), feat, (1, 0))

    @pl.when(step == pl.num_programs(0) - 1)
    def _():
        write_messages(rank_ref[0], state[...], total[:1], sorted_ref, out_refs)


def sum_kernel(n_total, *refs):
    in_refs, out_ref = refs[:-1], refs[-1]
    in_refs, total_refs = in_refs[: len(in_refs) - n_total], in_refs[len(in_refs) - n_total :]
    added = in_refs[0][...].astype(F32)
    for ref in in_refs[1:]:
        added = added + ref[...].astype(F32)
    if total_refs:
        total = total_refs[0][:1]
    else:
        total = added[ROWS : ROWS + 1] + added[ROWS + 1 : ROWS + 2]
    high, low = split(total)
    row = lax.broadcasted_iota(jnp.int32, added.shape, 0)
    added = jnp.where(row == ROWS, high.astype(F32), added)
    added = jnp.where(row == ROWS + 1, low.astype(F32), added)
    out_ref[...] = added.astype(BF16)


def query_kernel(rank_ref, queries_ref, grad_ref, taps_ref, message_ref, *refs):
    n_next = len(refs) - PARTS - 4
    next_refs, (numer_ref, inverse_ref, *refs) = refs[:n_next], refs[n_next:]
    out_refs, (state, sorted_ref) = refs[:PARTS], refs[PARTS:]
    tokens, frames, width = queries_ref.shape
    rows = tokens * frames
    blocks = spans(width)
    tot_high, tot_low = read_totals(message_ref)
    taps = taps_ref[...]
    taps = [taps[0:1] + 1.0, taps[1:2], taps[2:3]]
    state[...] = jnp.zeros_like(state)
    feat = jnp.maximum(take(queries_ref, 0, width), 0)
    denominator = jnp.full((rows, LANES), EPSILON, F32)
    for start, stop, *_ in blocks:
        pick = picks(start, stop)
        for tot in (tot_high, tot_low):
            weights = jnp.where(pick, tot[:, start:stop], 0.0).astype(BF16)
            denominator += dot(feat[:, start:stop], weights, (1, 1))
    lane = lax.broadcasted_iota(jnp.int32, (rows, LANES), 1)
    inverse = jnp.where((lane % COPY < H) & (lane < 3 * COPY), 1.0 / denominator, 0.0)
    inverse_ref[...] = inverse
    high, _ = split(inverse)
    high = high.astype(F32)
    middle = (inverse - high).astype(BF16).astype(F32)
    spread = jnp.where(lane < COPY, high, jnp.where(lane < 2 * COPY, middle, inverse - high - middle)).astype(BF16)
    for start, stop, *_ in blocks:
        frame = lax.broadcasted_iota(jnp.int32, (rows, stop - start), 0) % frames
        now = take(grad_ref, start, stop).astype(F32)
        later = jnp.concatenate([take(ref, start, stop).astype(F32) for ref in next_refs], 0)
        upstream = now * taps[0][:, start:stop]
        for lag in (1, 2):
            shifted = pltpu.roll(later, frames - lag, 0) if lag < frames else later
            if lag < frames:
                shifted = jnp.where(frame + lag < frames, pltpu.roll(now, rows - lag, 0), shifted)
            upstream += shifted * taps[lag][:, start:stop]
        upstream = upstream.astype(BF16).astype(F32)
        pick = jnp.where(picks(start, stop), 1.0, 0.0).astype(BF16)
        numer_ref[:, start:stop] = (upstream * dot(spread, pick, (1, 0))).astype(BF16)
    add_outer(state, feat, numer_ref)
    write_messages(rank_ref[0], state[...], jnp.zeros((1, width), F32), sorted_ref, out_refs)


def query_grad_kernel(scale, rank_ref, queries_ref, numer_ref, inverse_ref, *refs):
    message_refs, (out_ref, total_ref, state, sorted_ref, wide, across) = refs[:PARTS], refs[PARTS:]
    tokens, frames, width = queries_ref.shape
    rows = tokens * frames
    blocks = spans(width)
    tot_high, tot_low = read_totals(message_refs[0])
    for d, ref in enumerate(message_refs):
        sorted_ref[rank_ref[0] ^ d] = ref[...].astype(F32)
    load_state(sorted_ref, state)
    for i, block in enumerate(blocks):
        wide[i, : block[3] - block[2], : block[1] - block[0]] = columns_of(state, block)
        across[i, : block[1] - block[0], : block[3] - block[2]] = rows_of(state, block)
    summed = jnp.zeros((rows, LANES), F32)
    for i, (start, stop, low, high, _) in enumerate(blocks):
        pick = jnp.where(picks(start, stop), 1.0, 0.0).astype(BF16)
        feat = jnp.maximum(take(queries_ref, low, high), 0)
        attended = dot(feat, wide[i, : high - low, : stop - start], (1, 0))
        for part in split(numer_ref[:, start:stop].astype(F32) * attended):
            summed += dot(part, pick, (1, 1))
    high, low = split(-summed * inverse_ref[...])
    high, low = high.astype(F32), low.astype(F32)
    lane = lax.broadcasted_iota(jnp.int32, (rows, LANES), 1)
    sides = jnp.where((lane >= COPY) & (lane < 2 * COPY), low, high)
    pairs = jnp.where(lane < 2 * COPY, sides, 0.0).astype(BF16)
    sides = sides.astype(BF16)
    for i, (start, stop, low, high, _) in enumerate(blocks):
        queries = take(queries_ref, start, stop)
        pick = picks(start, stop)
        terms = dot(pairs, jnp.maximum(queries, 0), (0, 0))
        terms = jnp.sum(jnp.where(pick, terms, 0.0), 0, keepdims=True)
        total_ref[:, start:stop] = jnp.broadcast_to(terms, (8, stop - start))
        row = lax.broadcasted_iota(jnp.int32, (LANES, stop - start), 0)
        tot = jnp.where(row < 2 * COPY, tot_high[:, start:stop], tot_low[:, start:stop])
        tot = jnp.where(pick, tot, 0.0).astype(BF16)
        grad = dot(numer_ref[:, low:high], across[i, : stop - start, : high - low], (1, 1)) + dot(sides, tot, (1, 0))
        put(out_ref, start, stop, jnp.where(queries.astype(F32) > 0, grad * scale, 0.0).astype(BF16))


def key_grad_kernel(scale, keys_ref, values_ref, messages_ref, key_out, value_out, state, wide, across):
    blocks = spans(keys_ref.shape[2])
    load_state(messages_ref, state)
    rows = messages_ref[0].astype(F32)
    for part in range(1, PARTS):
        rows = rows + messages_ref[part].astype(F32)
    row = lax.broadcasted_iota(jnp.int32, rows.shape, 0)
    total = jnp.sum(jnp.where(row >= ROWS, rows, 0.0), 0, keepdims=True)
    for i, block in enumerate(blocks):
        across[i, : block[1] - block[0], : block[3] - block[2]] = rows_of(state, block)
        wide[i, : block[3] - block[2], : block[1] - block[0]] = columns_of(state, block)
    for i, (start, stop, low, high, _) in enumerate(blocks):
        grad = dot(take(values_ref, low, high), across[i, : stop - start, : high - low], (1, 1)) + total[:, start:stop]
        alive = take(keys_ref, start, stop).astype(F32) > 0
        put(key_out, start, stop, jnp.where(alive, grad * scale, 0.0).astype(BF16))
        feat = jnp.maximum(take(keys_ref, low, high), 0)
        grad = dot(feat, wide[i, : high - low, : stop - start], (1, 0))
        put(value_out, start, stop, (grad * scale).astype(BF16))


def cost(flops, size):
    return pl.CostEstimate(flops=flops, bytes_accessed=size, transcendentals=0)


def exchange(block, axis, distance):
    devices = range(lax.axis_size(axis))
    return lax.ppermute(block, axis, [(i, i ^ distance) for i in devices])


def added(parts, total=None):
    totals = [] if total is None else [total]
    return pl.pallas_call(
        functools.partial(sum_kernel, len(totals)),
        out_shape=jax.ShapeDtypeStruct(parts[0].shape, BF16),
        compiler_params=pltpu.CompilerParams(vmem_limit_bytes=8 << 20),
        cost_estimate=cost(0, 9 * 32 * parts[0].shape[1]),
    )(*parts, *totals)


def spread_out(messages):
    got = []
    for d in range(1, PARTS):
        got.append(exchange(messages[d], "frame", d))
    return [messages[0], *got]


def over_groups(part):
    frames = lax.axis_size("frame")
    for axis, steps in (("frame", range(PARTS, frames, PARTS)), ("space", range(1, lax.axis_size("space")))):
        if steps:
            part = added([part] + [exchange(part, axis, d) for d in steps])
    return part


def shards(grad_out, conv_taps, saved_queries, saved_keys, saved_values):
    frames, tokens, width = grad_out.shape
    devices = lax.axis_size("frame")
    rank = (lax.axis_index("frame") % PARTS).astype(jnp.int32).reshape(1)
    scale = 2.0 * math.sqrt(frames * devices * tokens * lax.axis_size("space"))
    grad_out, saved_queries, saved_keys, saved_values = (
        x.transpose(1, 0, 2) for x in (grad_out, saved_queries, saved_keys, saved_values)
    )
    array = jax.ShapeDtypeStruct(grad_out.shape, BF16)
    message = jax.ShapeDtypeStruct((ROWS + 2, width), BF16)
    smem = pl.BlockSpec(memory_space=pltpu.SMEM)
    vmem = pl.BlockSpec(memory_space=pltpu.VMEM)
    window = max(block[3] - block[2] for block in spans(width))
    state = pltpu.VMEM((E, width), F32)
    ordered = pltpu.VMEM((PARTS, ROWS + 2, width), F32)
    across = pltpu.VMEM((len(spans(width)), SPAN, window), BF16)
    wide = pltpu.VMEM((len(spans(width)), window, SPAN), BF16)
    size = 2 * frames * tokens * width
    steps = 2 if tokens % 2 == 0 else 1
    per_step = pl.BlockSpec((tokens // steps, frames, width), lambda i: (i, 0, 0))

    def halo(source):
        return lax.ppermute(source, "frame", [(i + 1, i) for i in range(devices - 1)])

    early = tokens // 5
    following = [halo(grad_out[:early])]
    key = pl.pallas_call(
        key_kernel,
        grid=(steps,),
        in_specs=[smem, per_step, per_step],
        out_specs=[pl.BlockSpec(message.shape, lambda i: (0, 0))] * PARTS,
        out_shape=[message] * PARTS,
        scratch_shapes=[state, pltpu.VMEM((8, width), F32), ordered],
        compiler_params=PARAMS,
        cost_estimate=cost(size * 512, 2 * size),
    )
    state_messages = key(rank, saved_keys, saved_values)
    following.append(halo(grad_out[early:]))
    part = over_groups(added(spread_out(state_messages)))
    query = pl.pallas_call(
        query_kernel,
        in_specs=[smem] + [vmem] * (4 + len(following)),
        out_shape=[jax.ShapeDtypeStruct((frames * tokens, width), BF16), jax.ShapeDtypeStruct((frames * tokens, LANES), F32)] + [message] * PARTS,
        scratch_shapes=[state, ordered],
        compiler_params=PARAMS,
        cost_estimate=cost(size * 1024, 4 * size),
    )
    numer, inverse, *grad_messages = query(rank, saved_queries, grad_out, conv_taps, part, *following)
    states = spread_out([part] * PARTS)
    grad_parts = spread_out(grad_messages)
    query_grad = pl.pallas_call(
        functools.partial(query_grad_kernel, scale),
        in_specs=[smem] + [vmem] * (3 + PARTS),
        out_shape=[array, jax.ShapeDtypeStruct((8, width), F32)],
        scratch_shapes=[state, ordered, wide, across],
        compiler_params=PARAMS,
        cost_estimate=cost(size * 1024, 3 * size),
    )
    grad_queries, total = query_grad(rank, saved_queries, numer, inverse, *states)
    part = over_groups(added(grad_parts, total))
    groups = [list(range(i, i + PARTS)) for i in range(0, devices, PARTS)]
    grads = lax.all_gather(part, "frame", axis_index_groups=groups if len(groups) > 1 else None)
    grad_keys, grad_values = pl.pallas_call(
        functools.partial(key_grad_kernel, scale),
        out_shape=[array, array],
        scratch_shapes=[state, wide, across],
        compiler_params=PARAMS,
        cost_estimate=cost(size * 1024, 4 * size),
    )(saved_keys, saved_values, grads)
    return tuple(x.transpose(1, 0, 2) for x in (grad_queries, grad_keys, grad_values))


def solution(mesh):
    block = P("frame", "space", None)
    return jax.shard_map(
        shards,
        mesh=mesh,
        in_specs=(block, P(), block, block, block),
        out_specs=(block, block, block),
        check_vma=False,
    )
```

time: 125 us -> 116 us (0.928)
  local copies, waits for them, and re-layouts: 20.2 us -> 6.7 us
  blocking collectives: 20.4 us -> 9.45 us
  starting transfers between devices: 26.9 us -> 36.2 us
  Pallas kernels: 21.8 us -> 31 us
  waiting for transfers between devices: 34.5 us -> 31.6 us
    unnamed x21 -> x10, local copies, waits for them, and re-layouts: 18.6 us -> 1.58 us
    all_gather x2 -> x1, blocking collectives: 20.4 us -> 9.45 us  [shards(): lax.all_gather(part, 'frame', axis_index_groups=groups if len(groups) > 1...]
    pallas_call x8, Pallas kernels: 21.8 us -> 31 us  [the longest x1 12.1 us: shards(): query(rank, saved_queries, grad_out, conv_taps, part, *following)]
    ppermute x20 -> x27, starting transfers between devices: 25.6 us -> 33.7 us  [exchange(): return lax.ppermute(block, axis, [(i, i ^ distance) for i in devices])]
    slice x0 -> x2, local copies, waits for them, and re-layouts: none -> 5.12 us  [the longest x1 3.84 us: shards(): following.append(halo(grad_out[early:]))]
    ppermute x20 -> x27, waiting for transfers between devices: 34.5 us -> 31.6 us  [exchange(): return lax.ppermute(block, axis, [(i, i ^ distance) for i in devices])]
    ppermute x1 -> x0, local copies, waits for them, and re-layouts: 1.55 us -> none  [shards(): lax.ppermute(source, 'frame', [(i + 1, i) for i in range(devices - 1)])]
    ppermute x1 -> x2, starting transfers between devices: 1.29 us -> 2.57 us  [halo(): lax.ppermute(source, 'frame', [(i + 1, i) for i in range(devices - 1)])]
  transfers between devices with their start and end apart: 21 -> 29, of which waited for: 9 -> 9; matrix products, arithmetic and copies ran while one was open for 4% -> 1% of each run, Pallas kernels for 3% -> 20%
where the time goes in v1:
time: 116 us
  starting transfers between devices  36.2 us (31%)
  waiting for transfers between devices  31.6 us (27%)
  Pallas kernels  31 us (27%)
  blocking collectives  9.45 us (8%)
  local copies, waits for them, and re-layouts  6.7 us (6%)
    ppermute x27, starting transfers between devices, exchange(): return lax.ppermute(block, axis, [(i, i ^ distance) for i in devices])  33.7 us
    ppermute x27, waiting for transfers between devices, exchange(): return lax.ppermute(block, axis, [(i, i ^ distance) for i in devices])  31.6 us
    pallas_call x1, Pallas kernels, shards(): query(rank, saved_queries, grad_out, conv_taps, part, *following)  12.1 us
    all_gather x1, blocking collectives, shards(): lax.all_gather(part, 'frame', axis_index_groups=groups if len(groups) > 1...  9.45 us
    pallas_call x1, Pallas kernels, shards(): query_grad(rank, saved_queries, numer, inverse, *states)  8.82 us
    pallas_call x1, Pallas kernels, shards(): pl.pallas_call(functools.partial(key_grad_kernel, scale), out_shape=[arra...  7.23 us
    slice x1, local copies, waits for them, and re-layouts, shards(): following.append(halo(grad_out[early:]))  3.84 us
    ppermute x2, starting transfers between devices, halo(): lax.ppermute(source, 'frame', [(i + 1, i) for i in range(devices - 1)])  2.57 us
  transfers between devices with their start and end apart: 29, of which 9 were waited for; matrix products, arithmetic and copies ran while one was open for 1% of the time, Pallas kernels for 20%

profile of v1, /device:TPU:0, one launch (start us, length us, event | category | flops | bytes accessed | tf_op | source)
XLA Modules:
  0.0 115.7 jit_solution(15000686597803108995)
XLA Ops:
  0.6 3.8 %slice.9 = bf16[176,2,2240]{2,1,0:T(2,128)(2,1)} slice(bf16[220,2,2240]{2,1,0:T(2,128)(2,1)} %bitcast.16), slice={[44:220], [0:2], [0:2240]} | slice | bytes 3153920 | tf_op jit(solution)/shard_map/slice | solution.py:320
  4.5 1.3 %collective-permute-start.11 = (bf16[176,2,2240]{2,1,0:T(2,128)(2,1)}, bf16[176,2,2240]{2,1,0:T(2,128)(2,1)}, u32[]{:S(2)}, u32[]{:S(2)}) collective-permute-start(bf16[176,2,2240]{2,1,0:T(2,128)(2,1)} %slice.9), channel_id=1, source_target_pairs={{4,0},{8,4},{12,8},{16,12},{20,16},{24,20},{28,24},{5,1},{9,5},{13... | collective-permute-start | bytes 4730888 | tf_op jit(solution)/shard_map/ppermute | solution.py:305
  5.8 1.3 %slice.8 = bf16[44,2,2240]{2,1,0:T(2,128)(2,1)S(1)} slice(bf16[220,2,2240]{2,1,0:T(2,128)(2,1)} %bitcast.17), slice={[0:44], [0:2], [0:2240]} | slice | bytes 788480 | tf_op jit(solution)/shard_map/slice | solution.py:308
  7.1 1.3 %collective-permute-start.10 = (bf16[44,2,2240]{2,1,0:T(2,128)(2,1)S(1)}, bf16[44,2,2240]{2,1,0:T(2,128)(2,1)S(1)}, u32[]{:S(2)}, u32[]{:S(2)}) collective-permute-start(bf16[44,2,2240]{2,1,0:T(2,128)(2,1)S(1)} %slice.8), channel_id=1, source_target_pairs={{4,0},{8,4},{12,8},{16,12},{20,16},{24,20},{28,24},{5,1},{9,5},{13... | collective-permute-start | bytes 1182728 | tf_op jit(solution)/shard_map/ppermute | solution.py:305
  8.4 1.6 %copy-done.1 = bf16[2,220,2240]{2,0,1:T(2,128)(2,1)S(1)} copy-done((bf16[2,220,2240]{2,0,1:T(2,128)(2,1)S(1)}, bf16[2,220,2240]{2,0,1:T(2,128)(2,1)}, u32[]{:S(2)}) %copy-start.1) | copy-done | bytes 1971224
  9.9 2.5 %shard_map.76 = (bf16[16,2240]{1,0:T(8,128)(2,1)S(1)}, bf16[16,2240]{1,0:T(8,128)(2,1)S(1)}, bf16[16,2240]{1,0:T(8,128)(2,1)S(1)}, bf16[16,2240]{1,0:T(8,128)(2,...) custom-call(s32[1]{0:T(128)} %bitcast.rank_ref, ...), custom_call_target="tpu_custom_call" | custom-call | flops 1009254400 | bytes 3942400 | tf_op jit(solution)/shard_map/pallas_call | solution.py:319
  12.4 1.8 %collective-permute-start = (bf16[16,2240]{1,0:T(8,128)(2,1)S(1)}, bf16[16,2240]{1,0:T(8,128)(2,1)S(1)}, u32[]{:S(2)}, u32[]{:S(2)}) collective-permute-start(bf16[16,2240]{1,0:T(8,128)(2,1)S(1)} %get-tuple-element.26), channel_id=1, source_target_pairs={{0,4},{4,0},{8,12},{12,8},{16,20},{20,16},{24,28},{28,24},{1,5},{5... | collective-permute-start | bytes 215048 | tf_op jit(solution)/shard_map/ppermute | solution.py:255
  14.3 3.0 %collective-permute-start.1 = (bf16[16,2240]{1,0:T(8,128)(2,1)S(1)}, bf16[16,2240]{1,0:T(8,128)(2,1)S(1)}, u32[]{:S(2)}, u32[]{:S(2)}) collective-permute-start(bf16[16,2240]{1,0:T(8,128)(2,1)S(1)} %get-tuple-element.27), channel_id=1, source_target_pairs={{0,8},{4,12},{8,0},{12,4},{16,24},{20,28},{24,16},{28,20},{1,9},{5... | collective-permute-start | bytes 215048 | tf_op jit(solution)/shard_map/ppermute | solution.py:255
  17.2 2.9 %collective-permute-start.3 = (bf16[16,2240]{1,0:T(8,128)(2,1)S(1)}, bf16[16,2240]{1,0:T(8,128)(2,1)S(1)}, u32[]{:S(2)}, u32[]{:S(2)}) collective-permute-start(bf16[16,2240]{1,0:T(8,128)(2,1)S(1)} %get-tuple-element.29), channel_id=1, source_target_pairs={{0,16},{4,20},{8,24},{12,28},{16,0},{20,4},{24,8},{28,12},{1,17},{... | collective-permute-start | bytes 215048 | tf_op jit(solution)/shard_map/ppermute | solution.py:255
  20.2 15.0 %collective-permute-done.1.refs_2_ = bf16[16,2240]{1,0:T(8,128)(2,1)S(1)} collective-permute-done((bf16[16,2240]{1,0:T(8,128)(2,1)S(1)}, bf16[16,2240]{1,0:T(8,128)(2,1)S(1)}, u32[]{:S(2)}, u32[]{:S(2)}) %collective-permute-start.1) | collective-permute-done | bytes 71712 | tf_op jit(solution)/shard_map/ppermute | solution.py:255
  35.2 2.4 %collective-permute-start.5 = (bf16[16,2240]{1,0:T(8,128)(2,1)S(1)}, bf16[16,2240]{1,0:T(8,128)(2,1)S(1)}, u32[]{:S(2)}, u32[]{:S(2)}) collective-permute-start(bf16[16,2240]{1,0:T(8,128)(2,1)S(1)} %get-tuple-element.31), channel_id=1, source_target_pairs={{0,24},{4,28},{8,16},{12,20},{16,8},{20,12},{24,0},{28,4},{1,25},{... | collective-permute-start | bytes 215048 | tf_op jit(solution)/shard_map/ppermute | solution.py:255
  37.6 1.5 %collective-permute-start.6 = (bf16[16,2240]{1,0:T(8,128)(2,1)S(1)}, bf16[16,2240]{1,0:T(8,128)(2,1)S(1)}, u32[]{:S(2)}, u32[]{:S(2)}) collective-permute-start(bf16[16,2240]{1,0:T(8,128)(2,1)S(1)} %get-tuple-element.32), channel_id=1, source_target_pairs={{0,28},{4,24},{8,20},{12,16},{16,12},{20,8},{24,4},{28,0},{1,29},{... | collective-permute-start | bytes 215048 | tf_op jit(solution)/shard_map/ppermute | solution.py:255
  40.7 1.9 %collective-permute-done.6.refs_7_ = bf16[16,2240]{1,0:T(8,128)(2,1)S(1)} collective-permute-done((bf16[16,2240]{1,0:T(8,128)(2,1)S(1)}, bf16[16,2240]{1,0:T(8,128)(2,1)S(1)}, u32[]{:S(2)}, u32[]{:S(2)}) %collective-permute-start.6) | collective-permute-done | bytes 71712 | tf_op jit(solution)/shard_map/ppermute | solution.py:255
  42.7 3.7 %collective-permute-start.9 = (bf16[16,2240]{1,0:T(8,128)(2,1)S(1)}, bf16[16,2240]{1,0:T(8,128)(2,1)S(1)}, u32[]{:S(2)}, u32[]{:S(2)}) collective-permute-start(bf16[16,2240]{1,0:T(8,128)(2,1)S(1)} %shard_map.77.refs_0_), channel_id=1, source_target_pairs={{0,3},{1,2},{2,1},{3,0},{4,7},{5,6},{6,5},{7,4},{8,11},{9,10},{10,... | collective-permute-start | bytes 215048 | tf_op jit(solution)/shard_map/ppermute | solution.py:255
  47.1 2.3 %collective-permute-done.9.refs_3_ = bf16[16,2240]{1,0:T(8,128)(2,1)S(1)} collective-permute-done((bf16[16,2240]{1,0:T(8,128)(2,1)S(1)}, bf16[16,2240]{1,0:T(8,128)(2,1)S(1)}, u32[]{:S(2)}, u32[]{:S(2)}) %collective-permute-start.9) | collective-permute-done | bytes 71712 | tf_op jit(solution)/shard_map/ppermute | solution.py:255
  49.5 3.5 %collective-permute-done.8.refs_2_ = bf16[16,2240]{1,0:T(8,128)(2,1)S(1)} collective-permute-done((bf16[16,2240]{1,0:T(8,128)(2,1)S(1)}, bf16[16,2240]{1,0:T(8,128)(2,1)S(1)}, u32[]{:S(2)}, u32[]{:S(2)}) %collective-permute-start.8) | collective-permute-done | bytes 71712 | tf_op jit(solution)/shard_map/ppermute | solution.py:255
  55.1 1.6 %collective-permute-start.16 = (bf16[16,2240]{1,0:T(8,128)(2,1)S(1)}, bf16[16,2240]{1,0:T(8,128)(2,1)S(1)}, u32[]{:S(2)}, u32[]{:S(2)}) collective-permute-start(bf16[16,2240]{1,0:T(8,128)(2,1)S(1)} %shard_map.78.message_ref.refs_0_), channel_id=1, source_target_pairs={{0,20},{4,16},{8,28},{12,24},{16,4},{20,0},{24,12},{28,8},{1,21},{... | collective-permute-start | bytes 215048 | tf_op jit(solution)/shard_map/ppermute | solution.py:255
  56.7 1.5 %collective-permute-done.18.refs_7_ = bf16[16,2240]{1,0:T(8,128)(2,1)S(1)} collective-permute-done((bf16[16,2240]{1,0:T(8,128)(2,1)S(1)}, bf16[16,2240]{1,0:T(8,128)(2,1)S(1)}, u32[]{:S(2)}, u32[]{:S(2)}) %collective-permute-start.18) | collective-permute-done | bytes 71712 | tf_op jit(solution)/shard_map/ppermute | solution.py:255
  58.3 1.3 %collective-permute-start.15 = (bf16[16,2240]{1,0:T(8,128)(2,1)S(1)}, bf16[16,2240]{1,0:T(8,128)(2,1)S(1)}, u32[]{:S(2)}, u32[]{:S(2)}) collective-permute-start(bf16[16,2240]{1,0:T(8,128)(2,1)S(1)} %shard_map.78.message_ref.refs_0_), channel_id=1, source_target_pairs={{0,16},{4,20},{8,24},{12,28},{16,0},{20,4},{24,8},{28,12},{1,17},{... | collective-permute-start | bytes 215048 | tf_op jit(solution)/shard_map/ppermute | solution.py:255
  59.7 1.6 %collective-permute-start.13 = (bf16[16,2240]{1,0:T(8,128)(2,1)S(1)}, bf16[16,2240]{1,0:T(8,128)(2,1)S(1)}, u32[]{:S(2)}, u32[]{:S(2)}) collective-permute-start(bf16[16,2240]{1,0:T(8,128)(2,1)S(1)} %shard_map.78.message_ref.refs_0_), channel_id=1, source_target_pairs={{0,8},{4,12},{8,0},{12,4},{16,24},{20,28},{24,16},{28,20},{1,9},{5... | collective-permute-start | bytes 215048 | tf_op jit(solution)/shard_map/ppermute | solution.py:255
  61.3 12.1 %shard_map.79 = (bf16[440,2240]{1,0:T(8,128)(2,1)S(1)}, f32[440,128]{1,0:T(8,128)S(1)}, bf16[16,2240]{1,0:T(8,128)(2,1)S(1)}, bf16[16,2240]{1,0:T(8,128)(2,1)S(1...) custom-call(s32[1]{0:T(128)} %bitcast.rank_ref, ...), custom_call_target="tpu_custom_call" | custom-call | flops 2018508800 | bytes 7884800 | tf_op jit(solution)/shard_map/pallas_call | solution.py:330
  74.0 1.2 collective-permute-start.20
  76.2 1.3 %collective-permute-start.23 = (bf16[16,2240]{1,0:T(8,128)(2,1)S(1)}, bf16[16,2240]{1,0:T(8,128)(2,1)S(1)}, u32[]{:S(2)}, u32[]{:S(2)}) collective-permute-start(bf16[16,2240]{1,0:T(8,128)(2,1)S(1)} %get-tuple-element.41), channel_id=1, source_target_pairs={{0,20},{4,16},{8,28},{12,24},{16,4},{20,0},{24,12},{28,8},{1,21},{... | collective-permute-start | bytes 215048 | tf_op jit(solution)/shard_map/ppermute | solution.py:255
  77.5 1.2 %collective-permute-start.24 = (bf16[16,2240]{1,0:T(8,128)(2,1)S(1)}, bf16[16,2240]{1,0:T(8,128)(2,1)S(1)}, u32[]{:S(2)}, u32[]{:S(2)}) collective-permute-start(bf16[16,2240]{1,0:T(8,128)(2,1)S(1)} %get-tuple-element.42), channel_id=1, source_target_pairs={{0,24},{4,28},{8,16},{12,20},{16,8},{20,12},{24,0},{28,4},{1,25},{... | collective-permute-start | bytes 215048 | tf_op jit(solution)/shard_map/ppermute | solution.py:255
  78.7 1.2 %collective-permute-start.25 = (bf16[16,2240]{1,0:T(8,128)(2,1)S(1)}, bf16[16,2240]{1,0:T(8,128)(2,1)S(1)}, u32[]{:S(2)}, u32[]{:S(2)}) collective-permute-start(bf16[16,2240]{1,0:T(8,128)(2,1)S(1)} %get-tuple-element.43), channel_id=1, source_target_pairs={{0,28},{4,24},{8,20},{12,16},{16,12},{20,8},{24,4},{28,0},{1,29},{... | collective-permute-start | bytes 215048 | tf_op jit(solution)/shard_map/ppermute | solution.py:255
  79.9 8.8 %shard_map.80 = (bf16[220,2,2240]{2,1,0:T(2,128)(2,1)}, f32[8,2240]{1,0:T(8,128)S(1)}) custom-call(s32[1]{0:T(128)} %bitcast.rank_ref, bf16[220,2,2240]{2,1,0:T(2,128)(2,1)S(1)} %bitcast.15, bf16[440,2240]{1,0:T(8,128)(2,1)S(1)} %get-tuple-element.33.numer_ref, f32[440,128]{1,0:T(8,128)S(1)} %get-tuple-element.34.inverse_ref, ...), custom_call_target="tpu_custom_call" | custom-call | flops 2018508800 | bytes 5913600 | tf_op jit(solution)/shard_map/pallas_call | solution.py:341
  88.9 2.5 %collective-permute-start.28 = (bf16[16,2240]{1,0:T(8,128)(2,1)S(1)}, bf16[16,2240]{1,0:T(8,128)(2,1)S(1)}, u32[]{:S(2)}, u32[]{:S(2)}) collective-permute-start(bf16[16,2240]{1,0:T(8,128)(2,1)S(1)} %shard_map.81.refs_0_), channel_id=1, source_target_pairs={{0,3},{1,2},{2,1},{3,0},{4,7},{5,6},{6,5},{7,4},{8,11},{9,10},{10,... | collective-permute-start | bytes 215048 | tf_op jit(solution)/shard_map/ppermute | solution.py:255
  91.4 1.9 %collective-permute-start.26 = (bf16[16,2240]{1,0:T(8,128)(2,1)S(1)}, bf16[16,2240]{1,0:T(8,128)(2,1)S(1)}, u32[]{:S(2)}, u32[]{:S(2)}) collective-permute-start(bf16[16,2240]{1,0:T(8,128)(2,1)S(1)} %shard_map.81.refs_0_), channel_id=1, source_target_pairs={{0,1},{1,0},{2,3},{3,2},{4,5},{5,4},{6,7},{7,6},{8,9},{9,8},{10,11... | collective-permute-start | bytes 215048 | tf_op jit(solution)/shard_map/ppermute | solution.py:255
  93.3 2.7 %collective-permute-done.28.refs_3_ = bf16[16,2240]{1,0:T(8,128)(2,1)S(1)} collective-permute-done((bf16[16,2240]{1,0:T(8,128)(2,1)S(1)}, bf16[16,2240]{1,0:T(8,128)(2,1)S(1)}, u32[]{:S(2)}, u32[]{:S(2)}) %collective-permute-start.28) | collective-permute-done | bytes 71712 | tf_op jit(solution)/shard_map/ppermute | solution.py:255
  96.0 3.0 %collective-permute-done.27.refs_2_ = bf16[16,2240]{1,0:T(8,128)(2,1)S(1)} collective-permute-done((bf16[16,2240]{1,0:T(8,128)(2,1)S(1)}, bf16[16,2240]{1,0:T(8,128)(2,1)S(1)}, u32[]{:S(2)}, u32[]{:S(2)}) %collective-permute-start.27) | collective-permute-done | bytes 71712 | tf_op jit(solution)/shard_map/ppermute | solution.py:255
  99.0 9.4 %all-gather = bf16[128,2240]{1,0:T(8,128)(2,1)S(1)} all-gather(bf16[16,2240]{1,0:T(8,128)(2,1)S(1)} %shard_map.82), channel_id=2, replica_groups=mesh['frame'=8,'space'=4] {'frame'}, dimensions={0}, use_global_device_ids=true | all-gather | bytes 645120 | tf_op jit(solution)/shard_map/all_gather | solution.py:344
  108.5 7.2 %shard_map.83 = (bf16[220,2,2240]{2,1,0:T(2,128)(2,1)}, bf16[220,2,2240]{2,1,0:T(2,128)(2,1)}) custom-call(bf16[220,2,2240]{2,1,0:T(2,128)(2,1)S(1)} %bitcast.10, bf16[220,2,2240]{2,1,0:T(2,128)(2,1)S(1)} %bitcast.12, bf16[8,16,2240]{2,1,0:T(8,128)(2,1)S(1)} %bitcast.13), custom_call_target="tpu_custom_call" | custom-call | flops 2018508800 | bytes 7884800 | tf_op jit(solution)/shard_map/pallas_call | solution.py:345
  (47 shorter events, 6.7 us)
Async XLA Ops:
  4.5 55.2 %collective-permute-start.11 = (bf16[176,2,2240]{2,1,0:T(2,128)(2,1)}, bf16[176,2,2240]{2,1,0:T(2,128)(2,1)}, u32[]{:S(2)}, u32[]{:S(2)}) collective-permute-start(bf16[176,2,2240]{2,1,0:T(2,128)(2,1)} %slice.9), channel_id=1, source_target_pairs={{4,0},{8,4},{12,8},{16,12},{20,16},{24,20},{28,24},{5,1},{9,5},{13... | collective-permute-start | bytes 4730888 | tf_op jit(solution)/shard_map/ppermute | solution.py:305
  7.1 52.5 %collective-permute-start.10 = (bf16[44,2,2240]{2,1,0:T(2,128)(2,1)S(1)}, bf16[44,2,2240]{2,1,0:T(2,128)(2,1)S(1)}, u32[]{:S(2)}, u32[]{:S(2)}) collective-permute-start(bf16[44,2,2240]{2,1,0:T(2,128)(2,1)S(1)} %slice.8), channel_id=1, source_target_pairs={{4,0},{8,4},{12,8},{16,12},{20,16},{24,20},{28,24},{5,1},{9,5},{13... | collective-permute-start | bytes 1182728 | tf_op jit(solution)/shard_map/ppermute | solution.py:305
  9.9 51.3 %copy-start.4 = (f32[3,2240]{1,0:T(4,128)S(1)}, f32[3,2240]{1,0:T(4,128)}, u32[]{:S(2)}) copy-start(f32[3,2240]{1,0:T(4,128)} %taps_ref.1) | copy-start | bytes 80644
  12.4 4.8 %collective-permute-start = (bf16[16,2240]{1,0:T(8,128)(2,1)S(1)}, bf16[16,2240]{1,0:T(8,128)(2,1)S(1)}, u32[]{:S(2)}, u32[]{:S(2)}) collective-permute-start(bf16[16,2240]{1,0:T(8,128)(2,1)S(1)} %get-tuple-element.26), channel_id=1, source_target_pairs={{0,4},{4,0},{8,12},{12,8},{16,20},{20,16},{24,28},{28,24},{1,5},{5... | collective-permute-start | bytes 215048 | tf_op jit(solution)/shard_map/ppermute | solution.py:255
  14.3 20.9 %collective-permute-start.1 = (bf16[16,2240]{1,0:T(8,128)(2,1)S(1)}, bf16[16,2240]{1,0:T(8,128)(2,1)S(1)}, u32[]{:S(2)}, u32[]{:S(2)}) collective-permute-start(bf16[16,2240]{1,0:T(8,128)(2,1)S(1)} %get-tuple-element.27), channel_id=1, source_target_pairs={{0,8},{4,12},{8,0},{12,4},{16,24},{20,28},{24,16},{28,20},{1,9},{5... | collective-permute-start | bytes 215048 | tf_op jit(solution)/shard_map/ppermute | solution.py:255
  17.2 18.0 %collective-permute-start.2 = (bf16[16,2240]{1,0:T(8,128)(2,1)S(1)}, bf16[16,2240]{1,0:T(8,128)(2,1)S(1)}, u32[]{:S(2)}, u32[]{:S(2)}) collective-permute-start(bf16[16,2240]{1,0:T(8,128)(2,1)S(1)} %get-tuple-element.28), channel_id=1, source_target_pairs={{0,12},{4,8},{8,4},{12,0},{16,28},{20,24},{24,20},{28,16},{1,13},{... | collective-permute-start | bytes 215048 | tf_op jit(solution)/shard_map/ppermute | solution.py:255
  17.2 20.4 %collective-permute-start.3 = (bf16[16,2240]{1,0:T(8,128)(2,1)S(1)}, bf16[16,2240]{1,0:T(8,128)(2,1)S(1)}, u32[]{:S(2)}, u32[]{:S(2)}) collective-permute-start(bf16[16,2240]{1,0:T(8,128)(2,1)S(1)} %get-tuple-element.29), channel_id=1, source_target_pairs={{0,16},{4,20},{8,24},{12,28},{16,0},{20,4},{24,8},{28,12},{1,17},{... | collective-permute-start | bytes 215048 | tf_op jit(solution)/shard_map/ppermute | solution.py:255
  35.2 4.5 %collective-permute-start.4 = (bf16[16,2240]{1,0:T(8,128)(2,1)S(1)}, bf16[16,2240]{1,0:T(8,128)(2,1)S(1)}, u32[]{:S(2)}, u32[]{:S(2)}) collective-permute-start(bf16[16,2240]{1,0:T(8,128)(2,1)S(1)} %get-tuple-element.30), channel_id=1, source_target_pairs={{0,20},{4,16},{8,28},{12,24},{16,4},{20,0},{24,12},{28,8},{1,21},{... | collective-permute-start | bytes 215048 | tf_op jit(solution)/shard_map/ppermute | solution.py:255
  35.2 5.5 %collective-permute-start.5 = (bf16[16,2240]{1,0:T(8,128)(2,1)S(1)}, bf16[16,2240]{1,0:T(8,128)(2,1)S(1)}, u32[]{:S(2)}, u32[]{:S(2)}) collective-permute-start(bf16[16,2240]{1,0:T(8,128)(2,1)S(1)} %get-tuple-element.31), channel_id=1, source_target_pairs={{0,24},{4,28},{8,16},{12,20},{16,8},{20,12},{24,0},{28,4},{1,25},{... | collective-permute-start | bytes 215048 | tf_op jit(solution)/shard_map/ppermute | solution.py:255
  37.6 5.0 %collective-permute-start.6 = (bf16[16,2240]{1,0:T(8,128)(2,1)S(1)}, bf16[16,2240]{1,0:T(8,128)(2,1)S(1)}, u32[]{:S(2)}, u32[]{:S(2)}) collective-permute-start(bf16[16,2240]{1,0:T(8,128)(2,1)S(1)} %get-tuple-element.32), channel_id=1, source_target_pairs={{0,28},{4,24},{8,20},{12,16},{16,12},{20,8},{24,4},{28,0},{1,29},{... | collective-permute-start | bytes 215048 | tf_op jit(solution)/shard_map/ppermute | solution.py:255
  42.7 6.8 %collective-permute-start.9 = (bf16[16,2240]{1,0:T(8,128)(2,1)S(1)}, bf16[16,2240]{1,0:T(8,128)(2,1)S(1)}, u32[]{:S(2)}, u32[]{:S(2)}) collective-permute-start(bf16[16,2240]{1,0:T(8,128)(2,1)S(1)} %shard_map.77.refs_0_), channel_id=1, source_target_pairs={{0,3},{1,2},{2,1},{3,0},{4,7},{5,6},{6,5},{7,4},{8,11},{9,10},{10,... | collective-permute-start | bytes 215048 | tf_op jit(solution)/shard_map/ppermute | solution.py:255
  46.3 6.6 %collective-permute-start.8 = (bf16[16,2240]{1,0:T(8,128)(2,1)S(1)}, bf16[16,2240]{1,0:T(8,128)(2,1)S(1)}, u32[]{:S(2)}, u32[]{:S(2)}) collective-permute-start(bf16[16,2240]{1,0:T(8,128)(2,1)S(1)} %shard_map.77.refs_0_), channel_id=1, source_target_pairs={{0,2},{1,3},{2,0},{3,1},{4,6},{5,7},{6,4},{7,5},{8,10},{9,11},{10,... | collective-permute-start | bytes 215048 | tf_op jit(solution)/shard_map/ppermute | solution.py:255
  46.3 6.6 %collective-permute-start.7 = (bf16[16,2240]{1,0:T(8,128)(2,1)S(1)}, bf16[16,2240]{1,0:T(8,128)(2,1)S(1)}, u32[]{:S(2)}, u32[]{:S(2)}) collective-permute-start(bf16[16,2240]{1,0:T(8,128)(2,1)S(1)} %shard_map.77.refs_0_), channel_id=1, source_target_pairs={{0,1},{1,0},{2,3},{3,2},{4,5},{5,4},{6,7},{7,6},{8,9},{9,8},{10,11... | collective-permute-start | bytes 215048 | tf_op jit(solution)/shard_map/ppermute | solution.py:255
  53.1 5.2 %collective-permute-start.18 = (bf16[16,2240]{1,0:T(8,128)(2,1)S(1)}, bf16[16,2240]{1,0:T(8,128)(2,1)S(1)}, u32[]{:S(2)}, u32[]{:S(2)}) collective-permute-start(bf16[16,2240]{1,0:T(8,128)(2,1)S(1)} %shard_map.78.message_ref.refs_0_), channel_id=1, source_target_pairs={{0,28},{4,24},{8,20},{12,16},{16,12},{20,8},{24,4},{28,0},{1,29},{... | collective-permute-start | bytes 215048 | tf_op jit(solution)/shard_map/ppermute | solution.py:255
  54.0 19.4 %collective-permute-start.17 = (bf16[16,2240]{1,0:T(8,128)(2,1)S(1)}, bf16[16,2240]{1,0:T(8,128)(2,1)S(1)}, u32[]{:S(2)}, u32[]{:S(2)}) collective-permute-start(bf16[16,2240]{1,0:T(8,128)(2,1)S(1)} %shard_map.78.message_ref.refs_0_), channel_id=1, source_target_pairs={{0,24},{4,28},{8,16},{12,20},{16,8},{20,12},{24,0},{28,4},{1,25},{... | collective-permute-start | bytes 215048 | tf_op jit(solution)/shard_map/ppermute | solution.py:255
  55.1 18.5 %collective-permute-start.16 = (bf16[16,2240]{1,0:T(8,128)(2,1)S(1)}, bf16[16,2240]{1,0:T(8,128)(2,1)S(1)}, u32[]{:S(2)}, u32[]{:S(2)}) collective-permute-start(bf16[16,2240]{1,0:T(8,128)(2,1)S(1)} %shard_map.78.message_ref.refs_0_), channel_id=1, source_target_pairs={{0,20},{4,16},{8,28},{12,24},{16,4},{20,0},{24,12},{28,8},{1,21},{... | collective-permute-start | bytes 215048 | tf_op jit(solution)/shard_map/ppermute | solution.py:255
  58.3 15.7 %collective-permute-start.15 = (bf16[16,2240]{1,0:T(8,128)(2,1)S(1)}, bf16[16,2240]{1,0:T(8,128)(2,1)S(1)}, u32[]{:S(2)}, u32[]{:S(2)}) collective-permute-start(bf16[16,2240]{1,0:T(8,128)(2,1)S(1)} %shard_map.78.message_ref.refs_0_), channel_id=1, source_target_pairs={{0,16},{4,20},{8,24},{12,28},{16,0},{20,4},{24,8},{28,12},{1,17},{... | collective-permute-start | bytes 215048 | tf_op jit(solution)/shard_map/ppermute | solution.py:255
  59.6 15.5 %collective-permute-start.14 = (bf16[16,2240]{1,0:T(8,128)(2,1)S(1)}, bf16[16,2240]{1,0:T(8,128)(2,1)S(1)}, u32[]{:S(2)}, u32[]{:S(2)}) collective-permute-start(bf16[16,2240]{1,0:T(8,128)(2,1)S(1)} %shard_map.78.message_ref.refs_0_), channel_id=1, source_target_pairs={{0,12},{4,8},{8,4},{12,0},{16,28},{20,24},{24,20},{28,16},{1,13},{... | collective-permute-start | bytes 215048 | tf_op jit(solution)/shard_map/ppermute | solution.py:255
  59.7 15.8 %collective-permute-start.13 = (bf16[16,2240]{1,0:T(8,128)(2,1)S(1)}, bf16[16,2240]{1,0:T(8,128)(2,1)S(1)}, u32[]{:S(2)}, u32[]{:S(2)}) collective-permute-start(bf16[16,2240]{1,0:T(8,128)(2,1)S(1)} %shard_map.78.message_ref.refs_0_), channel_id=1, source_target_pairs={{0,8},{4,12},{8,0},{12,4},{16,24},{20,28},{24,16},{28,20},{1,9},{5... | collective-permute-start | bytes 215048 | tf_op jit(solution)/shard_map/ppermute | solution.py:255
  61.3 18.6 %copy-start.3 = (bf16[2,220,2240]{2,0,1:T(2,128)(2,1)S(1)}, bf16[2,220,2240]{2,0,1:T(2,128)(2,1)}, u32[]{:S(2)}) copy-start(bf16[2,220,2240]{2,0,1:T(2,128)(2,1)} %param.7) | copy-start | bytes 5913604
  73.4 2.8 %collective-permute-start.12 = (bf16[16,2240]{1,0:T(8,128)(2,1)S(1)}, bf16[16,2240]{1,0:T(8,128)(2,1)S(1)}, u32[]{:S(2)}, u32[]{:S(2)}) collective-permute-start(bf16[16,2240]{1,0:T(8,128)(2,1)S(1)} %shard_map.78.message_ref.refs_0_), channel_id=1, source_target_pairs={{0,4},{4,0},{8,12},{12,8},{16,20},{20,16},{24,28},{28,24},{1,5},{5... | collective-permute-start | bytes 215048 | tf_op jit(solution)/shard_map/ppermute | solution.py:255
  73.6 3.9 %collective-permute-start.19 = (bf16[16,2240]{1,0:T(8,128)(2,1)S(1)}, bf16[16,2240]{1,0:T(8,128)(2,1)S(1)}, u32[]{:S(2)}, u32[]{:S(2)}) collective-permute-start(bf16[16,2240]{1,0:T(8,128)(2,1)S(1)} %get-tuple-element.37), channel_id=1, source_target_pairs={{0,4},{4,0},{8,12},{12,8},{16,20},{20,16},{24,28},{28,24},{1,5},{5... | collective-permute-start | bytes 215048 | tf_op jit(solution)/shard_map/ppermute | solution.py:255
  74.0 4.7 %collective-permute-start.20 = (bf16[16,2240]{1,0:T(8,128)(2,1)S(1)}, bf16[16,2240]{1,0:T(8,128)(2,1)S(1)}, u32[]{:S(2)}, u32[]{:S(2)}) collective-permute-start(bf16[16,2240]{1,0:T(8,128)(2,1)S(1)} %get-tuple-element.38), channel_id=1, source_target_pairs={{0,8},{4,12},{8,0},{12,4},{16,24},{20,28},{24,16},{28,20},{1,9},{5... | collective-permute-start | bytes 215048 | tf_op jit(solution)/shard_map/ppermute | solution.py:255
  75.1 13.6 %collective-permute-start.21 = (bf16[16,2240]{1,0:T(8,128)(2,1)S(1)}, bf16[16,2240]{1,0:T(8,128)(2,1)S(1)}, u32[]{:S(2)}, u32[]{:S(2)}) collective-permute-start(bf16[16,2240]{1,0:T(8,128)(2,1)S(1)} %get-tuple-element.39), channel_id=1, source_target_pairs={{0,12},{4,8},{8,4},{12,0},{16,28},{20,24},{24,20},{28,16},{1,13},{... | collective-permute-start | bytes 215048 | tf_op jit(solution)/shard_map/ppermute | solution.py:255
  75.5 13.2 %collective-permute-start.22 = (bf16[16,2240]{1,0:T(8,128)(2,1)S(1)}, bf16[16,2240]{1,0:T(8,128)(2,1)S(1)}, u32[]{:S(2)}, u32[]{:S(2)}) collective-permute-start(bf16[16,2240]{1,0:T(8,128)(2,1)S(1)} %get-tuple-element.40), channel_id=1, source_target_pairs={{0,16},{4,20},{8,24},{12,28},{16,0},{20,4},{24,8},{28,12},{1,17},{... | collective-permute-start | bytes 215048 | tf_op jit(solution)/shard_map/ppermute | solution.py:255
  76.2 12.5 %collective-permute-start.23 = (bf16[16,2240]{1,0:T(8,128)(2,1)S(1)}, bf16[16,2240]{1,0:T(8,128)(2,1)S(1)}, u32[]{:S(2)}, u32[]{:S(2)}) collective-permute-start(bf16[16,2240]{1,0:T(8,128)(2,1)S(1)} %get-tuple-element.41), channel_id=1, source_target_pairs={{0,20},{4,16},{8,28},{12,24},{16,4},{20,0},{24,12},{28,8},{1,21},{... | collective-permute-start | bytes 215048 | tf_op jit(solution)/shard_map/ppermute | solution.py:255
  77.5 11.3 %collective-permute-start.24 = (bf16[16,2240]{1,0:T(8,128)(2,1)S(1)}, bf16[16,2240]{1,0:T(8,128)(2,1)S(1)}, u32[]{:S(2)}, u32[]{:S(2)}) collective-permute-start(bf16[16,2240]{1,0:T(8,128)(2,1)S(1)} %get-tuple-element.42), channel_id=1, source_target_pairs={{0,24},{4,28},{8,16},{12,20},{16,8},{20,12},{24,0},{28,4},{1,25},{... | collective-permute-start | bytes 215048 | tf_op jit(solution)/shard_map/ppermute | solution.py:255
  78.7 10.1 %collective-permute-start.25 = (bf16[16,2240]{1,0:T(8,128)(2,1)S(1)}, bf16[16,2240]{1,0:T(8,128)(2,1)S(1)}, u32[]{:S(2)}, u32[]{:S(2)}) collective-permute-start(bf16[16,2240]{1,0:T(8,128)(2,1)S(1)} %get-tuple-element.43), channel_id=1, source_target_pairs={{0,28},{4,24},{8,20},{12,16},{16,12},{20,8},{24,4},{28,0},{1,29},{... | collective-permute-start | bytes 215048 | tf_op jit(solution)/shard_map/ppermute | solution.py:255
  79.9 28.6 %copy-start.2 = (bf16[2,220,2240]{2,0,1:T(2,128)(2,1)S(1)}, bf16[2,220,2240]{2,0,1:T(2,128)(2,1)}, u32[]{:S(2)}) copy-start(bf16[2,220,2240]{2,0,1:T(2,128)(2,1)} %param.9) | copy-start | bytes 5913604
  88.9 7.1 %collective-permute-start.28 = (bf16[16,2240]{1,0:T(8,128)(2,1)S(1)}, bf16[16,2240]{1,0:T(8,128)(2,1)S(1)}, u32[]{:S(2)}, u32[]{:S(2)}) collective-permute-start(bf16[16,2240]{1,0:T(8,128)(2,1)S(1)} %shard_map.81.refs_0_), channel_id=1, source_target_pairs={{0,3},{1,2},{2,1},{3,0},{4,7},{5,6},{6,5},{7,4},{8,11},{9,10},{10,... | collective-permute-start | bytes 215048 | tf_op jit(solution)/shard_map/ppermute | solution.py:255
  91.4 7.5 %collective-permute-start.27 = (bf16[16,2240]{1,0:T(8,128)(2,1)S(1)}, bf16[16,2240]{1,0:T(8,128)(2,1)S(1)}, u32[]{:S(2)}, u32[]{:S(2)}) collective-permute-start(bf16[16,2240]{1,0:T(8,128)(2,1)S(1)} %shard_map.81.refs_0_), channel_id=1, source_target_pairs={{0,2},{1,3},{2,0},{3,1},{4,6},{5,7},{6,4},{7,5},{8,10},{9,11},{10,... | collective-permute-start | bytes 215048 | tf_op jit(solution)/shard_map/ppermute | solution.py:255
  91.4 7.5 %collective-permute-start.26 = (bf16[16,2240]{1,0:T(8,128)(2,1)S(1)}, bf16[16,2240]{1,0:T(8,128)(2,1)S(1)}, u32[]{:S(2)}, u32[]{:S(2)}) collective-permute-start(bf16[16,2240]{1,0:T(8,128)(2,1)S(1)} %shard_map.81.refs_0_), channel_id=1, source_target_pairs={{0,1},{1,0},{2,3},{3,2},{4,5},{5,4},{6,7},{7,6},{8,9},{9,8},{10,11... | collective-permute-start | bytes 215048 | tf_op jit(solution)/shard_map/ppermute | solution.py:255
  (2 other events, 9.3 us)

commit v2 on v1

--- a/solution.py
+++ b/solution.py
@@ -18,7 +18,7 @@
 PARTS = E // ROWS
 COPY = 32
 F32, BF16 = jnp.float32, jnp.bfloat16
-PARAMS = pltpu.CompilerParams(vmem_limit_bytes=48 << 20)
+PARAMS = pltpu.CompilerParams(vmem_limit_bytes=24 << 20)
 
 
 def spans(width):
@@ -37,12 +37,17 @@
 
 
 def head_of_lane(rows, start, stop):
-    return (lax.broadcasted_iota(jnp.int32, (rows, stop - start), 1) + start) // E
-
-
-def picks(start, stop):
-    row = lax.broadcasted_iota(jnp.int32, (LANES, stop - start), 0)
-    return (row % COPY == head_of_lane(LANES, start, stop)) & (row < 3 * COPY)
+    lane = lax.broadcasted_iota(jnp.int32, (1, stop - start), 1) + start
+    head = jnp.full((1, stop - start), start // E, jnp.int32)
+    for h in range(start // E + 1, (stop - 1) // E + 1):
+        head += (lane >= h * E).astype(jnp.int32)
+    return jnp.broadcast_to(head, (rows, stop - start))
+
+
+def picks(start, stop, rows=LANES):
+    row = lax.broadcasted_iota(jnp.int32, (rows, 1), 0) & (LANES - 1)
+    slot = jnp.where(row < 3 * COPY, row & (COPY - 1), -1)
+    return jnp.broadcast_to(slot, (rows, stop - start)) == head_of_lane(rows, start, stop)
 
 
 def split(x):
@@ -65,8 +70,45 @@
     return block.reshape(block.shape[0] * block.shape[1], stop - start)
 
 
-def put(ref, start, stop, rows):
-    ref[:, :, start:stop] = rows.reshape(ref.shape[0], ref.shape[1], stop - start)
+def flat(ref):
+    tokens, frames, width = ref.shape
+    return ref.reshape(tokens * frames, width)
+
+
+def relay_kernel(*refs):
+    count = len(refs) // 2
+    in_refs, out_refs, sems = refs[:count], refs[count : 2 * count], refs[2 * count]
+    copies = [
+        pltpu.make_async_copy(flat(source), target, sems.at[i])
+        for i, (source, target) in enumerate(zip(in_refs, out_refs))
+    ]
+    for copy in copies:
+        copy.start()
+    for copy in copies:
+        copy.wait()
+
+
+class Leaving:
+    def __init__(self, source, target, sems):
+        self.source, self.target, self.sems, self.copies, self.held = source, flat(target), sems, [], None
+
+    def put(self, start, stop, rows):
+        self.source[:, start:stop] = rows
+        held, self.held = self.held, (start, stop)
+        if held:
+            self.send(*held)
+
+    def send(self, start, stop):
+        copy = pltpu.make_async_copy(
+            self.source.at[:, start:stop], self.target.at[:, start:stop], self.sems.at[len(self.copies)]
+        )
+        copy.start()
+        self.copies.append(copy)
+
+    def finish(self):
+        self.send(*self.held)
+        for copy in self.copies:
+            copy.wait()
 
 
 def write_messages(rank, state, total, sorted_ref, out_refs):
@@ -146,35 +188,47 @@
     out_ref[...] = added.astype(BF16)
 
 
-def query_kernel(rank_ref, queries_ref, grad_ref, taps_ref, message_ref, *refs):
-    n_next = len(refs) - PARTS - 4
+def query_kernel(frames, rank_ref, queries_ref, grad_ref, taps_ref, message_ref, *refs):
+    n_next = len(refs) - PARTS - 6
     next_refs, (numer_ref, inverse_ref, *refs) = refs[:n_next], refs[n_next:]
-    out_refs, (state, sorted_ref) = refs[:PARTS], refs[PARTS:]
-    tokens, frames, width = queries_ref.shape
-    rows = tokens * frames
+    out_refs, (state, sorted_ref, next_ref, sems) = refs[:PARTS], refs[PARTS:]
+    rows, width = queries_ref.shape
     blocks = spans(width)
+    arrivals = []
+    for i, (start, stop, *_) in enumerate(blocks):
+        first, copies = 0, []
+        for j, source in enumerate(next_refs):
+            source = flat(source)
+            last = first + source.shape[0]
+            target = next_ref.at[first:last, start:stop]
+            copies.append(pltpu.make_async_copy(source.at[:, start:stop], target, sems.at[j, i]))
+            copies[-1].start()
+            first = last
+        arrivals.append(copies)
     tot_high, tot_low = read_totals(message_ref)
     taps = taps_ref[...]
     taps = [taps[0:1] + 1.0, taps[1:2], taps[2:3]]
     state[...] = jnp.zeros_like(state)
-    feat = jnp.maximum(take(queries_ref, 0, width), 0)
-    denominator = jnp.full((rows, LANES), EPSILON, F32)
+    denominator = jnp.zeros((rows, 2 * LANES), F32)
     for start, stop, *_ in blocks:
-        pick = picks(start, stop)
-        for tot in (tot_high, tot_low):
-            weights = jnp.where(pick, tot[:, start:stop], 0.0).astype(BF16)
-            denominator += dot(feat[:, start:stop], weights, (1, 1))
+        row = lax.broadcasted_iota(jnp.int32, (2 * LANES, stop - start), 0)
+        tot = jnp.where(row < LANES, tot_high[:, start:stop], tot_low[:, start:stop])
+        weights = jnp.where(picks(start, stop, 2 * LANES), tot, 0.0).astype(BF16)
+        denominator += dot(jnp.maximum(queries_ref[:, start:stop], 0), weights, (1, 1))
+    denominator = denominator[:, :LANES] + denominator[:, LANES:] + EPSILON
     lane = lax.broadcasted_iota(jnp.int32, (rows, LANES), 1)
-    inverse = jnp.where((lane % COPY < H) & (lane < 3 * COPY), 1.0 / denominator, 0.0)
+    inverse = jnp.where(((lane & (COPY - 1)) < H) & (lane < 3 * COPY), 1.0 / denominator, 0.0)
     inverse_ref[...] = inverse
-    high, _ = split(inverse)
-    high = high.astype(F32)
+    high = inverse.astype(BF16).astype(F32)
     middle = (inverse - high).astype(BF16).astype(F32)
     spread = jnp.where(lane < COPY, high, jnp.where(lane < 2 * COPY, middle, inverse - high - middle)).astype(BF16)
-    for start, stop, *_ in blocks:
-        frame = lax.broadcasted_iota(jnp.int32, (rows, stop - start), 0) % frames
-        now = take(grad_ref, start, stop).astype(F32)
-        later = jnp.concatenate([take(ref, start, stop).astype(F32) for ref in next_refs], 0)
+    frame_of_row = lax.broadcasted_iota(jnp.int32, (rows, 1), 0) % frames
+    for i, (start, stop, *_) in enumerate(blocks):
+        for copy in arrivals[i]:
+            copy.wait()
+        frame = jnp.broadcast_to(frame_of_row, (rows, stop - start))
+        now = grad_ref[:, start:stop].astype(F32)
+        later = next_ref[:, start:stop].astype(F32)
         upstream = now * taps[0][:, start:stop]
         for lag in (1, 2):
             shifted = pltpu.roll(later, frames - lag, 0) if lag < frames else later
@@ -184,14 +238,14 @@
         upstream = upstream.astype(BF16).astype(F32)
         pick = jnp.where(picks(start, stop), 1.0, 0.0).astype(BF16)
         numer_ref[:, start:stop] = (upstream * dot(spread, pick, (1, 0))).astype(BF16)
-    add_outer(state, feat, numer_ref)
+    add_outer(state, jnp.maximum(queries_ref[...], 0), numer_ref)
     write_messages(rank_ref[0], state[...], jnp.zeros((1, width), F32), sorted_ref, out_refs)
 
 
 def query_grad_kernel(scale, rank_ref, queries_ref, numer_ref, inverse_ref, *refs):
-    message_refs, (out_ref, total_ref, state, sorted_ref, wide, across) = refs[:PARTS], refs[PARTS:]
-    tokens, frames, width = queries_ref.shape
-    rows = tokens * frames
+    message_refs, refs = refs[:PARTS], refs[PARTS:]
+    out_ref, total_ref, state, sorted_ref, wide, across, held, sems = refs
+    rows, width = queries_ref.shape
     blocks = spans(width)
     tot_high, tot_low = read_totals(message_refs[0])
     for d, ref in enumerate(message_refs):
@@ -203,18 +257,18 @@
     summed = jnp.zeros((rows, LANES), F32)
     for i, (start, stop, low, high, _) in enumerate(blocks):
         pick = jnp.where(picks(start, stop), 1.0, 0.0).astype(BF16)
-        feat = jnp.maximum(take(queries_ref, low, high), 0)
+        feat = jnp.maximum(queries_ref[:, low:high], 0)
         attended = dot(feat, wide[i, : high - low, : stop - start], (1, 0))
-        for part in split(numer_ref[:, start:stop].astype(F32) * attended):
-            summed += dot(part, pick, (1, 1))
+        summed += dot((numer_ref[:, start:stop].astype(F32) * attended).astype(BF16), pick, (1, 1))
     high, low = split(-summed * inverse_ref[...])
     high, low = high.astype(F32), low.astype(F32)
     lane = lax.broadcasted_iota(jnp.int32, (rows, LANES), 1)
     sides = jnp.where((lane >= COPY) & (lane < 2 * COPY), low, high)
     pairs = jnp.where(lane < 2 * COPY, sides, 0.0).astype(BF16)
     sides = sides.astype(BF16)
+    leaving = Leaving(held, out_ref, sems)
     for i, (start, stop, low, high, _) in enumerate(blocks):
-        queries = take(queries_ref, start, stop)
+        queries = queries_ref[:, start:stop]
         pick = picks(start, stop)
         terms = dot(pairs, jnp.maximum(queries, 0), (0, 0))
         terms = jnp.sum(jnp.where(pick, terms, 0.0), 0, keepdims=True)
@@ -223,27 +277,33 @@
         tot = jnp.where(row < 2 * COPY, tot_high[:, start:stop], tot_low[:, start:stop])
         tot = jnp.where(pick, tot, 0.0).astype(BF16)
         grad = dot(numer_ref[:, low:high], across[i, : stop - start, : high - low], (1, 1)) + dot(sides, tot, (1, 0))
-        put(out_ref, start, stop, jnp.where(queries.astype(F32) > 0, grad * scale, 0.0).astype(BF16))
-
-
-def key_grad_kernel(scale, keys_ref, values_ref, messages_ref, key_out, value_out, state, wide, across):
-    blocks = spans(keys_ref.shape[2])
+        leaving.put(start, stop, jnp.where(queries.astype(F32) > 0, grad * scale, 0.0).astype(BF16))
+    leaving.finish()
+
+
+def key_grad_kernel(scale, keys_ref, values_ref, messages_ref, key_out, value_out, *refs):
+    state, wide, across, key_held, value_held, key_sems, value_sems = refs
+    blocks = spans(keys_ref.shape[1])
     load_state(messages_ref, state)
     rows = messages_ref[0].astype(F32)
     for part in range(1, PARTS):
         rows = rows + messages_ref[part].astype(F32)
     row = lax.broadcasted_iota(jnp.int32, rows.shape, 0)
     total = jnp.sum(jnp.where(row >= ROWS, rows, 0.0), 0, keepdims=True)
+    key_leaving = Leaving(key_held, key_out, key_sems)
+    value_leaving = Leaving(value_held, value_out, value_sems)
     for i, block in enumerate(blocks):
-        across[i, : block[1] - block[0], : block[3] - block[2]] = rows_of(state, block)
-        wide[i, : block[3] - block[2], : block[1] - block[0]] = columns_of(state, block)
-    for i, (start, stop, low, high, _) in enumerate(blocks):
-        grad = dot(take(values_ref, low, high), across[i, : stop - start, : high - low], (1, 1)) + total[:, start:stop]
-        alive = take(keys_ref, start, stop).astype(F32) > 0
-        put(key_out, start, stop, jnp.where(alive, grad * scale, 0.0).astype(BF16))
-        feat = jnp.maximum(take(keys_ref, low, high), 0)
+        start, stop, low, high, _ = block
+        across[i, : stop - start, : high - low] = rows_of(state, block)
+        wide[i, : high - low, : stop - start] = columns_of(state, block)
+        grad = dot(values_ref[:, low:high], across[i, : stop - start, : high - low], (1, 1)) + total[:, start:stop]
+        alive = keys_ref[:, start:stop].astype(F32) > 0
+        key_leaving.put(start, stop, jnp.where(alive, grad * scale, 0.0).astype(BF16))
+        feat = jnp.maximum(keys_ref[:, low:high], 0)
         grad = dot(feat, wide[i, : high - low, : stop - start], (1, 0))
-        put(value_out, start, stop, (grad * scale).astype(BF16))
+        value_leaving.put(start, stop, (grad * scale).astype(BF16))
+    key_leaving.finish()
+    value_leaving.finish()
 
 
 def cost(flops, size):
@@ -275,8 +335,11 @@
 def over_groups(part):
     frames = lax.axis_size("frame")
     for axis, steps in (("frame", range(PARTS, frames, PARTS)), ("space", range(1, lax.axis_size("space")))):
-        if steps:
-            part = added([part] + [exchange(part, axis, d) for d in steps])
+        got = []
+        for d in steps:
+            got.append(exchange(part, axis, d))
+        if got:
+            part = added([part, *got])
     return part
 
 
@@ -301,10 +364,26 @@
     steps = 2 if tokens % 2 == 0 else 1
     per_step = pl.BlockSpec((tokens // steps, frames, width), lambda i: (i, 0, 0))
 
+    anywhere = pl.BlockSpec(memory_space=pl.ANY)
+    merged = jax.ShapeDtypeStruct((frames * tokens, width), BF16)
+    held = pltpu.VMEM(merged.shape, BF16)
+    sems = pltpu.SemaphoreType.DMA((len(spans(width)),))
+
+    def relay(*sources):
+        return pl.pallas_call(
+            relay_kernel,
+            in_specs=[anywhere] * len(sources),
+            out_specs=[vmem] * len(sources),
+            out_shape=[merged] * len(sources),
+            scratch_shapes=[pltpu.SemaphoreType.DMA((len(sources),))],
+            compiler_params=PARAMS,
+            cost_estimate=cost(0, 2 * size * len(sources)),
+        )(*sources)
+
     def halo(source):
         return lax.ppermute(source, "frame", [(i + 1, i) for i in range(devices - 1)])
 
-    early = tokens // 5
+    early = tokens * 2 // 5 // 8 * 8
     following = [halo(grad_out[:early])]
     key = pl.pallas_call(
         key_kernel,
@@ -318,37 +397,42 @@
     )
     state_messages = key(rank, saved_keys, saved_values)
     following.append(halo(grad_out[early:]))
+    query_rows, grad_rows = relay(saved_queries, grad_out)
     part = over_groups(added(spread_out(state_messages)))
     query = pl.pallas_call(
-        query_kernel,
-        in_specs=[smem] + [vmem] * (4 + len(following)),
-        out_shape=[jax.ShapeDtypeStruct((frames * tokens, width), BF16), jax.ShapeDtypeStruct((frames * tokens, LANES), F32)] + [message] * PARTS,
-        scratch_shapes=[state, ordered],
+        functools.partial(query_kernel, frames),
+        in_specs=[smem] + [vmem] * 4 + [anywhere] * len(following),
+        out_shape=[merged, jax.ShapeDtypeStruct((frames * tokens, LANES), F32)] + [message] * PARTS,
+        scratch_shapes=[state, ordered, held, pltpu.SemaphoreType.DMA((len(following), len(spans(width))))],
         compiler_params=PARAMS,
         cost_estimate=cost(size * 1024, 4 * size),
     )
-    numer, inverse, *grad_messages = query(rank, saved_queries, grad_out, conv_taps, part, *following)
+    numer, inverse, *grad_messages = query(rank, query_rows, grad_rows, conv_taps, part, *following)
     states = spread_out([part] * PARTS)
     grad_parts = spread_out(grad_messages)
     query_grad = pl.pallas_call(
         functools.partial(query_grad_kernel, scale),
         in_specs=[smem] + [vmem] * (3 + PARTS),
+        out_specs=[anywhere, vmem],
         out_shape=[array, jax.ShapeDtypeStruct((8, width), F32)],
-        scratch_shapes=[state, ordered, wide, across],
+        scratch_shapes=[state, ordered, wide, across, held, sems],
         compiler_params=PARAMS,
         cost_estimate=cost(size * 1024, 3 * size),
     )
-    grad_queries, total = query_grad(rank, saved_queries, numer, inverse, *states)
+    grad_queries, total = query_grad(rank, query_rows, numer, inverse, *states)
+    key_rows, value_rows = relay(saved_keys, saved_values)
     part = over_groups(added(grad_parts, total))
     groups = [list(range(i, i + PARTS)) for i in range(0, devices, PARTS)]
     grads = lax.all_gather(part, "frame", axis_index_groups=groups if len(groups) > 1 else None)
     grad_keys, grad_values = pl.pallas_call(
         functools.partial(key_grad_kernel, scale),
+        in_specs=[vmem] * 3,
+        out_specs=[anywhere] * 2,
         out_shape=[array, array],
-        scratch_shapes=[state, wide, across],
+        scratch_shapes=[state, wide, across, held, held, sems, sems],
         compiler_params=PARAMS,
         cost_estimate=cost(size * 1024, 4 * size),
-    )(saved_keys, saved_values, grads)
+    )(key_rows, value_rows, grads)
     return tuple(x.transpose(1, 0, 2) for x in (grad_queries, grad_keys, grad_values))
 
 

time: 116 us -> 112 us (0.966)
  waiting for transfers between devices: 31.6 us -> 25.7 us
  local copies, waits for them, and re-layouts: 6.7 us -> 7.88 us
    ppermute x27, waiting for transfers between devices: 31.6 us -> 25.7 us  [exchange(): return lax.ppermute(block, axis, [(i, i ^ distance) for i in devices])]
    unnamed x10 -> x14, local copies, waits for them, and re-layouts: 1.58 us -> 3.15 us
    pallas_call x3 -> x5, Pallas kernels: 28.1 us -> 28.7 us  [the longest x1 8.58 us: shards(): pl.pallas_call(functools.partial(key_grad_kernel, scale), in_specs=[vmem]...]
  transfers between devices with their start and end apart: 29 -> 29, of which waited for: 9 -> 7; matrix products, arithmetic and copies ran while one was open for 1% -> 1% of each run, Pallas kernels for 20% -> 20%
where the time goes in v2:
time: 112 us; the launch traced here: 111 us
  starting transfers between devices  35.8 us (32%)
  Pallas kernels  31.4 us (28%)
  waiting for transfers between devices  25.7 us (23%)
  blocking collectives  9.64 us (9%)
  local copies, waits for them, and re-layouts  7.88 us (7%)
    ppermute x27, starting transfers between devices, exchange(): return lax.ppermute(block, axis, [(i, i ^ distance) for i in devices])  33.2 us
    ppermute x27, waiting for transfers between devices, exchange(): return lax.ppermute(block, axis, [(i, i ^ distance) for i in devices])  25.7 us
    all_gather x1, blocking collectives, shards(): lax.all_gather(part, 'frame', axis_index_groups=groups if len(groups) > 1...  9.64 us
    pallas_call x1, Pallas kernels, shards(): pl.pallas_call(functools.partial(key_grad_kernel, scale), in_specs=[vmem]...  8.58 us
    pallas_call x1, Pallas kernels, shards(): grad_queries, total = query_grad(rank, query_rows, numer, inverse, *states)  7.88 us
    pallas_call x1, Pallas kernels, shards(): query(rank, query_rows, grad_rows, conv_taps, part, *following)  6.4 us
    pallas_call x2, Pallas kernels, relay(): pl.pallas_call(relay_kernel, in_specs=[anywhere] * len(sources), out_spec...  5.85 us
    slice x1, local copies, waits for them, and re-layouts, shards(): following.append(halo(grad_out[early:]))  3.29 us
  transfers between devices with their start and end apart: 29, of which 7 were waited for; matrix products, arithmetic and copies ran while one was open for 1% of the time, Pallas kernels for 20%

profile of v2, /device:TPU:0, one launch (start us, length us, event | category | flops | bytes accessed | tf_op | source)
XLA Modules:
  0.0 111.4 jit_solution(14330116955208352235)
XLA Ops:
  0.6 3.3 %slice.9 = bf16[132,2,2240]{2,1,0:T(2,128)(2,1)} slice(bf16[220,2,2240]{2,1,0:T(2,128)(2,1)} %bitcast.9), slice={[88:220], [0:2], [0:2240]} | slice | bytes 2365440 | tf_op jit(solution)/shard_map/slice | solution.py:399
  3.9 1.3 %collective-permute-start.11 = (bf16[132,2,2240]{2,1,0:T(2,128)(2,1)}, bf16[132,2,2240]{2,1,0:T(2,128)(2,1)S(1)}, u32[]{:S(2)}, u32[]{:S(2)}) collective-permute-start(bf16[132,2,2240]{2,1,0:T(2,128)(2,1)} %slice.9), channel_id=1, source_target_pairs={{4,0},{8,4},{12,8},{16,12},{20,16},{24,20},{28,24},{5,1},{9,5},{13... | collective-permute-start | bytes 3548168 | tf_op jit(solution)/shard_map/ppermute | solution.py:384
  5.2 1.4 %slice.8 = bf16[88,2,2240]{2,1,0:T(2,128)(2,1)} slice(bf16[220,2,2240]{2,1,0:T(2,128)(2,1)S(1)} %bitcast.10), slice={[0:88], [0:2], [0:2240]} | slice | bytes 1576960 | tf_op jit(solution)/shard_map/slice | solution.py:387
  6.7 1.3 %collective-permute-start.10 = (bf16[88,2,2240]{2,1,0:T(2,128)(2,1)}, bf16[88,2,2240]{2,1,0:T(2,128)(2,1)}, u32[]{:S(2)}, u32[]{:S(2)}) collective-permute-start(bf16[88,2,2240]{2,1,0:T(2,128)(2,1)} %slice.8), channel_id=1, source_target_pairs={{4,0},{8,4},{12,8},{16,12},{20,16},{24,20},{28,24},{5,1},{9,5},{13... | collective-permute-start | bytes 2365448 | tf_op jit(solution)/shard_map/ppermute | solution.py:384
  8.0 1.6 %copy-done.1 = bf16[2,220,2240]{2,0,1:T(2,128)(2,1)S(1)} copy-done((bf16[2,220,2240]{2,0,1:T(2,128)(2,1)S(1)}, bf16[2,220,2240]{2,0,1:T(2,128)(2,1)}, u32[]{:S(2)}) %copy-start.1) | copy-done | bytes 1971224
  9.5 1.6 %copy-done.3 = bf16[2,220,2240]{2,0,1:T(2,128)(2,1)S(1)} copy-done((bf16[2,220,2240]{2,0,1:T(2,128)(2,1)S(1)}, bf16[2,220,2240]{2,0,1:T(2,128)(2,1)}, u32[]{:S(2)}) %copy-start.3) | copy-done | bytes 1971224
  11.1 2.3 %shard_map.77 = (bf16[16,2240]{1,0:T(8,128)(2,1)S(1)}, bf16[16,2240]{1,0:T(8,128)(2,1)S(1)}, bf16[16,2240]{1,0:T(8,128)(2,1)S(1)}, bf16[16,2240]{1,0:T(8,128)(2,...) custom-call(s32[1]{0:T(128)} %bitcast.rank_ref, ...), custom_call_target="tpu_custom_call" | custom-call | flops 1009254400 | bytes 3942400 | tf_op jit(solution)/shard_map/pallas_call | solution.py:398
  13.4 1.8 %collective-permute-start = (bf16[16,2240]{1,0:T(8,128)(2,1)S(1)}, bf16[16,2240]{1,0:T(8,128)(2,1)S(1)}, u32[]{:S(2)}, u32[]{:S(2)}) collective-permute-start(bf16[16,2240]{1,0:T(8,128)(2,1)S(1)} %get-tuple-element.32), channel_id=1, source_target_pairs={{0,4},{4,0},{8,12},{12,8},{16,20},{20,16},{24,28},{28,24},{1,5},{5... | collective-permute-start | bytes 215048 | tf_op jit(solution)/shard_map/ppermute | solution.py:315
  15.3 3.0 %collective-permute-start.1 = (bf16[16,2240]{1,0:T(8,128)(2,1)S(1)}, bf16[16,2240]{1,0:T(8,128)(2,1)S(1)}, u32[]{:S(2)}, u32[]{:S(2)}) collective-permute-start(bf16[16,2240]{1,0:T(8,128)(2,1)S(1)} %get-tuple-element.33), channel_id=1, source_target_pairs={{0,8},{4,12},{8,0},{12,4},{16,24},{20,28},{24,16},{28,20},{1,9},{5... | collective-permute-start | bytes 215048 | tf_op jit(solution)/shard_map/ppermute | solution.py:315
  18.2 2.9 %collective-permute-start.3 = (bf16[16,2240]{1,0:T(8,128)(2,1)S(1)}, bf16[16,2240]{1,0:T(8,128)(2,1)S(1)}, u32[]{:S(2)}, u32[]{:S(2)}) collective-permute-start(bf16[16,2240]{1,0:T(8,128)(2,1)S(1)} %get-tuple-element.35), channel_id=1, source_target_pairs={{0,16},{4,20},{8,24},{12,28},{16,0},{20,4},{24,8},{28,12},{1,17},{... | collective-permute-start | bytes 215048 | tf_op jit(solution)/shard_map/ppermute | solution.py:315
  21.1 13.5 %collective-permute-done.1.refs_2_ = bf16[16,2240]{1,0:T(8,128)(2,1)S(1)} collective-permute-done((bf16[16,2240]{1,0:T(8,128)(2,1)S(1)}, bf16[16,2240]{1,0:T(8,128)(2,1)S(1)}, u32[]{:S(2)}, u32[]{:S(2)}) %collective-permute-start.1) | collective-permute-done | bytes 71712 | tf_op jit(solution)/shard_map/ppermute | solution.py:315
  34.6 2.4 %collective-permute-start.5 = (bf16[16,2240]{1,0:T(8,128)(2,1)S(1)}, bf16[16,2240]{1,0:T(8,128)(2,1)S(1)}, u32[]{:S(2)}, u32[]{:S(2)}) collective-permute-start(bf16[16,2240]{1,0:T(8,128)(2,1)S(1)} %get-tuple-element.37), channel_id=1, source_target_pairs={{0,24},{4,28},{8,16},{12,20},{16,8},{20,12},{24,0},{28,4},{1,25},{... | collective-permute-start | bytes 215048 | tf_op jit(solution)/shard_map/ppermute | solution.py:315
  37.0 1.5 %collective-permute-start.6 = (bf16[16,2240]{1,0:T(8,128)(2,1)S(1)}, bf16[16,2240]{1,0:T(8,128)(2,1)S(1)}, u32[]{:S(2)}, u32[]{:S(2)}) collective-permute-start(bf16[16,2240]{1,0:T(8,128)(2,1)S(1)} %get-tuple-element.38), channel_id=1, source_target_pairs={{0,28},{4,24},{8,20},{12,16},{16,12},{20,8},{24,4},{28,0},{1,29},{... | collective-permute-start | bytes 215048 | tf_op jit(solution)/shard_map/ppermute | solution.py:315
  40.1 1.9 %collective-permute-done.6.refs_7_ = bf16[16,2240]{1,0:T(8,128)(2,1)S(1)} collective-permute-done((bf16[16,2240]{1,0:T(8,128)(2,1)S(1)}, bf16[16,2240]{1,0:T(8,128)(2,1)S(1)}, u32[]{:S(2)}, u32[]{:S(2)}) %collective-permute-start.6) | collective-permute-done | bytes 71712 | tf_op jit(solution)/shard_map/ppermute | solution.py:315
  42.1 3.7 %collective-permute-start.9 = (bf16[16,2240]{1,0:T(8,128)(2,1)S(1)}, bf16[16,2240]{1,0:T(8,128)(2,1)S(1)}, u32[]{:S(2)}, u32[]{:S(2)}) collective-permute-start(bf16[16,2240]{1,0:T(8,128)(2,1)S(1)} %shard_map.78.refs_0_), channel_id=1, source_target_pairs={{0,3},{1,2},{2,1},{3,0},{4,7},{5,6},{6,5},{7,4},{8,11},{9,10},{10,... | collective-permute-start | bytes 215048 | tf_op jit(solution)/shard_map/ppermute | solution.py:315
  46.6 2.3 %collective-permute-done.9.refs_3_ = bf16[16,2240]{1,0:T(8,128)(2,1)S(1)} collective-permute-done((bf16[16,2240]{1,0:T(8,128)(2,1)S(1)}, bf16[16,2240]{1,0:T(8,128)(2,1)S(1)}, u32[]{:S(2)}, u32[]{:S(2)}) %collective-permute-start.9) | collective-permute-done | bytes 71712 | tf_op jit(solution)/shard_map/ppermute | solution.py:315
  48.9 3.5 %collective-permute-done.8.refs_2_ = bf16[16,2240]{1,0:T(8,128)(2,1)S(1)} collective-permute-done((bf16[16,2240]{1,0:T(8,128)(2,1)S(1)}, bf16[16,2240]{1,0:T(8,128)(2,1)S(1)}, u32[]{:S(2)}, u32[]{:S(2)}) %collective-permute-start.8) | collective-permute-done | bytes 71712 | tf_op jit(solution)/shard_map/ppermute | solution.py:315
  53.4 3.0 %shard_map.76 = (bf16[440,2240]{1,0:T(8,128)(2,1)S(1)}, bf16[440,2240]{1,0:T(8,128)(2,1)S(1)}) custom-call(bf16[220,2,2240]{2,1,0:T(2,128)(2,1)S(1)} %bitcast.16, bf16[220,2,2240]{2,1,0:T(2,128)(2,1)S(1)} %bitcast.11), custom_call_target="tpu_custom_call" | custom-call | bytes 7884800 | tf_op jit(solution)/shard_map/pallas_call | solution.py:373
  56.5 1.2 %collective-permute-start.17 = (bf16[16,2240]{1,0:T(8,128)(2,1)S(1)}, bf16[16,2240]{1,0:T(8,128)(2,1)S(1)}, u32[]{:S(2)}, u32[]{:S(2)}) collective-permute-start(bf16[16,2240]{1,0:T(8,128)(2,1)S(1)} %shard_map.79.message_ref.refs_0_), channel_id=1, source_target_pairs={{0,24},{4,28},{8,16},{12,20},{16,8},{20,12},{24,0},{28,4},{1,25},{... | collective-permute-start | bytes 215048 | tf_op jit(solution)/shard_map/ppermute | solution.py:315
  57.7 1.6 %collective-permute-start.16 = (bf16[16,2240]{1,0:T(8,128)(2,1)S(1)}, bf16[16,2240]{1,0:T(8,128)(2,1)S(1)}, u32[]{:S(2)}, u32[]{:S(2)}) collective-permute-start(bf16[16,2240]{1,0:T(8,128)(2,1)S(1)} %shard_map.79.message_ref.refs_0_), channel_id=1, source_target_pairs={{0,20},{4,16},{8,28},{12,24},{16,4},{20,0},{24,12},{28,8},{1,21},{... | collective-permute-start | bytes 215048 | tf_op jit(solution)/shard_map/ppermute | solution.py:315
  60.5 1.0 collective-permute-start.13
  61.5 6.4 %shard_map.80 = (bf16[440,2240]{1,0:T(8,128)(2,1)S(1)}, f32[440,128]{1,0:T(8,128)S(1)}, bf16[16,2240]{1,0:T(8,128)(2,1)S(1)}, bf16[16,2240]{1,0:T(8,128)(2,1)S(1...) custom-call(s32[1]{0:T(128)} %bitcast.rank_ref, ...), custom_call_target="tpu_custom_call" | custom-call | flops 2018508800 | bytes 7884800 | tf_op jit(solution)/shard_map/pallas_call | solution.py:410
  68.5 1.4 %collective-permute-start.20 = (bf16[16,2240]{1,0:T(8,128)(2,1)S(1)}, bf16[16,2240]{1,0:T(8,128)(2,1)S(1)}, u32[]{:S(2)}, u32[]{:S(2)}) collective-permute-start(bf16[16,2240]{1,0:T(8,128)(2,1)S(1)} %get-tuple-element.46), channel_id=1, source_target_pairs={{0,8},{4,12},{8,0},{12,4},{16,24},{20,28},{24,16},{28,20},{1,9},{5... | collective-permute-start | bytes 215048 | tf_op jit(solution)/shard_map/ppermute | solution.py:315
  70.3 1.2 %collective-permute-start.22 = (bf16[16,2240]{1,0:T(8,128)(2,1)S(1)}, bf16[16,2240]{1,0:T(8,128)(2,1)S(1)}, u32[]{:S(2)}, u32[]{:S(2)}) collective-permute-start(bf16[16,2240]{1,0:T(8,128)(2,1)S(1)} %get-tuple-element.48), channel_id=1, source_target_pairs={{0,16},{4,20},{8,24},{12,28},{16,0},{20,4},{24,8},{28,12},{1,17},{... | collective-permute-start | bytes 215048 | tf_op jit(solution)/shard_map/ppermute | solution.py:315
  72.0 1.8 %collective-permute-start.24 = (bf16[16,2240]{1,0:T(8,128)(2,1)S(1)}, bf16[16,2240]{1,0:T(8,128)(2,1)S(1)}, u32[]{:S(2)}, u32[]{:S(2)}) collective-permute-start(bf16[16,2240]{1,0:T(8,128)(2,1)S(1)} %get-tuple-element.50), channel_id=1, source_target_pairs={{0,24},{4,28},{8,16},{12,20},{16,8},{20,12},{24,0},{28,4},{1,25},{... | collective-permute-start | bytes 215048 | tf_op jit(solution)/shard_map/ppermute | solution.py:315
  74.7 7.9 %shard_map.81 = (bf16[220,2,2240]{2,1,0:T(2,128)(2,1)}, f32[8,2240]{1,0:T(8,128)S(1)}) custom-call(s32[1]{0:T(128)} %bitcast.rank_ref, bf16[440,2240]{1,0:T(8,128)(2,1)S(1)} %get-tuple-element.29.queries_ref, bf16[440,2240]{1,0:T(8,128)(2,1)S(1)} %get-tuple-element.39.numer_ref, f32[440,128]{1,0:T(8,128)S(1)} %get-tuple-element.40.inverse_ref, ...), custom_call_target="tpu_custom_call" | custom-call | flops 2018508800 | bytes 5913600 | tf_op jit(solution)/shard_map/pallas_call | solution.py:422
  82.8 2.5 %collective-permute-start.28 = (bf16[16,2240]{1,0:T(8,128)(2,1)S(1)}, bf16[16,2240]{1,0:T(8,128)(2,1)S(1)}, u32[]{:S(2)}, u32[]{:S(2)}) collective-permute-start(bf16[16,2240]{1,0:T(8,128)(2,1)S(1)} %shard_map.83.refs_0_), channel_id=1, source_target_pairs={{0,3},{1,2},{2,1},{3,0},{4,7},{5,6},{6,5},{7,4},{8,11},{9,10},{10,... | collective-permute-start | bytes 215048 | tf_op jit(solution)/shard_map/ppermute | solution.py:315
  85.3 1.9 %collective-permute-start.26 = (bf16[16,2240]{1,0:T(8,128)(2,1)S(1)}, bf16[16,2240]{1,0:T(8,128)(2,1)S(1)}, u32[]{:S(2)}, u32[]{:S(2)}) collective-permute-start(bf16[16,2240]{1,0:T(8,128)(2,1)S(1)} %shard_map.83.refs_0_), channel_id=1, source_target_pairs={{0,1},{1,0},{2,3},{3,2},{4,5},{5,4},{6,7},{7,6},{8,9},{9,8},{10,11... | collective-permute-start | bytes 215048 | tf_op jit(solution)/shard_map/ppermute | solution.py:315
  87.2 2.8 %shard_map.82 = (bf16[440,2240]{1,0:T(8,128)(2,1)S(1)}, bf16[440,2240]{1,0:T(8,128)(2,1)S(1)}) custom-call(bf16[220,2,2240]{2,1,0:T(2,128)(2,1)S(1)} %bitcast.13, bf16[220,2,2240]{2,1,0:T(2,128)(2,1)S(1)} %bitcast.15), custom_call_target="tpu_custom_call" | custom-call | bytes 7884800 | tf_op jit(solution)/shard_map/pallas_call | solution.py:373
  90.1 2.9 %collective-permute-done.27.refs_2_ = bf16[16,2240]{1,0:T(8,128)(2,1)S(1)} collective-permute-done((bf16[16,2240]{1,0:T(8,128)(2,1)S(1)}, bf16[16,2240]{1,0:T(8,128)(2,1)S(1)}, u32[]{:S(2)}, u32[]{:S(2)}) %collective-permute-start.27) | collective-permute-done | bytes 71712 | tf_op jit(solution)/shard_map/ppermute | solution.py:315
  93.0 9.6 %all-gather = bf16[128,2240]{1,0:T(8,128)(2,1)S(1)} all-gather(bf16[16,2240]{1,0:T(8,128)(2,1)S(1)} %shard_map.84), channel_id=2, replica_groups=mesh['frame'=8,'space'=4] {'frame'}, dimensions={0}, use_global_device_ids=true | all-gather | bytes 645120 | tf_op jit(solution)/shard_map/all_gather | solution.py:426
  102.7 8.6 %shard_map.85 = (bf16[220,2,2240]{2,1,0:T(2,128)(2,1)}, bf16[220,2,2240]{2,1,0:T(2,128)(2,1)}) custom-call(bf16[440,2240]{1,0:T(8,128)(2,1)S(1)} %get-tuple-element.42.keys_ref, bf16[440,2240]{1,0:T(8,128)(2,1)S(1)} %get-tuple-element.43.values_ref, bf16[8,16,2240]{2,1,0:T(8,128)(2,1)S(1)} %bitcast.17), custom_call_target="tpu_custom_call" | custom-call | flops 2018508800 | bytes 7884800 | tf_op jit(solution)/shard_map/pallas_call | solution.py:427
  (53 shorter events, 7.3 us)
Async XLA Ops:
  3.9 56.5 %collective-permute-start.11 = (bf16[132,2,2240]{2,1,0:T(2,128)(2,1)}, bf16[132,2,2240]{2,1,0:T(2,128)(2,1)S(1)}, u32[]{:S(2)}, u32[]{:S(2)}) collective-permute-start(bf16[132,2,2240]{2,1,0:T(2,128)(2,1)} %slice.9), channel_id=1, source_target_pairs={{4,0},{8,4},{12,8},{16,12},{20,16},{24,20},{28,24},{5,1},{9,5},{13... | collective-permute-start | bytes 3548168 | tf_op jit(solution)/shard_map/ppermute | solution.py:384
  6.7 53.4 %collective-permute-start.10 = (bf16[88,2,2240]{2,1,0:T(2,128)(2,1)}, bf16[88,2,2240]{2,1,0:T(2,128)(2,1)}, u32[]{:S(2)}, u32[]{:S(2)}) collective-permute-start(bf16[88,2,2240]{2,1,0:T(2,128)(2,1)} %slice.8), channel_id=1, source_target_pairs={{4,0},{8,4},{12,8},{16,12},{20,16},{24,20},{28,24},{5,1},{9,5},{13... | collective-permute-start | bytes 2365448 | tf_op jit(solution)/shard_map/ppermute | solution.py:384
  11.1 42.3 %copy-start.5 = (bf16[2,220,2240]{2,0,1:T(2,128)(2,1)S(1)}, bf16[2,220,2240]{2,0,1:T(2,128)(2,1)}, u32[]{:S(2)}) copy-start(bf16[2,220,2240]{2,0,1:T(2,128)(2,1)} %param.7) | copy-start | bytes 5913604
  13.4 4.8 %collective-permute-start = (bf16[16,2240]{1,0:T(8,128)(2,1)S(1)}, bf16[16,2240]{1,0:T(8,128)(2,1)S(1)}, u32[]{:S(2)}, u32[]{:S(2)}) collective-permute-start(bf16[16,2240]{1,0:T(8,128)(2,1)S(1)} %get-tuple-element.32), channel_id=1, source_target_pairs={{0,4},{4,0},{8,12},{12,8},{16,20},{20,16},{24,28},{28,24},{1,5},{5... | collective-permute-start | bytes 215048 | tf_op jit(solution)/shard_map/ppermute | solution.py:315
  15.3 19.4 %collective-permute-start.1 = (bf16[16,2240]{1,0:T(8,128)(2,1)S(1)}, bf16[16,2240]{1,0:T(8,128)(2,1)S(1)}, u32[]{:S(2)}, u32[]{:S(2)}) collective-permute-start(bf16[16,2240]{1,0:T(8,128)(2,1)S(1)} %get-tuple-element.33), channel_id=1, source_target_pairs={{0,8},{4,12},{8,0},{12,4},{16,24},{20,28},{24,16},{28,20},{1,9},{5... | collective-permute-start | bytes 215048 | tf_op jit(solution)/shard_map/ppermute | solution.py:315
  18.2 16.4 %collective-permute-start.2 = (bf16[16,2240]{1,0:T(8,128)(2,1)S(1)}, bf16[16,2240]{1,0:T(8,128)(2,1)S(1)}, u32[]{:S(2)}, u32[]{:S(2)}) collective-permute-start(bf16[16,2240]{1,0:T(8,128)(2,1)S(1)} %get-tuple-element.34), channel_id=1, source_target_pairs={{0,12},{4,8},{8,4},{12,0},{16,28},{20,24},{24,20},{28,16},{1,13},{... | collective-permute-start | bytes 215048 | tf_op jit(solution)/shard_map/ppermute | solution.py:315
  18.2 18.8 %collective-permute-start.3 = (bf16[16,2240]{1,0:T(8,128)(2,1)S(1)}, bf16[16,2240]{1,0:T(8,128)(2,1)S(1)}, u32[]{:S(2)}, u32[]{:S(2)}) collective-permute-start(bf16[16,2240]{1,0:T(8,128)(2,1)S(1)} %get-tuple-element.35), channel_id=1, source_target_pairs={{0,16},{4,20},{8,24},{12,28},{16,0},{20,4},{24,8},{28,12},{1,17},{... | collective-permute-start | bytes 215048 | tf_op jit(solution)/shard_map/ppermute | solution.py:315
  34.6 4.5 %collective-permute-start.4 = (bf16[16,2240]{1,0:T(8,128)(2,1)S(1)}, bf16[16,2240]{1,0:T(8,128)(2,1)S(1)}, u32[]{:S(2)}, u32[]{:S(2)}) collective-permute-start(bf16[16,2240]{1,0:T(8,128)(2,1)S(1)} %get-tuple-element.36), channel_id=1, source_target_pairs={{0,20},{4,16},{8,28},{12,24},{16,4},{20,0},{24,12},{28,8},{1,21},{... | collective-permute-start | bytes 215048 | tf_op jit(solution)/shard_map/ppermute | solution.py:315
  34.6 5.5 %collective-permute-start.5 = (bf16[16,2240]{1,0:T(8,128)(2,1)S(1)}, bf16[16,2240]{1,0:T(8,128)(2,1)S(1)}, u32[]{:S(2)}, u32[]{:S(2)}) collective-permute-start(bf16[16,2240]{1,0:T(8,128)(2,1)S(1)} %get-tuple-element.37), channel_id=1, source_target_pairs={{0,24},{4,28},{8,16},{12,20},{16,8},{20,12},{24,0},{28,4},{1,25},{... | collective-permute-start | bytes 215048 | tf_op jit(solution)/shard_map/ppermute | solution.py:315
  37.0 5.0 %collective-permute-start.6 = (bf16[16,2240]{1,0:T(8,128)(2,1)S(1)}, bf16[16,2240]{1,0:T(8,128)(2,1)S(1)}, u32[]{:S(2)}, u32[]{:S(2)}) collective-permute-start(bf16[16,2240]{1,0:T(8,128)(2,1)S(1)} %get-tuple-element.38), channel_id=1, source_target_pairs={{0,28},{4,24},{8,20},{12,16},{16,12},{20,8},{24,4},{28,0},{1,29},{... | collective-permute-start | bytes 215048 | tf_op jit(solution)/shard_map/ppermute | solution.py:315
  42.1 6.8 %collective-permute-start.9 = (bf16[16,2240]{1,0:T(8,128)(2,1)S(1)}, bf16[16,2240]{1,0:T(8,128)(2,1)S(1)}, u32[]{:S(2)}, u32[]{:S(2)}) collective-permute-start(bf16[16,2240]{1,0:T(8,128)(2,1)S(1)} %shard_map.78.refs_0_), channel_id=1, source_target_pairs={{0,3},{1,2},{2,1},{3,0},{4,7},{5,6},{6,5},{7,4},{8,11},{9,10},{10,... | collective-permute-start | bytes 215048 | tf_op jit(solution)/shard_map/ppermute | solution.py:315
  45.8 6.6 %collective-permute-start.8 = (bf16[16,2240]{1,0:T(8,128)(2,1)S(1)}, bf16[16,2240]{1,0:T(8,128)(2,1)S(1)}, u32[]{:S(2)}, u32[]{:S(2)}) collective-permute-start(bf16[16,2240]{1,0:T(8,128)(2,1)S(1)} %shard_map.78.refs_0_), channel_id=1, source_target_pairs={{0,2},{1,3},{2,0},{3,1},{4,6},{5,7},{6,4},{7,5},{8,10},{9,11},{10,... | collective-permute-start | bytes 215048 | tf_op jit(solution)/shard_map/ppermute | solution.py:315
  45.8 6.6 %collective-permute-start.7 = (bf16[16,2240]{1,0:T(8,128)(2,1)S(1)}, bf16[16,2240]{1,0:T(8,128)(2,1)S(1)}, u32[]{:S(2)}, u32[]{:S(2)}) collective-permute-start(bf16[16,2240]{1,0:T(8,128)(2,1)S(1)} %shard_map.78.refs_0_), channel_id=1, source_target_pairs={{0,1},{1,0},{2,3},{3,2},{4,5},{5,4},{6,7},{7,6},{8,9},{9,8},{10,11... | collective-permute-start | bytes 215048 | tf_op jit(solution)/shard_map/ppermute | solution.py:315
  52.5 6.8 %collective-permute-start.18 = (bf16[16,2240]{1,0:T(8,128)(2,1)S(1)}, bf16[16,2240]{1,0:T(8,128)(2,1)S(1)}, u32[]{:S(2)}, u32[]{:S(2)}) collective-permute-start(bf16[16,2240]{1,0:T(8,128)(2,1)S(1)} %shard_map.79.message_ref.refs_0_), channel_id=1, source_target_pairs={{0,28},{4,24},{8,20},{12,16},{16,12},{20,8},{24,4},{28,0},{1,29},{... | collective-permute-start | bytes 215048 | tf_op jit(solution)/shard_map/ppermute | solution.py:315
  56.5 11.5 %collective-permute-start.17 = (bf16[16,2240]{1,0:T(8,128)(2,1)S(1)}, bf16[16,2240]{1,0:T(8,128)(2,1)S(1)}, u32[]{:S(2)}, u32[]{:S(2)}) collective-permute-start(bf16[16,2240]{1,0:T(8,128)(2,1)S(1)} %shard_map.79.message_ref.refs_0_), channel_id=1, source_target_pairs={{0,24},{4,28},{8,16},{12,20},{16,8},{20,12},{24,0},{28,4},{1,25},{... | collective-permute-start | bytes 215048 | tf_op jit(solution)/shard_map/ppermute | solution.py:315
  57.7 10.7 %collective-permute-start.16 = (bf16[16,2240]{1,0:T(8,128)(2,1)S(1)}, bf16[16,2240]{1,0:T(8,128)(2,1)S(1)}, u32[]{:S(2)}, u32[]{:S(2)}) collective-permute-start(bf16[16,2240]{1,0:T(8,128)(2,1)S(1)} %shard_map.79.message_ref.refs_0_), channel_id=1, source_target_pairs={{0,20},{4,16},{8,28},{12,24},{16,4},{20,0},{24,12},{28,8},{1,21},{... | collective-permute-start | bytes 215048 | tf_op jit(solution)/shard_map/ppermute | solution.py:315
  59.3 9.2 %collective-permute-start.15 = (bf16[16,2240]{1,0:T(8,128)(2,1)S(1)}, bf16[16,2240]{1,0:T(8,128)(2,1)S(1)}, u32[]{:S(2)}, u32[]{:S(2)}) collective-permute-start(bf16[16,2240]{1,0:T(8,128)(2,1)S(1)} %shard_map.79.message_ref.refs_0_), channel_id=1, source_target_pairs={{0,16},{4,20},{8,24},{12,28},{16,0},{20,4},{24,8},{28,12},{1,17},{... | collective-permute-start | bytes 215048 | tf_op jit(solution)/shard_map/ppermute | solution.py:315
  60.1 9.8 %collective-permute-start.14 = (bf16[16,2240]{1,0:T(8,128)(2,1)S(1)}, bf16[16,2240]{1,0:T(8,128)(2,1)S(1)}, u32[]{:S(2)}, u32[]{:S(2)}) collective-permute-start(bf16[16,2240]{1,0:T(8,128)(2,1)S(1)} %shard_map.79.message_ref.refs_0_), channel_id=1, source_target_pairs={{0,12},{4,8},{8,4},{12,0},{16,28},{20,24},{24,20},{28,16},{1,13},{... | collective-permute-start | bytes 215048 | tf_op jit(solution)/shard_map/ppermute | solution.py:315
  60.5 9.8 %collective-permute-start.13 = (bf16[16,2240]{1,0:T(8,128)(2,1)S(1)}, bf16[16,2240]{1,0:T(8,128)(2,1)S(1)}, u32[]{:S(2)}, u32[]{:S(2)}) collective-permute-start(bf16[16,2240]{1,0:T(8,128)(2,1)S(1)} %shard_map.79.message_ref.refs_0_), channel_id=1, source_target_pairs={{0,8},{4,12},{8,0},{12,4},{16,24},{20,28},{24,16},{28,20},{1,9},{5... | collective-permute-start | bytes 215048 | tf_op jit(solution)/shard_map/ppermute | solution.py:315
  67.9 3.6 %collective-permute-start.12 = (bf16[16,2240]{1,0:T(8,128)(2,1)S(1)}, bf16[16,2240]{1,0:T(8,128)(2,1)S(1)}, u32[]{:S(2)}, u32[]{:S(2)}) collective-permute-start(bf16[16,2240]{1,0:T(8,128)(2,1)S(1)} %shard_map.79.message_ref.refs_0_), channel_id=1, source_target_pairs={{0,4},{4,0},{8,12},{12,8},{16,20},{20,16},{24,28},{28,24},{1,5},{5... | collective-permute-start | bytes 215048 | tf_op jit(solution)/shard_map/ppermute | solution.py:315
  68.4 3.6 %collective-permute-start.19 = (bf16[16,2240]{1,0:T(8,128)(2,1)S(1)}, bf16[16,2240]{1,0:T(8,128)(2,1)S(1)}, u32[]{:S(2)}, u32[]{:S(2)}) collective-permute-start(bf16[16,2240]{1,0:T(8,128)(2,1)S(1)} %get-tuple-element.45), channel_id=1, source_target_pairs={{0,4},{4,0},{8,12},{12,8},{16,20},{20,16},{24,28},{28,24},{1,5},{5... | collective-permute-start | bytes 215048 | tf_op jit(solution)/shard_map/ppermute | solution.py:315
  68.5 5.3 %collective-permute-start.20 = (bf16[16,2240]{1,0:T(8,128)(2,1)S(1)}, bf16[16,2240]{1,0:T(8,128)(2,1)S(1)}, u32[]{:S(2)}, u32[]{:S(2)}) collective-permute-start(bf16[16,2240]{1,0:T(8,128)(2,1)S(1)} %get-tuple-element.46), channel_id=1, source_target_pairs={{0,8},{4,12},{8,0},{12,4},{16,24},{20,28},{24,16},{28,20},{1,9},{5... | collective-permute-start | bytes 215048 | tf_op jit(solution)/shard_map/ppermute | solution.py:315
  69.9 12.7 %collective-permute-start.21 = (bf16[16,2240]{1,0:T(8,128)(2,1)S(1)}, bf16[16,2240]{1,0:T(8,128)(2,1)S(1)}, u32[]{:S(2)}, u32[]{:S(2)}) collective-permute-start(bf16[16,2240]{1,0:T(8,128)(2,1)S(1)} %get-tuple-element.47), channel_id=1, source_target_pairs={{0,12},{4,8},{8,4},{12,0},{16,28},{20,24},{24,20},{28,16},{1,13},{... | collective-permute-start | bytes 215048 | tf_op jit(solution)/shard_map/ppermute | solution.py:315
  70.3 12.3 %collective-permute-start.22 = (bf16[16,2240]{1,0:T(8,128)(2,1)S(1)}, bf16[16,2240]{1,0:T(8,128)(2,1)S(1)}, u32[]{:S(2)}, u32[]{:S(2)}) collective-permute-start(bf16[16,2240]{1,0:T(8,128)(2,1)S(1)} %get-tuple-element.48), channel_id=1, source_target_pairs={{0,16},{4,20},{8,24},{12,28},{16,0},{20,4},{24,8},{28,12},{1,17},{... | collective-permute-start | bytes 215048 | tf_op jit(solution)/shard_map/ppermute | solution.py:315
  71.5 11.1 %collective-permute-start.23 = (bf16[16,2240]{1,0:T(8,128)(2,1)S(1)}, bf16[16,2240]{1,0:T(8,128)(2,1)S(1)}, u32[]{:S(2)}, u32[]{:S(2)}) collective-permute-start(bf16[16,2240]{1,0:T(8,128)(2,1)S(1)} %get-tuple-element.49), channel_id=1, source_target_pairs={{0,20},{4,16},{8,28},{12,24},{16,4},{20,0},{24,12},{28,8},{1,21},{... | collective-permute-start | bytes 215048 | tf_op jit(solution)/shard_map/ppermute | solution.py:315
  72.0 10.6 %collective-permute-start.24 = (bf16[16,2240]{1,0:T(8,128)(2,1)S(1)}, bf16[16,2240]{1,0:T(8,128)(2,1)S(1)}, u32[]{:S(2)}, u32[]{:S(2)}) collective-permute-start(bf16[16,2240]{1,0:T(8,128)(2,1)S(1)} %get-tuple-element.50), channel_id=1, source_target_pairs={{0,24},{4,28},{8,16},{12,20},{16,8},{20,12},{24,0},{28,4},{1,25},{... | collective-permute-start | bytes 215048 | tf_op jit(solution)/shard_map/ppermute | solution.py:315
  73.8 8.8 %collective-permute-start.25 = (bf16[16,2240]{1,0:T(8,128)(2,1)S(1)}, bf16[16,2240]{1,0:T(8,128)(2,1)S(1)}, u32[]{:S(2)}, u32[]{:S(2)}) collective-permute-start(bf16[16,2240]{1,0:T(8,128)(2,1)S(1)} %get-tuple-element.51), channel_id=1, source_target_pairs={{0,28},{4,24},{8,20},{12,16},{16,12},{20,8},{24,4},{28,0},{1,29},{... | collective-permute-start | bytes 215048 | tf_op jit(solution)/shard_map/ppermute | solution.py:315
  74.7 12.5 %copy-start.2 = (bf16[2,220,2240]{2,0,1:T(2,128)(2,1)S(1)}, bf16[2,220,2240]{2,0,1:T(2,128)(2,1)}, u32[]{:S(2)}) copy-start(bf16[2,220,2240]{2,0,1:T(2,128)(2,1)} %param.8) | copy-start | bytes 5913604
  74.7 12.5 %copy-start.4 = (bf16[2,220,2240]{2,0,1:T(2,128)(2,1)S(1)}, bf16[2,220,2240]{2,0,1:T(2,128)(2,1)}, u32[]{:S(2)}) copy-start(bf16[2,220,2240]{2,0,1:T(2,128)(2,1)} %param.9) | copy-start | bytes 5913604
  82.8 7.3 %collective-permute-start.28 = (bf16[16,2240]{1,0:T(8,128)(2,1)S(1)}, bf16[16,2240]{1,0:T(8,128)(2,1)S(1)}, u32[]{:S(2)}, u32[]{:S(2)}) collective-permute-start(bf16[16,2240]{1,0:T(8,128)(2,1)S(1)} %shard_map.83.refs_0_), channel_id=1, source_target_pairs={{0,3},{1,2},{2,1},{3,0},{4,7},{5,6},{6,5},{7,4},{8,11},{9,10},{10,... | collective-permute-start | bytes 215048 | tf_op jit(solution)/shard_map/ppermute | solution.py:315
  85.3 7.6 %collective-permute-start.27 = (bf16[16,2240]{1,0:T(8,128)(2,1)S(1)}, bf16[16,2240]{1,0:T(8,128)(2,1)S(1)}, u32[]{:S(2)}, u32[]{:S(2)}) collective-permute-start(bf16[16,2240]{1,0:T(8,128)(2,1)S(1)} %shard_map.83.refs_0_), channel_id=1, source_target_pairs={{0,2},{1,3},{2,0},{3,1},{4,6},{5,7},{6,4},{7,5},{8,10},{9,11},{10,... | collective-permute-start | bytes 215048 | tf_op jit(solution)/shard_map/ppermute | solution.py:315
  85.3 7.6 %collective-permute-start.26 = (bf16[16,2240]{1,0:T(8,128)(2,1)S(1)}, bf16[16,2240]{1,0:T(8,128)(2,1)S(1)}, u32[]{:S(2)}, u32[]{:S(2)}) collective-permute-start(bf16[16,2240]{1,0:T(8,128)(2,1)S(1)} %shard_map.83.refs_0_), channel_id=1, source_target_pairs={{0,1},{1,0},{2,3},{3,2},{4,5},{5,4},{6,7},{7,6},{8,9},{9,8},{10,11... | collective-permute-start | bytes 215048 | tf_op jit(solution)/shard_map/ppermute | solution.py:315
  (4 other events, 15.8 us)

commit v3 on v2

--- a/solution.py
+++ b/solution.py
@@ -18,6 +18,7 @@
 PARTS = E // ROWS
 COPY = 32
 F32, BF16 = jnp.float32, jnp.bfloat16
+LARGE = pltpu.CompilerParams(vmem_limit_bytes=60 << 20)
 PARAMS = pltpu.CompilerParams(vmem_limit_bytes=24 << 20)
 
 
@@ -63,11 +64,6 @@
         for h in heads:
             part = jnp.where(owner == h, product[h * E - low : (h + 1) * E - low], part)
         state[:, start:stop] += part
-
-
-def take(ref, start, stop):
-    block = ref[:, :, start:stop]
-    return block.reshape(block.shape[0] * block.shape[1], stop - start)
 
 
 def flat(ref):
@@ -90,25 +86,26 @@
 
 class Leaving:
     def __init__(self, source, target, sems):
-        self.source, self.target, self.sems, self.copies, self.held = source, flat(target), sems, [], None
-
-    def put(self, start, stop, rows):
+        self.source, self.target, self.sems, self.copies, self.sent = source, flat(target), sems, [], 0
+
+    def put(self, start, stop, rows, send):
         self.source[:, start:stop] = rows
-        held, self.held = self.held, (start, stop)
-        if held:
-            self.send(*held)
-
-    def send(self, start, stop):
-        copy = pltpu.make_async_copy(
-            self.source.at[:, start:stop], self.target.at[:, start:stop], self.sems.at[len(self.copies)]
-        )
-        copy.start()
-        self.copies.append(copy)
+        if send:
+            columns = slice(self.sent, stop)
+            copy = pltpu.make_async_copy(
+                self.source.at[:, columns], self.target.at[:, columns], self.sems.at[len(self.copies)]
+            )
+            copy.start()
+            self.copies.append(copy)
+            self.sent = stop
 
     def finish(self):
-        self.send(*self.held)
         for copy in self.copies:
             copy.wait()
+
+
+def last_of(i, count, pieces):
+    return (i + 1) * pieces // count > i * pieces // count
 
 
 def write_messages(rank, state, total, sorted_ref, out_refs):
@@ -153,22 +150,25 @@
 
 
 def key_kernel(rank_ref, keys_ref, values_ref, *refs):
-    out_refs, (state, total, sorted_ref) = refs[:PARTS], refs[PARTS:]
-    step = pl.program_id(0)
-
-    @pl.when(step == 0)
-    def _():
-        state[...] = jnp.zeros_like(state)
-        total[...] = jnp.zeros_like(total)
-
-    width = keys_ref.shape[2]
-    feat = jnp.maximum(take(keys_ref, 0, width), 0)
-    add_outer(state, feat, take(values_ref, 0, width))
-    total[...] += dot(jnp.ones((8, feat.shape[0]), BF16), feat, (1, 0))
-
-    @pl.when(step == pl.num_programs(0) - 1)
-    def _():
-        write_messages(rank_ref[0], state[...], total[:1], sorted_ref, out_refs)
+    out_refs, (state, total, sorted_ref, key_rows, value_rows, sems) = refs[:PARTS], refs[PARTS:]
+    tokens, frames, _ = keys_ref.shape
+    cuts = [0, tokens // 16 * 8, tokens]
+    arrivals = []
+    for first, last in zip(cuts, cuts[1:]):
+        rows = slice(first * frames, last * frames)
+        for source, target in ((keys_ref, key_rows), (values_ref, value_rows)):
+            arrivals.append(pltpu.make_async_copy(flat(source).at[rows], target.at[rows], sems.at[len(arrivals)]))
+            arrivals[-1].start()
+    state[...] = jnp.zeros_like(state)
+    total[...] = jnp.zeros_like(total)
+    for i, (first, last) in enumerate(zip(cuts, cuts[1:])):
+        rows = slice(first * frames, last * frames)
+        for copy in arrivals[2 * i : 2 * i + 2]:
+            copy.wait()
+        feat = jnp.maximum(key_rows[rows], 0)
+        add_outer(state, feat, value_rows.at[rows])
+        total[...] += dot(jnp.ones((8, feat.shape[0]), BF16), feat, (1, 0))
+    write_messages(rank_ref[0], state[...], total[:1], sorted_ref, out_refs)
 
 
 def sum_kernel(n_total, *refs):
@@ -188,29 +188,11 @@
     out_ref[...] = added.astype(BF16)
 
 
-def query_kernel(frames, rank_ref, queries_ref, grad_ref, taps_ref, message_ref, *refs):
-    n_next = len(refs) - PARTS - 6
-    next_refs, (numer_ref, inverse_ref, *refs) = refs[:n_next], refs[n_next:]
-    out_refs, (state, sorted_ref, next_ref, sems) = refs[:PARTS], refs[PARTS:]
+def denominator_kernel(queries_ref, message_ref, inverse_ref, spread_ref):
     rows, width = queries_ref.shape
-    blocks = spans(width)
-    arrivals = []
-    for i, (start, stop, *_) in enumerate(blocks):
-        first, copies = 0, []
-        for j, source in enumerate(next_refs):
-            source = flat(source)
-            last = first + source.shape[0]
-            target = next_ref.at[first:last, start:stop]
-            copies.append(pltpu.make_async_copy(source.at[:, start:stop], target, sems.at[j, i]))
-            copies[-1].start()
-            first = last
-        arrivals.append(copies)
     tot_high, tot_low = read_totals(message_ref)
-    taps = taps_ref[...]
-    taps = [taps[0:1] + 1.0, taps[1:2], taps[2:3]]
-    state[...] = jnp.zeros_like(state)
     denominator = jnp.zeros((rows, 2 * LANES), F32)
-    for start, stop, *_ in blocks:
+    for start, stop, *_ in spans(width):
         row = lax.broadcasted_iota(jnp.int32, (2 * LANES, stop - start), 0)
         tot = jnp.where(row < LANES, tot_high[:, start:stop], tot_low[:, start:stop])
         weights = jnp.where(picks(start, stop, 2 * LANES), tot, 0.0).astype(BF16)
@@ -221,39 +203,55 @@
     inverse_ref[...] = inverse
     high = inverse.astype(BF16).astype(F32)
     middle = (inverse - high).astype(BF16).astype(F32)
-    spread = jnp.where(lane < COPY, high, jnp.where(lane < 2 * COPY, middle, inverse - high - middle)).astype(BF16)
-    frame_of_row = lax.broadcasted_iota(jnp.int32, (rows, 1), 0) % frames
+    low = inverse - high - middle
+    spread_ref[...] = jnp.where(lane < COPY, high, jnp.where(lane < 2 * COPY, middle, low)).astype(BF16)
+
+
+def query_kernel(frames, rank_ref, queries_ref, grad_ref, taps_ref, spread_ref, source_ref, *refs):
+    numer_ref, *refs = refs
+    out_refs, (state, sorted_ref, next_ref, sems) = refs[:PARTS], refs[PARTS:]
+    rows, width = queries_ref.shape
+    blocks = spans(width)
+    taps = taps_ref[...]
+    taps = [taps[0:1] + 1.0, taps[1:2], taps[2:3]]
+    state[...] = jnp.zeros_like(state)
+    group = 8 if 8 % frames == 0 and rows % 8 == 0 else rows
     for i, (start, stop, *_) in enumerate(blocks):
-        for copy in arrivals[i]:
-            copy.wait()
-        frame = jnp.broadcast_to(frame_of_row, (rows, stop - start))
-        now = grad_ref[:, start:stop].astype(F32)
-        later = next_ref[:, start:stop].astype(F32)
+        arrival = pltpu.make_async_copy(flat(source_ref).at[:, start:stop], next_ref.at[:, start:stop], sems.at[i])
+        arrival.start()
+        arrival.wait()
+        shape = (rows // group, group, stop - start)
+        frame = lax.broadcasted_iota(jnp.int32, shape, 1) % frames
+        now = grad_ref[:, start:stop].astype(F32).reshape(shape)
+        later = next_ref[:, start:stop].astype(F32).reshape(shape)
         upstream = now * taps[0][:, start:stop]
         for lag in (1, 2):
-            shifted = pltpu.roll(later, frames - lag, 0) if lag < frames else later
+            shifted = later
             if lag < frames:
-                shifted = jnp.where(frame + lag < frames, pltpu.roll(now, rows - lag, 0), shifted)
+                mixed = jnp.where(frame >= lag, now, later)
+                ahead, behind = pltpu.roll(mixed, group - lag, 1), pltpu.roll(mixed, frames - lag, 1)
+                shifted = jnp.where(frame + lag < frames, ahead, behind)
             upstream += shifted * taps[lag][:, start:stop]
-        upstream = upstream.astype(BF16).astype(F32)
+        upstream = upstream.reshape(rows, stop - start)
         pick = jnp.where(picks(start, stop), 1.0, 0.0).astype(BF16)
-        numer_ref[:, start:stop] = (upstream * dot(spread, pick, (1, 0))).astype(BF16)
+        numer_ref[:, start:stop] = (upstream * dot(spread_ref[...], pick, (1, 0))).astype(BF16)
     add_outer(state, jnp.maximum(queries_ref[...], 0), numer_ref)
     write_messages(rank_ref[0], state[...], jnp.zeros((1, width), F32), sorted_ref, out_refs)
 
 
-def query_grad_kernel(scale, rank_ref, queries_ref, numer_ref, inverse_ref, *refs):
-    message_refs, refs = refs[:PARTS], refs[PARTS:]
-    out_ref, total_ref, state, sorted_ref, wide, across, held, sems = refs
+def sort_messages(rank, message_refs, sorted_ref, state):
+    for d, ref in enumerate(message_refs):
+        sorted_ref[rank ^ d] = ref[...].astype(F32)
+    load_state(sorted_ref, state)
+
+
+def side_kernel(rank_ref, queries_ref, numer_ref, inverse_ref, *refs):
+    message_refs, (sides_ref, total_ref, state, sorted_ref, wide) = refs[:PARTS], refs[PARTS:]
     rows, width = queries_ref.shape
     blocks = spans(width)
-    tot_high, tot_low = read_totals(message_refs[0])
-    for d, ref in enumerate(message_refs):
-        sorted_ref[rank_ref[0] ^ d] = ref[...].astype(F32)
-    load_state(sorted_ref, state)
+    sort_messages(rank_ref[0], message_refs, sorted_ref, state)
     for i, block in enumerate(blocks):
         wide[i, : block[3] - block[2], : block[1] - block[0]] = columns_of(state, block)
-        across[i, : block[1] - block[0], : block[3] - block[2]] = rows_of(state, block)
     summed = jnp.zeros((rows, LANES), F32)
     for i, (start, stop, low, high, _) in enumerate(blocks):
         pick = jnp.where(picks(start, stop), 1.0, 0.0).astype(BF16)
@@ -265,19 +263,29 @@
     lane = lax.broadcasted_iota(jnp.int32, (rows, LANES), 1)
     sides = jnp.where((lane >= COPY) & (lane < 2 * COPY), low, high)
     pairs = jnp.where(lane < 2 * COPY, sides, 0.0).astype(BF16)
-    sides = sides.astype(BF16)
+    sides_ref[...] = sides.astype(BF16)
+    for start, stop, *_ in blocks:
+        terms = dot(pairs, jnp.maximum(queries_ref[:, start:stop], 0), (0, 0))
+        terms = jnp.sum(jnp.where(picks(start, stop), terms, 0.0), 0, keepdims=True)
+        total_ref[:, start:stop] = jnp.broadcast_to(terms, (8, stop - start))
+
+
+def query_grad_kernel(scale, rank_ref, queries_ref, numer_ref, sides_ref, *refs):
+    message_refs, (out_ref, state, sorted_ref, across, held, sems) = refs[:PARTS], refs[PARTS:]
+    blocks = spans(queries_ref.shape[1])
+    tot_high, tot_low = read_totals(message_refs[0])
+    sort_messages(rank_ref[0], message_refs, sorted_ref, state)
+    for i, block in enumerate(blocks):
+        across[i, : block[1] - block[0], : block[3] - block[2]] = rows_of(state, block)
     leaving = Leaving(held, out_ref, sems)
     for i, (start, stop, low, high, _) in enumerate(blocks):
-        queries = queries_ref[:, start:stop]
-        pick = picks(start, stop)
-        terms = dot(pairs, jnp.maximum(queries, 0), (0, 0))
-        terms = jnp.sum(jnp.where(pick, terms, 0.0), 0, keepdims=True)
-        total_ref[:, start:stop] = jnp.broadcast_to(terms, (8, stop - start))
         row = lax.broadcasted_iota(jnp.int32, (LANES, stop - start), 0)
         tot = jnp.where(row < 2 * COPY, tot_high[:, start:stop], tot_low[:, start:stop])
-        tot = jnp.where(pick, tot, 0.0).astype(BF16)
-        grad = dot(numer_ref[:, low:high], across[i, : stop - start, : high - low], (1, 1)) + dot(sides, tot, (1, 0))
-        leaving.put(start, stop, jnp.where(queries.astype(F32) > 0, grad * scale, 0.0).astype(BF16))
+        tot = jnp.where(picks(start, stop), tot, 0.0).astype(BF16)
+        grad = dot(numer_ref[:, low:high], across[i, : stop - start, : high - low], (1, 1))
+        grad += dot(sides_ref[...], tot, (1, 0))
+        grad = jnp.where(queries_ref[:, start:stop].astype(F32) > 0, grad * scale, 0.0).astype(BF16)
+        leaving.put(start, stop, grad, last_of(i, len(blocks), 3))
     leaving.finish()
 
 
@@ -296,12 +304,15 @@
         start, stop, low, high, _ = block
         across[i, : stop - start, : high - low] = rows_of(state, block)
         wide[i, : high - low, : stop - start] = columns_of(state, block)
+    for i, (start, stop, low, high, _) in enumerate(blocks):
         grad = dot(values_ref[:, low:high], across[i, : stop - start, : high - low], (1, 1)) + total[:, start:stop]
         alive = keys_ref[:, start:stop].astype(F32) > 0
-        key_leaving.put(start, stop, jnp.where(alive, grad * scale, 0.0).astype(BF16))
+        grad = jnp.where(alive, grad * scale, 0.0).astype(BF16)
+        key_leaving.put(start, stop, grad, last_of(i, len(blocks), 2))
+    for i, (start, stop, low, high, _) in enumerate(blocks):
         feat = jnp.maximum(keys_ref[:, low:high], 0)
         grad = dot(feat, wide[i, : high - low, : stop - start], (1, 0))
-        value_leaving.put(start, stop, (grad * scale).astype(BF16))
+        value_leaving.put(start, stop, (grad * scale).astype(BF16), last_of(i, len(blocks), 3))
     key_leaving.finish()
     value_leaving.finish()
 
@@ -361,8 +372,6 @@
     across = pltpu.VMEM((len(spans(width)), SPAN, window), BF16)
     wide = pltpu.VMEM((len(spans(width)), window, SPAN), BF16)
     size = 2 * frames * tokens * width
-    steps = 2 if tokens % 2 == 0 else 1
-    per_step = pl.BlockSpec((tokens // steps, frames, width), lambda i: (i, 0, 0))
 
     anywhere = pl.BlockSpec(memory_space=pl.ANY)
     merged = jax.ShapeDtypeStruct((frames * tokens, width), BF16)
@@ -380,46 +389,57 @@
             cost_estimate=cost(0, 2 * size * len(sources)),
         )(*sources)
 
-    def halo(source):
-        return lax.ppermute(source, "frame", [(i + 1, i) for i in range(devices - 1)])
-
-    early = tokens * 2 // 5 // 8 * 8
-    following = [halo(grad_out[:early])]
     key = pl.pallas_call(
         key_kernel,
-        grid=(steps,),
-        in_specs=[smem, per_step, per_step],
-        out_specs=[pl.BlockSpec(message.shape, lambda i: (0, 0))] * PARTS,
+        in_specs=[smem, anywhere, anywhere],
+        out_specs=[vmem] * PARTS,
         out_shape=[message] * PARTS,
-        scratch_shapes=[state, pltpu.VMEM((8, width), F32), ordered],
+        scratch_shapes=[state, pltpu.VMEM((8, width), F32), ordered, held, held, pltpu.SemaphoreType.DMA((4,))],
+        compiler_params=LARGE,
+        cost_estimate=cost(size * 512, 2 * size),
+    )
+    state_messages = key(rank, saved_keys, saved_values)
+    following = lax.ppermute(grad_out, "frame", [(i + 1, i) for i in range(devices - 1)])
+    query_rows, grad_rows = relay(saved_queries, grad_out)
+    part = over_groups(added(spread_out(state_messages)))
+    per_head = (frames * tokens, LANES)
+    denominators = pl.pallas_call(
+        denominator_kernel,
+        out_shape=[jax.ShapeDtypeStruct(per_head, F32), jax.ShapeDtypeStruct(per_head, BF16)],
+        compiler_params=PARAMS,
+        cost_estimate=cost(size * 128, size),
+    )
+    inverse, spread = denominators(query_rows, part)
+    query = pl.pallas_call(
+        functools.partial(query_kernel, frames),
+        in_specs=[smem] + [vmem] * 4 + [anywhere],
+        out_shape=[merged] + [message] * PARTS,
+        scratch_shapes=[state, ordered, held, sems],
+        compiler_params=PARAMS,
+        cost_estimate=cost(size * 1024, 4 * size),
+    )
+    numer, *grad_messages = query(rank, query_rows, grad_rows, conv_taps, spread, following)
+    states = spread_out([part] * PARTS)
+    grad_parts = spread_out(grad_messages)
+    side = pl.pallas_call(
+        side_kernel,
+        in_specs=[smem] + [vmem] * (3 + PARTS),
+        out_shape=[jax.ShapeDtypeStruct(per_head, BF16), jax.ShapeDtypeStruct((8, width), F32)],
+        scratch_shapes=[state, ordered, wide],
         compiler_params=PARAMS,
         cost_estimate=cost(size * 512, 2 * size),
     )
-    state_messages = key(rank, saved_keys, saved_values)
-    following.append(halo(grad_out[early:]))
-    query_rows, grad_rows = relay(saved_queries, grad_out)
-    part = over_groups(added(spread_out(state_messages)))
-    query = pl.pallas_call(
-        functools.partial(query_kernel, frames),
-        in_specs=[smem] + [vmem] * 4 + [anywhere] * len(following),
-        out_shape=[merged, jax.ShapeDtypeStruct((frames * tokens, LANES), F32)] + [message] * PARTS,
-        scratch_shapes=[state, ordered, held, pltpu.SemaphoreType.DMA((len(following), len(spans(width))))],
-        compiler_params=PARAMS,
-        cost_estimate=cost(size * 1024, 4 * size),
-    )
-    numer, inverse, *grad_messages = query(rank, query_rows, grad_rows, conv_taps, part, *following)
-    states = spread_out([part] * PARTS)
-    grad_parts = spread_out(grad_messages)
+    sides, total = side(rank, query_rows, numer, inverse, *states)
     query_grad = pl.pallas_call(
         functools.partial(query_grad_kernel, scale),
         in_specs=[smem] + [vmem] * (3 + PARTS),
-        out_specs=[anywhere, vmem],
-        out_shape=[array, jax.ShapeDtypeStruct((8, width), F32)],
-        scratch_shapes=[state, ordered, wide, across, held, sems],
+        out_specs=anywhere,
+        out_shape=array,
+        scratch_shapes=[state, ordered, across, held, sems],
         compiler_params=PARAMS,
-        cost_estimate=cost(size * 1024, 3 * size),
-    )
-    grad_queries, total = query_grad(rank, query_rows, numer, inverse, *states)
+        cost_estimate=cost(size * 512, 3 * size),
+    )
+    grad_queries = query_grad(rank, query_rows, numer, sides, *states)
     key_rows, value_rows = relay(saved_keys, saved_values)
     part = over_groups(added(grad_parts, total))
     groups = [list(range(i, i + PARTS)) for i in range(0, devices, PARTS)]

time: 112 us -> 112 us (level)
  local copies, waits for them, and re-layouts: 7.88 us -> 0.91 us
  waiting for transfers between devices: 25.7 us -> 32.1 us
  Pallas kernels: 31.4 us -> 35.1 us
  starting transfers between devices: 35.8 us -> 32.7 us
    ppermute x27, waiting for transfers between devices: 25.7 us -> 32.1 us  [exchange(): return lax.ppermute(block, axis, [(i, i ^ distance) for i in devices])]
    pallas_call x2 -> x4, Pallas kernels: 14.3 us -> 19.9 us  [the longest x1 12.5 us: shards(): query(rank, query_rows, grad_rows, conv_taps, spread, following)]
    slice x2 -> x0, local copies, waits for them, and re-layouts: 4.73 us -> none  [the longest x1 3.29 us: shards(): following.append(halo(grad_out[early:]))]
    pallas_call x1, Pallas kernels: 8.58 us -> 4.9 us  [shards(): pl.pallas_call(functools.partial(key_grad_kernel, scale), in_specs=[vmem]...]
    unnamed x14 -> x12, local copies, waits for them, and re-layouts: 3.15 us -> 0.91 us
    pallas_call x1, Pallas kernels: 2.32 us -> 4.25 us  [shards(): state_messages = key(rank, saved_keys, saved_values)]
    ppermute x27, starting transfers between devices: 33.2 us -> 31.4 us  [exchange(): return lax.ppermute(block, axis, [(i, i ^ distance) for i in devices])]
    ppermute x2 -> x1, starting transfers between devices: 2.56 us -> 1.29 us  [shards(): lax.ppermute(grad_out, 'frame', [(i + 1, i) for i in range(devices - 1)])]
  transfers between devices with their start and end apart: 29 -> 28, of which waited for: 7 -> 8; matrix products, arithmetic and copies ran while one was open for 1% -> 0% of each run, Pallas kernels for 20% -> 27%
where the time goes in v3:
time: 112 us
  Pallas kernels  35.1 us (31%)
  starting transfers between devices  32.7 us (29%)
  waiting for transfers between devices  32.1 us (29%)
  blocking collectives  10.1 us (9%)
    ppermute x27, waiting for transfers between devices, exchange(): return lax.ppermute(block, axis, [(i, i ^ distance) for i in devices])  32.1 us
    ppermute x27, starting transfers between devices, exchange(): return lax.ppermute(block, axis, [(i, i ^ distance) for i in devices])  31.4 us
    pallas_call x1, Pallas kernels, shards(): query(rank, query_rows, grad_rows, conv_taps, spread, following)  12.5 us
    all_gather x1, blocking collectives, shards(): lax.all_gather(part, 'frame', axis_index_groups=groups if len(groups) > 1...  10.1 us
    pallas_call x2, Pallas kernels, relay(): pl.pallas_call(relay_kernel, in_specs=[anywhere] * len(sources), out_spec...  5.67 us
    pallas_call x1, Pallas kernels, shards(): pl.pallas_call(functools.partial(key_grad_kernel, scale), in_specs=[vmem]...  4.9 us
    pallas_call x1, Pallas kernels, shards(): state_messages = key(rank, saved_keys, saved_values)  4.25 us
    pallas_call x1, Pallas kernels, shards(): grad_queries = query_grad(rank, query_rows, numer, sides, *states)  3.64 us
  transfers between devices with their start and end apart: 28, of which 8 were waited for; matrix products, arithmetic and copies ran while one was open for 0% of the time, Pallas kernels for 27%

profile of v3, /device:TPU:0, one launch (start us, length us, event | category | flops | bytes accessed | tf_op | source)
XLA Modules:
  0.0 111.8 jit_solution(7844458202616352108)
XLA Ops:
  0.6 1.3 %collective-permute-start.10 = (bf16[220,2,2240]{2,1,0:T(2,128)(2,1)}, bf16[220,2,2240]{2,1,0:T(2,128)(2,1)}, u32[]{:S(2)}, u32[]{:S(2)}) collective-permute-start(bf16[220,2,2240]{2,1,0:T(2,128)(2,1)} %bitcast.14), channel_id=1, source_target_pairs={{4,0},{8,4},{12,8},{16,12},{20,16},{24,20},{28,24},{5,1},{9,5},{13... | collective-permute-start | bytes 5913608 | tf_op jit(solution)/shard_map/ppermute | solution.py:402
  2.0 4.2 %shard_map.77 = (bf16[16,2240]{1,0:T(8,128)(2,1)}, bf16[16,2240]{1,0:T(8,128)(2,1)}, bf16[16,2240]{1,0:T(8,128)(2,1)}, bf16[16,2240]{1,0:T(8,128)(2,1)}, bf16[16...) custom-call(s32[1]{0:T(128)} %bitcast.rank_ref, ...), custom_call_target="tpu_custom_call" | custom-call | flops 1009254400 | bytes 3942400 | tf_op jit(solution)/shard_map/pallas_call | solution.py:401
  6.2 1.2 %collective-permute-start = (bf16[16,2240]{1,0:T(8,128)(2,1)}, bf16[16,2240]{1,0:T(8,128)(2,1)S(1)}, u32[]{:S(2)}, u32[]{:S(2)}) collective-permute-start(bf16[16,2240]{1,0:T(8,128)(2,1)} %get-tuple-element.33), channel_id=1, source_target_pairs={{0,4},{4,0},{8,12},{12,8},{16,20},{20,16},{24,28},{28,24},{1,5},{5... | collective-permute-start | bytes 215048 | tf_op jit(solution)/shard_map/ppermute | solution.py:326
  7.4 3.0 %collective-permute-start.1 = (bf16[16,2240]{1,0:T(8,128)(2,1)}, bf16[16,2240]{1,0:T(8,128)(2,1)S(1)}, u32[]{:S(2)}, u32[]{:S(2)}) collective-permute-start(bf16[16,2240]{1,0:T(8,128)(2,1)} %get-tuple-element.34), channel_id=1, source_target_pairs={{0,8},{4,12},{8,0},{12,4},{16,24},{20,28},{24,16},{28,20},{1,9},{5... | collective-permute-start | bytes 215048 | tf_op jit(solution)/shard_map/ppermute | solution.py:326
  10.4 2.8 %collective-permute-start.3 = (bf16[16,2240]{1,0:T(8,128)(2,1)}, bf16[16,2240]{1,0:T(8,128)(2,1)S(1)}, u32[]{:S(2)}, u32[]{:S(2)}) collective-permute-start(bf16[16,2240]{1,0:T(8,128)(2,1)} %get-tuple-element.36), channel_id=1, source_target_pairs={{0,16},{4,20},{8,24},{12,28},{16,0},{20,4},{24,8},{28,12},{1,17},{... | collective-permute-start | bytes 215048 | tf_op jit(solution)/shard_map/ppermute | solution.py:326
  13.2 18.9 %collective-permute-done.1.refs_2_ = bf16[16,2240]{1,0:T(8,128)(2,1)S(1)} collective-permute-done((bf16[16,2240]{1,0:T(8,128)(2,1)}, bf16[16,2240]{1,0:T(8,128)(2,1)S(1)}, u32[]{:S(2)}, u32[]{:S(2)}) %collective-permute-start.1) | collective-permute-done | bytes 71712 | tf_op jit(solution)/shard_map/ppermute | solution.py:326
  32.1 2.4 %collective-permute-start.5 = (bf16[16,2240]{1,0:T(8,128)(2,1)}, bf16[16,2240]{1,0:T(8,128)(2,1)S(1)}, u32[]{:S(2)}, u32[]{:S(2)}) collective-permute-start(bf16[16,2240]{1,0:T(8,128)(2,1)} %get-tuple-element.38), channel_id=1, source_target_pairs={{0,24},{4,28},{8,16},{12,20},{16,8},{20,12},{24,0},{28,4},{1,25},{... | collective-permute-start | bytes 215048 | tf_op jit(solution)/shard_map/ppermute | solution.py:326
  34.8 2.8 %collective-permute-done.5.refs_6_ = bf16[16,2240]{1,0:T(8,128)(2,1)S(1)} collective-permute-done((bf16[16,2240]{1,0:T(8,128)(2,1)}, bf16[16,2240]{1,0:T(8,128)(2,1)S(1)}, u32[]{:S(2)}, u32[]{:S(2)}) %collective-permute-start.5) | collective-permute-done | bytes 71712 | tf_op jit(solution)/shard_map/ppermute | solution.py:326
  37.6 1.8 %collective-permute-done.6.refs_7_ = bf16[16,2240]{1,0:T(8,128)(2,1)S(1)} collective-permute-done((bf16[16,2240]{1,0:T(8,128)(2,1)}, bf16[16,2240]{1,0:T(8,128)(2,1)S(1)}, u32[]{:S(2)}, u32[]{:S(2)}) %collective-permute-start.6) | collective-permute-done | bytes 71712 | tf_op jit(solution)/shard_map/ppermute | solution.py:326
  39.4 0.9 copy-done.4
  40.4 3.7 %collective-permute-start.9 = (bf16[16,2240]{1,0:T(8,128)(2,1)S(1)}, bf16[16,2240]{1,0:T(8,128)(2,1)S(1)}, u32[]{:S(2)}, u32[]{:S(2)}) collective-permute-start(bf16[16,2240]{1,0:T(8,128)(2,1)S(1)} %shard_map.78.refs_0_), channel_id=1, source_target_pairs={{0,3},{1,2},{2,1},{3,0},{4,7},{5,6},{6,5},{7,4},{8,11},{9,10},{10,... | collective-permute-start | bytes 215048 | tf_op jit(solution)/shard_map/ppermute | solution.py:326
  44.9 1.9 %collective-permute-done.9.refs_3_ = bf16[16,2240]{1,0:T(8,128)(2,1)S(1)} collective-permute-done((bf16[16,2240]{1,0:T(8,128)(2,1)S(1)}, bf16[16,2240]{1,0:T(8,128)(2,1)S(1)}, u32[]{:S(2)}, u32[]{:S(2)}) %collective-permute-start.9) | collective-permute-done | bytes 71712 | tf_op jit(solution)/shard_map/ppermute | solution.py:326
  46.8 3.0 %collective-permute-done.8.refs_2_ = bf16[16,2240]{1,0:T(8,128)(2,1)S(1)} collective-permute-done((bf16[16,2240]{1,0:T(8,128)(2,1)S(1)}, bf16[16,2240]{1,0:T(8,128)(2,1)S(1)}, u32[]{:S(2)}, u32[]{:S(2)}) %collective-permute-start.8) | collective-permute-done | bytes 71712 | tf_op jit(solution)/shard_map/ppermute | solution.py:326
  49.9 2.0 %collective-permute-start.17 = (bf16[16,2240]{1,0:T(8,128)(2,1)S(1)}, bf16[16,2240]{1,0:T(8,128)(2,1)S(1)}, u32[]{:S(2)}, u32[]{:S(2)}) collective-permute-start(bf16[16,2240]{1,0:T(8,128)(2,1)S(1)} %shard_map.79.message_ref.refs_0_), channel_id=1, source_target_pairs={{0,28},{4,24},{8,20},{12,16},{16,12},{20,8},{24,4},{28,0},{1,29},{... | collective-permute-start | bytes 215048 | tf_op jit(solution)/shard_map/ppermute | solution.py:326
  51.8 2.8 %shard_map.76 = (bf16[440,2240]{1,0:T(8,128)(2,1)S(1)}, bf16[440,2240]{1,0:T(8,128)(2,1)S(1)}) custom-call(bf16[220,2,2240]{2,1,0:T(2,128)(2,1)S(1)} %bitcast.13, bf16[220,2,2240]{2,1,0:T(2,128)(2,1)S(1)} %bitcast.15), custom_call_target="tpu_custom_call" | custom-call | bytes 7884800 | tf_op jit(solution)/shard_map/pallas_call | solution.py:382
  54.7 0.9 collective-permute-start.16
  56.4 0.9 collective-permute-start.14
  58.1 0.9 collective-permute-start.13
  58.9 1.1 collective-permute-start.12
  60.0 12.5 %shard_map.81 = (bf16[440,2240]{1,0:T(8,128)(2,1)S(1)}, bf16[16,2240]{1,0:T(8,128)(2,1)S(1)}, bf16[16,2240]{1,0:T(8,128)(2,1)S(1)}, bf16[16,2240]{1,0:T(8,128)(2...) custom-call(s32[1]{0:T(128)} %bitcast.rank_ref, ...), custom_call_target="tpu_custom_call" | custom-call | flops 2018508800 | bytes 7884800 | tf_op jit(solution)/shard_map/pallas_call | solution.py:421
  73.1 1.0 collective-permute-start.19
  74.1 2.8 %shard_map.84 = (bf16[440,2240]{1,0:T(8,128)(2,1)S(1)}, bf16[440,2240]{1,0:T(8,128)(2,1)S(1)}) custom-call(bf16[220,2,2240]{2,1,0:T(2,128)(2,1)S(1)} %bitcast.10, bf16[220,2,2240]{2,1,0:T(2,128)(2,1)S(1)} %bitcast.12), custom_call_target="tpu_custom_call" | custom-call | bytes 7884800 | tf_op jit(solution)/shard_map/pallas_call | solution.py:382
  77.5 1.3 %collective-permute-start.21 = (bf16[16,2240]{1,0:T(8,128)(2,1)S(1)}, bf16[16,2240]{1,0:T(8,128)(2,1)S(1)}, u32[]{:S(2)}, u32[]{:S(2)}) collective-permute-start(bf16[16,2240]{1,0:T(8,128)(2,1)S(1)} %get-tuple-element.50), channel_id=1, source_target_pairs={{0,16},{4,20},{8,24},{12,28},{16,0},{20,4},{24,8},{28,12},{1,17},{... | collective-permute-start | bytes 215048 | tf_op jit(solution)/shard_map/ppermute | solution.py:326
  79.5 2.1 %collective-permute-start.23 = (bf16[16,2240]{1,0:T(8,128)(2,1)S(1)}, bf16[16,2240]{1,0:T(8,128)(2,1)S(1)}, u32[]{:S(2)}, u32[]{:S(2)}) collective-permute-start(bf16[16,2240]{1,0:T(8,128)(2,1)S(1)} %get-tuple-element.52), channel_id=1, source_target_pairs={{0,24},{4,28},{8,16},{12,20},{16,8},{20,12},{24,0},{28,4},{1,25},{... | collective-permute-start | bytes 215048 | tf_op jit(solution)/shard_map/ppermute | solution.py:326
  81.9 3.0 %shard_map.82 = (bf16[440,128]{1,0:T(8,128)(2,1)S(1)}, f32[8,2240]{1,0:T(8,128)S(1)}) custom-call(s32[1]{0:T(128)} %bitcast.rank_ref, bf16[440,2240]{1,0:T(8,128)(2,1)S(1)} %get-tuple-element.30.queries_ref, bf16[440,2240]{1,0:T(8,128)(2,1)S(1)} %get-tuple-element.41.numer_ref, f32[440,128]{1,0:T(8,128)S(1)} %get-tuple-element.42.inverse_ref, ...), custom_call_target="tpu_custom_call" | custom-call | flops 1009254400 | bytes 3942400 | tf_op jit(solution)/shard_map/pallas_call | solution.py:432
  84.8 1.1 collective-permute-done.22.refs_5_
  86.9 2.5 %collective-permute-start.27 = (bf16[16,2240]{1,0:T(8,128)(2,1)S(1)}, bf16[16,2240]{1,0:T(8,128)(2,1)S(1)}, u32[]{:S(2)}, u32[]{:S(2)}) collective-permute-start(bf16[16,2240]{1,0:T(8,128)(2,1)S(1)} %shard_map.85.refs_0_), channel_id=1, source_target_pairs={{0,3},{1,2},{2,1},{3,0},{4,7},{5,6},{6,5},{7,4},{8,11},{9,10},{10,... | collective-permute-start | bytes 215048 | tf_op jit(solution)/shard_map/ppermute | solution.py:326
  89.5 1.9 %collective-permute-start.25 = (bf16[16,2240]{1,0:T(8,128)(2,1)S(1)}, bf16[16,2240]{1,0:T(8,128)(2,1)S(1)}, u32[]{:S(2)}, u32[]{:S(2)}) collective-permute-start(bf16[16,2240]{1,0:T(8,128)(2,1)S(1)} %shard_map.85.refs_0_), channel_id=1, source_target_pairs={{0,1},{1,0},{2,3},{3,2},{4,5},{5,4},{6,7},{7,6},{8,9},{9,8},{10,11... | collective-permute-start | bytes 215048 | tf_op jit(solution)/shard_map/ppermute | solution.py:326
  91.4 3.6 %shard_map.83 = bf16[220,2,2240]{2,1,0:T(2,128)(2,1)} custom-call(s32[1]{0:T(128)} %bitcast.rank_ref, bf16[440,2240]{1,0:T(8,128)(2,1)S(1)} %get-tuple-element.30.queries_ref, bf16[440,2240]{1,0:T(8,128)(2,1)S(1)} %get-tuple-element.41.numer_ref, bf16[440,128]{1,0:T(8,128)(2,1)S(1)} %get-tuple-element.43.sides_ref, ...), custom_call_target="tpu_custom_call" | custom-call | flops 1009254400 | bytes 5913600 | tf_op jit(solution)/shard_map/pallas_call | solution.py:442
  95.0 1.5 %collective-permute-done.26.refs_2_ = bf16[16,2240]{1,0:T(8,128)(2,1)S(1)} collective-permute-done((bf16[16,2240]{1,0:T(8,128)(2,1)S(1)}, bf16[16,2240]{1,0:T(8,128)(2,1)S(1)}, u32[]{:S(2)}, u32[]{:S(2)}) %collective-permute-start.26) | collective-permute-done | bytes 71712 | tf_op jit(solution)/shard_map/ppermute | solution.py:326
  96.6 10.1 %all-gather = bf16[128,2240]{1,0:T(8,128)(2,1)S(1)} all-gather(bf16[16,2240]{1,0:T(8,128)(2,1)S(1)} %shard_map.86), channel_id=2, replica_groups=mesh['frame'=8,'space'=4] {'frame'}, dimensions={0}, use_global_device_ids=true | all-gather | bytes 645120 | tf_op jit(solution)/shard_map/all_gather | solution.py:446
  106.7 4.9 %shard_map.87 = (bf16[220,2,2240]{2,1,0:T(2,128)(2,1)}, bf16[220,2,2240]{2,1,0:T(2,128)(2,1)}) custom-call(bf16[440,2240]{1,0:T(8,128)(2,1)S(1)} %get-tuple-element.44.keys_ref, bf16[440,2240]{1,0:T(8,128)(2,1)S(1)} %get-tuple-element.45.values_ref, bf16[8,16,2240]{2,1,0:T(8,128)(2,1)S(1)} %bitcast.16), custom_call_target="tpu_custom_call" | custom-call | flops 2018508800 | bytes 7884800 | tf_op jit(solution)/shard_map/pallas_call | solution.py:447
  (49 shorter events, 5.9 us)
Async XLA Ops:
  0.6 58.3 %collective-permute-start.10 = (bf16[220,2,2240]{2,1,0:T(2,128)(2,1)}, bf16[220,2,2240]{2,1,0:T(2,128)(2,1)}, u32[]{:S(2)}, u32[]{:S(2)}) collective-permute-start(bf16[220,2,2240]{2,1,0:T(2,128)(2,1)} %bitcast.14), channel_id=1, source_target_pairs={{4,0},{8,4},{12,8},{16,12},{20,16},{24,20},{28,24},{5,1},{9,5},{13... | collective-permute-start | bytes 5913608 | tf_op jit(solution)/shard_map/ppermute | solution.py:402
  1.9 49.9 %copy-start.2 = (bf16[2,220,2240]{2,0,1:T(2,128)(2,1)S(1)}, bf16[2,220,2240]{2,0,1:T(2,128)(2,1)}, u32[]{:S(2)}) copy-start(bf16[2,220,2240]{2,0,1:T(2,128)(2,1)} %param.7) | copy-start | bytes 5913604
  2.0 49.9 %copy-start.3 = (bf16[2,220,2240]{2,0,1:T(2,128)(2,1)S(1)}, bf16[2,220,2240]{2,0,1:T(2,128)(2,1)}, u32[]{:S(2)}) copy-start(bf16[2,220,2240]{2,0,1:T(2,128)(2,1)} %param.5) | copy-start | bytes 5913604
  6.2 7.0 %collective-permute-start = (bf16[16,2240]{1,0:T(8,128)(2,1)}, bf16[16,2240]{1,0:T(8,128)(2,1)S(1)}, u32[]{:S(2)}, u32[]{:S(2)}) collective-permute-start(bf16[16,2240]{1,0:T(8,128)(2,1)} %get-tuple-element.33), channel_id=1, source_target_pairs={{0,4},{4,0},{8,12},{12,8},{16,20},{20,16},{24,28},{28,24},{1,5},{5... | collective-permute-start | bytes 215048 | tf_op jit(solution)/shard_map/ppermute | solution.py:326
  7.4 24.7 %collective-permute-start.1 = (bf16[16,2240]{1,0:T(8,128)(2,1)}, bf16[16,2240]{1,0:T(8,128)(2,1)S(1)}, u32[]{:S(2)}, u32[]{:S(2)}) collective-permute-start(bf16[16,2240]{1,0:T(8,128)(2,1)} %get-tuple-element.34), channel_id=1, source_target_pairs={{0,8},{4,12},{8,0},{12,4},{16,24},{20,28},{24,16},{28,20},{1,9},{5... | collective-permute-start | bytes 215048 | tf_op jit(solution)/shard_map/ppermute | solution.py:326
  10.4 24.2 %collective-permute-start.2 = (bf16[16,2240]{1,0:T(8,128)(2,1)}, bf16[16,2240]{1,0:T(8,128)(2,1)S(1)}, u32[]{:S(2)}, u32[]{:S(2)}) collective-permute-start(bf16[16,2240]{1,0:T(8,128)(2,1)} %get-tuple-element.35), channel_id=1, source_target_pairs={{0,12},{4,8},{8,4},{12,0},{16,28},{20,24},{24,20},{28,16},{1,13},{... | collective-permute-start | bytes 215048 | tf_op jit(solution)/shard_map/ppermute | solution.py:326
  10.4 24.4 %collective-permute-start.3 = (bf16[16,2240]{1,0:T(8,128)(2,1)}, bf16[16,2240]{1,0:T(8,128)(2,1)S(1)}, u32[]{:S(2)}, u32[]{:S(2)}) collective-permute-start(bf16[16,2240]{1,0:T(8,128)(2,1)} %get-tuple-element.36), channel_id=1, source_target_pairs={{0,16},{4,20},{8,24},{12,28},{16,0},{20,4},{24,8},{28,12},{1,17},{... | collective-permute-start | bytes 215048 | tf_op jit(solution)/shard_map/ppermute | solution.py:326
  13.2 21.6 %collective-permute-start.4 = (bf16[16,2240]{1,0:T(8,128)(2,1)}, bf16[16,2240]{1,0:T(8,128)(2,1)S(1)}, u32[]{:S(2)}, u32[]{:S(2)}) collective-permute-start(bf16[16,2240]{1,0:T(8,128)(2,1)} %get-tuple-element.37), channel_id=1, source_target_pairs={{0,20},{4,16},{8,28},{12,24},{16,4},{20,0},{24,12},{28,8},{1,21},{... | collective-permute-start | bytes 215048 | tf_op jit(solution)/shard_map/ppermute | solution.py:326
  32.1 5.5 %collective-permute-start.5 = (bf16[16,2240]{1,0:T(8,128)(2,1)}, bf16[16,2240]{1,0:T(8,128)(2,1)S(1)}, u32[]{:S(2)}, u32[]{:S(2)}) collective-permute-start(bf16[16,2240]{1,0:T(8,128)(2,1)} %get-tuple-element.38), channel_id=1, source_target_pairs={{0,24},{4,28},{8,16},{12,20},{16,8},{20,12},{24,0},{28,4},{1,25},{... | collective-permute-start | bytes 215048 | tf_op jit(solution)/shard_map/ppermute | solution.py:326
  34.5 4.9 %collective-permute-start.6 = (bf16[16,2240]{1,0:T(8,128)(2,1)}, bf16[16,2240]{1,0:T(8,128)(2,1)S(1)}, u32[]{:S(2)}, u32[]{:S(2)}) collective-permute-start(bf16[16,2240]{1,0:T(8,128)(2,1)} %get-tuple-element.39), channel_id=1, source_target_pairs={{0,28},{4,24},{8,20},{12,16},{16,12},{20,8},{24,4},{28,0},{1,29},{... | collective-permute-start | bytes 215048 | tf_op jit(solution)/shard_map/ppermute | solution.py:326
  40.4 6.3 %collective-permute-start.9 = (bf16[16,2240]{1,0:T(8,128)(2,1)S(1)}, bf16[16,2240]{1,0:T(8,128)(2,1)S(1)}, u32[]{:S(2)}, u32[]{:S(2)}) collective-permute-start(bf16[16,2240]{1,0:T(8,128)(2,1)S(1)} %shard_map.78.refs_0_), channel_id=1, source_target_pairs={{0,3},{1,2},{2,1},{3,0},{4,7},{5,6},{6,5},{7,4},{8,11},{9,10},{10,... | collective-permute-start | bytes 215048 | tf_op jit(solution)/shard_map/ppermute | solution.py:326
  44.1 5.7 %collective-permute-start.8 = (bf16[16,2240]{1,0:T(8,128)(2,1)S(1)}, bf16[16,2240]{1,0:T(8,128)(2,1)S(1)}, u32[]{:S(2)}, u32[]{:S(2)}) collective-permute-start(bf16[16,2240]{1,0:T(8,128)(2,1)S(1)} %shard_map.78.refs_0_), channel_id=1, source_target_pairs={{0,2},{1,3},{2,0},{3,1},{4,6},{5,7},{6,4},{7,5},{8,10},{9,11},{10,... | collective-permute-start | bytes 215048 | tf_op jit(solution)/shard_map/ppermute | solution.py:326
  44.1 5.7 %collective-permute-start.7 = (bf16[16,2240]{1,0:T(8,128)(2,1)S(1)}, bf16[16,2240]{1,0:T(8,128)(2,1)S(1)}, u32[]{:S(2)}, u32[]{:S(2)}) collective-permute-start(bf16[16,2240]{1,0:T(8,128)(2,1)S(1)} %shard_map.78.refs_0_), channel_id=1, source_target_pairs={{0,1},{1,0},{2,3},{3,2},{4,5},{5,4},{6,7},{7,6},{8,9},{9,8},{10,11... | collective-permute-start | bytes 215048 | tf_op jit(solution)/shard_map/ppermute | solution.py:326
  49.9 8.2 %collective-permute-start.17 = (bf16[16,2240]{1,0:T(8,128)(2,1)S(1)}, bf16[16,2240]{1,0:T(8,128)(2,1)S(1)}, u32[]{:S(2)}, u32[]{:S(2)}) collective-permute-start(bf16[16,2240]{1,0:T(8,128)(2,1)S(1)} %shard_map.79.message_ref.refs_0_), channel_id=1, source_target_pairs={{0,28},{4,24},{8,20},{12,16},{16,12},{20,8},{24,4},{28,0},{1,29},{... | collective-permute-start | bytes 215048 | tf_op jit(solution)/shard_map/ppermute | solution.py:326
  54.7 17.8 %collective-permute-start.16 = (bf16[16,2240]{1,0:T(8,128)(2,1)S(1)}, bf16[16,2240]{1,0:T(8,128)(2,1)S(1)}, u32[]{:S(2)}, u32[]{:S(2)}) collective-permute-start(bf16[16,2240]{1,0:T(8,128)(2,1)S(1)} %shard_map.79.message_ref.refs_0_), channel_id=1, source_target_pairs={{0,24},{4,28},{8,16},{12,20},{16,8},{20,12},{24,0},{28,4},{1,25},{... | collective-permute-start | bytes 215048 | tf_op jit(solution)/shard_map/ppermute | solution.py:326
  55.6 17.0 %collective-permute-start.15 = (bf16[16,2240]{1,0:T(8,128)(2,1)S(1)}, bf16[16,2240]{1,0:T(8,128)(2,1)S(1)}, u32[]{:S(2)}, u32[]{:S(2)}) collective-permute-start(bf16[16,2240]{1,0:T(8,128)(2,1)S(1)} %shard_map.79.message_ref.refs_0_), channel_id=1, source_target_pairs={{0,20},{4,16},{8,28},{12,24},{16,4},{20,0},{24,12},{28,8},{1,21},{... | collective-permute-start | bytes 215048 | tf_op jit(solution)/shard_map/ppermute | solution.py:326
  56.4 16.7 %collective-permute-start.14 = (bf16[16,2240]{1,0:T(8,128)(2,1)S(1)}, bf16[16,2240]{1,0:T(8,128)(2,1)S(1)}, u32[]{:S(2)}, u32[]{:S(2)}) collective-permute-start(bf16[16,2240]{1,0:T(8,128)(2,1)S(1)} %shard_map.79.message_ref.refs_0_), channel_id=1, source_target_pairs={{0,16},{4,20},{8,24},{12,28},{16,0},{20,4},{24,8},{28,12},{1,17},{... | collective-permute-start | bytes 215048 | tf_op jit(solution)/shard_map/ppermute | solution.py:326
  58.1 18.9 %collective-permute-start.13 = (bf16[16,2240]{1,0:T(8,128)(2,1)S(1)}, bf16[16,2240]{1,0:T(8,128)(2,1)S(1)}, u32[]{:S(2)}, u32[]{:S(2)}) collective-permute-start(bf16[16,2240]{1,0:T(8,128)(2,1)S(1)} %shard_map.79.message_ref.refs_0_), channel_id=1, source_target_pairs={{0,12},{4,8},{8,4},{12,0},{16,28},{20,24},{24,20},{28,16},{1,13},{... | collective-permute-start | bytes 215048 | tf_op jit(solution)/shard_map/ppermute | solution.py:326
  58.9 18.5 %collective-permute-start.12 = (bf16[16,2240]{1,0:T(8,128)(2,1)S(1)}, bf16[16,2240]{1,0:T(8,128)(2,1)S(1)}, u32[]{:S(2)}, u32[]{:S(2)}) collective-permute-start(bf16[16,2240]{1,0:T(8,128)(2,1)S(1)} %shard_map.79.message_ref.refs_0_), channel_id=1, source_target_pairs={{0,8},{4,12},{8,0},{12,4},{16,24},{20,28},{24,16},{28,20},{1,9},{5... | collective-permute-start | bytes 215048 | tf_op jit(solution)/shard_map/ppermute | solution.py:326
  60.0 14.1 %copy-start = (bf16[2,220,2240]{2,0,1:T(2,128)(2,1)S(1)}, bf16[2,220,2240]{2,0,1:T(2,128)(2,1)}, u32[]{:S(2)}) copy-start(bf16[2,220,2240]{2,0,1:T(2,128)(2,1)} %param.8) | copy-start | bytes 5913604
  60.0 14.1 %copy-start.1 = (bf16[2,220,2240]{2,0,1:T(2,128)(2,1)S(1)}, bf16[2,220,2240]{2,0,1:T(2,128)(2,1)}, u32[]{:S(2)}) copy-start(bf16[2,220,2240]{2,0,1:T(2,128)(2,1)} %param.9) | copy-start | bytes 5913604
  72.5 6.3 %collective-permute-start.11 = (bf16[16,2240]{1,0:T(8,128)(2,1)S(1)}, bf16[16,2240]{1,0:T(8,128)(2,1)S(1)}, u32[]{:S(2)}, u32[]{:S(2)}) collective-permute-start(bf16[16,2240]{1,0:T(8,128)(2,1)S(1)} %shard_map.79.message_ref.refs_0_), channel_id=1, source_target_pairs={{0,4},{4,0},{8,12},{12,8},{16,20},{20,16},{24,28},{28,24},{1,5},{5... | collective-permute-start | bytes 215048 | tf_op jit(solution)/shard_map/ppermute | solution.py:326
  72.6 6.9 %collective-permute-start.18 = (bf16[16,2240]{1,0:T(8,128)(2,1)S(1)}, bf16[16,2240]{1,0:T(8,128)(2,1)S(1)}, u32[]{:S(2)}, u32[]{:S(2)}) collective-permute-start(bf16[16,2240]{1,0:T(8,128)(2,1)S(1)} %get-tuple-element.47), channel_id=1, source_target_pairs={{0,4},{4,0},{8,12},{12,8},{16,20},{20,16},{24,28},{28,24},{1,5},{5... | collective-permute-start | bytes 215048 | tf_op jit(solution)/shard_map/ppermute | solution.py:326
  73.1 8.6 %collective-permute-start.19 = (bf16[16,2240]{1,0:T(8,128)(2,1)S(1)}, bf16[16,2240]{1,0:T(8,128)(2,1)S(1)}, u32[]{:S(2)}, u32[]{:S(2)}) collective-permute-start(bf16[16,2240]{1,0:T(8,128)(2,1)S(1)} %get-tuple-element.48), channel_id=1, source_target_pairs={{0,8},{4,12},{8,0},{12,4},{16,24},{20,28},{24,16},{28,20},{1,9},{5... | collective-permute-start | bytes 215048 | tf_op jit(solution)/shard_map/ppermute | solution.py:326
  76.9 7.9 %collective-permute-start.20 = (bf16[16,2240]{1,0:T(8,128)(2,1)S(1)}, bf16[16,2240]{1,0:T(8,128)(2,1)S(1)}, u32[]{:S(2)}, u32[]{:S(2)}) collective-permute-start(bf16[16,2240]{1,0:T(8,128)(2,1)S(1)} %get-tuple-element.49), channel_id=1, source_target_pairs={{0,12},{4,8},{8,4},{12,0},{16,28},{20,24},{24,20},{28,16},{1,13},{... | collective-permute-start | bytes 215048 | tf_op jit(solution)/shard_map/ppermute | solution.py:326
  77.5 7.4 %collective-permute-start.21 = (bf16[16,2240]{1,0:T(8,128)(2,1)S(1)}, bf16[16,2240]{1,0:T(8,128)(2,1)S(1)}, u32[]{:S(2)}, u32[]{:S(2)}) collective-permute-start(bf16[16,2240]{1,0:T(8,128)(2,1)S(1)} %get-tuple-element.50), channel_id=1, source_target_pairs={{0,16},{4,20},{8,24},{12,28},{16,0},{20,4},{24,8},{28,12},{1,17},{... | collective-permute-start | bytes 215048 | tf_op jit(solution)/shard_map/ppermute | solution.py:326
  78.8 7.1 %collective-permute-start.22 = (bf16[16,2240]{1,0:T(8,128)(2,1)S(1)}, bf16[16,2240]{1,0:T(8,128)(2,1)S(1)}, u32[]{:S(2)}, u32[]{:S(2)}) collective-permute-start(bf16[16,2240]{1,0:T(8,128)(2,1)S(1)} %get-tuple-element.51), channel_id=1, source_target_pairs={{0,20},{4,16},{8,28},{12,24},{16,4},{20,0},{24,12},{28,8},{1,21},{... | collective-permute-start | bytes 215048 | tf_op jit(solution)/shard_map/ppermute | solution.py:326
  79.5 6.4 %collective-permute-start.23 = (bf16[16,2240]{1,0:T(8,128)(2,1)S(1)}, bf16[16,2240]{1,0:T(8,128)(2,1)S(1)}, u32[]{:S(2)}, u32[]{:S(2)}) collective-permute-start(bf16[16,2240]{1,0:T(8,128)(2,1)S(1)} %get-tuple-element.52), channel_id=1, source_target_pairs={{0,24},{4,28},{8,16},{12,20},{16,8},{20,12},{24,0},{28,4},{1,25},{... | collective-permute-start | bytes 215048 | tf_op jit(solution)/shard_map/ppermute | solution.py:326
  81.7 5.1 %collective-permute-start.24 = (bf16[16,2240]{1,0:T(8,128)(2,1)S(1)}, bf16[16,2240]{1,0:T(8,128)(2,1)S(1)}, u32[]{:S(2)}, u32[]{:S(2)}) collective-permute-start(bf16[16,2240]{1,0:T(8,128)(2,1)S(1)} %get-tuple-element.53), channel_id=1, source_target_pairs={{0,28},{4,24},{8,20},{12,16},{16,12},{20,8},{24,4},{28,0},{1,29},{... | collective-permute-start | bytes 215048 | tf_op jit(solution)/shard_map/ppermute | solution.py:326
  86.9 8.1 %collective-permute-start.27 = (bf16[16,2240]{1,0:T(8,128)(2,1)S(1)}, bf16[16,2240]{1,0:T(8,128)(2,1)S(1)}, u32[]{:S(2)}, u32[]{:S(2)}) collective-permute-start(bf16[16,2240]{1,0:T(8,128)(2,1)S(1)} %shard_map.85.refs_0_), channel_id=1, source_target_pairs={{0,3},{1,2},{2,1},{3,0},{4,7},{5,6},{6,5},{7,4},{8,11},{9,10},{10,... | collective-permute-start | bytes 215048 | tf_op jit(solution)/shard_map/ppermute | solution.py:326
  89.5 7.1 %collective-permute-start.26 = (bf16[16,2240]{1,0:T(8,128)(2,1)S(1)}, bf16[16,2240]{1,0:T(8,128)(2,1)S(1)}, u32[]{:S(2)}, u32[]{:S(2)}) collective-permute-start(bf16[16,2240]{1,0:T(8,128)(2,1)S(1)} %shard_map.85.refs_0_), channel_id=1, source_target_pairs={{0,2},{1,3},{2,0},{3,1},{4,6},{5,7},{6,4},{7,5},{8,10},{9,11},{10,... | collective-permute-start | bytes 215048 | tf_op jit(solution)/shard_map/ppermute | solution.py:326
  89.5 7.1 %collective-permute-start.25 = (bf16[16,2240]{1,0:T(8,128)(2,1)S(1)}, bf16[16,2240]{1,0:T(8,128)(2,1)S(1)}, u32[]{:S(2)}, u32[]{:S(2)}) collective-permute-start(bf16[16,2240]{1,0:T(8,128)(2,1)S(1)} %shard_map.85.refs_0_), channel_id=1, source_target_pairs={{0,1},{1,0},{2,3},{3,2},{4,5},{5,4},{6,7},{7,6},{8,9},{9,8},{10,11... | collective-permute-start | bytes 215048 | tf_op jit(solution)/shard_map/ppermute | solution.py:326
  (2 other events, 6.2 us)

commit v4 on v3

--- a/solution.py
+++ b/solution.py
@@ -113,8 +113,9 @@
     for part in range(PARTS):
         rows = state[part * ROWS : (part + 1) * ROWS, :]
         sorted_ref[part] = jnp.concatenate([rows, high.astype(F32), low.astype(F32)], 0)
-    for d, out in enumerate(out_refs):
-        out[...] = sorted_ref[rank ^ d].astype(BF16)
+    for k, out in enumerate(out_refs):
+        for i in range(PARTS // 2):
+            out[i] = sorted_ref[rank ^ (2 * i + k)].astype(BF16)
 
 
 def load_state(messages, state):
@@ -150,7 +151,7 @@
 
 
 def key_kernel(rank_ref, keys_ref, values_ref, *refs):
-    out_refs, (state, total, sorted_ref, key_rows, value_rows, sems) = refs[:PARTS], refs[PARTS:]
+    out_refs, (state, total, sorted_ref, key_rows, value_rows, sems) = refs[:2], refs[2:]
     tokens, frames, _ = keys_ref.shape
     cuts = [0, tokens // 16 * 8, tokens]
     arrivals = []
@@ -171,21 +172,35 @@
     write_messages(rank_ref[0], state[...], total[:1], sorted_ref, out_refs)
 
 
+def renewed(added, total):
+    high, low = split(total)
+    row = lax.broadcasted_iota(jnp.int32, added.shape, 0)
+    added = jnp.where(row == ROWS, high.astype(F32), added)
+    return jnp.where(row == ROWS + 1, low.astype(F32), added).astype(BF16)
+
+
+def total_in(added):
+    return added[ROWS : ROWS + 1] + added[ROWS + 1 : ROWS + 2]
+
+
+def pair_kernel(own_ref, got_ref, *out_refs):
+    for i, out in enumerate(out_refs):
+        added = own_ref[i].astype(F32) + got_ref[i].astype(F32)
+        out[...] = renewed(added, total_in(added))
+
+
 def sum_kernel(n_total, *refs):
     in_refs, out_ref = refs[:-1], refs[-1]
     in_refs, total_refs = in_refs[: len(in_refs) - n_total], in_refs[len(in_refs) - n_total :]
     added = in_refs[0][...].astype(F32)
     for ref in in_refs[1:]:
         added = added + ref[...].astype(F32)
-    if total_refs:
-        total = total_refs[0][:1]
-    else:
-        total = added[ROWS : ROWS + 1] + added[ROWS + 1 : ROWS + 2]
-    high, low = split(total)
-    row = lax.broadcasted_iota(jnp.int32, added.shape, 0)
-    added = jnp.where(row == ROWS, high.astype(F32), added)
-    added = jnp.where(row == ROWS + 1, low.astype(F32), added)
-    out_ref[...] = added.astype(BF16)
+    out_ref[...] = renewed(added, total_refs[0][:1] if total_refs else total_in(added))
+
+
+def stack_kernel(*refs):
+    for i, ref in enumerate(refs[:-1]):
+        refs[-1][i] = ref[...]
 
 
 def denominator_kernel(queries_ref, message_ref, inverse_ref, spread_ref):
@@ -207,19 +222,29 @@
     spread_ref[...] = jnp.where(lane < COPY, high, jnp.where(lane < 2 * COPY, middle, low)).astype(BF16)
 
 
-def query_kernel(frames, rank_ref, queries_ref, grad_ref, taps_ref, spread_ref, source_ref, *refs):
-    numer_ref, *refs = refs
-    out_refs, (state, sorted_ref, next_ref, sems) = refs[:PARTS], refs[PARTS:]
+def query_kernel(frames, rank_ref, queries_ref, grad_ref, taps_ref, spread_ref, *refs):
+    source_refs, (numer_ref, *refs) = refs[:2], refs[2:]
+    out_refs, (state, sorted_ref, next_ref, sems) = refs[:2], refs[2:]
     rows, width = queries_ref.shape
     blocks = spans(width)
     taps = taps_ref[...]
     taps = [taps[0:1] + 1.0, taps[1:2], taps[2:3]]
     state[...] = jnp.zeros_like(state)
     group = 8 if 8 % frames == 0 and rows % 8 == 0 else rows
+    cuts, arrivals = sorted({0, 1, min(4, len(blocks)), len(blocks)}), {}
+    for k, (begin, end) in enumerate(zip(cuts, cuts[1:])):
+        columns, first = slice(blocks[begin][0], blocks[end - 1][1]), 0
+        arrivals[begin] = []
+        for j, source in enumerate(source_refs):
+            last = first + source.shape[0] * frames
+            target = next_ref.at[first:last, columns]
+            copy = pltpu.make_async_copy(flat(source).at[:, columns], target, sems.at[j, k])
+            copy.start()
+            arrivals[begin].append(copy)
+            first = last
     for i, (start, stop, *_) in enumerate(blocks):
-        arrival = pltpu.make_async_copy(flat(source_ref).at[:, start:stop], next_ref.at[:, start:stop], sems.at[i])
-        arrival.start()
-        arrival.wait()
+        for copy in arrivals.get(i, ()):
+            copy.wait()
         shape = (rows // group, group, stop - start)
         frame = lax.broadcasted_iota(jnp.int32, shape, 1) % frames
         now = grad_ref[:, start:stop].astype(F32).reshape(shape)
@@ -240,13 +265,14 @@
 
 
 def sort_messages(rank, message_refs, sorted_ref, state):
-    for d, ref in enumerate(message_refs):
-        sorted_ref[rank ^ d] = ref[...].astype(F32)
+    for k, stack in enumerate(message_refs):
+        for i in range(PARTS // 2):
+            sorted_ref[rank ^ (2 * i + k)] = stack[i].astype(F32)
     load_state(sorted_ref, state)
 
 
 def side_kernel(rank_ref, queries_ref, numer_ref, inverse_ref, *refs):
-    message_refs, (sides_ref, total_ref, state, sorted_ref, wide) = refs[:PARTS], refs[PARTS:]
+    message_refs, (sides_ref, total_ref, state, sorted_ref, wide) = refs[:2], refs[2:]
     rows, width = queries_ref.shape
     blocks = spans(width)
     sort_messages(rank_ref[0], message_refs, sorted_ref, state)
@@ -271,9 +297,9 @@
 
 
 def query_grad_kernel(scale, rank_ref, queries_ref, numer_ref, sides_ref, *refs):
-    message_refs, (out_ref, state, sorted_ref, across, held, sems) = refs[:PARTS], refs[PARTS:]
+    message_refs, (out_ref, state, sorted_ref, across, held, sems) = refs[:2], refs[2:]
     blocks = spans(queries_ref.shape[1])
-    tot_high, tot_low = read_totals(message_refs[0])
+    tot_high, tot_low = read_totals(message_refs[0].at[0])
     sort_messages(rank_ref[0], message_refs, sorted_ref, state)
     for i, block in enumerate(blocks):
         across[i, : block[1] - block[0], : block[3] - block[2]] = rows_of(state, block)
@@ -336,11 +362,33 @@
     )(*parts, *totals)
 
 
-def spread_out(messages):
-    got = []
-    for d in range(1, PARTS):
-        got.append(exchange(messages[d], "frame", d))
-    return [messages[0], *got]
+def small(kernel, out_shape, *arrays):
+    return pl.pallas_call(
+        kernel,
+        out_shape=out_shape,
+        compiler_params=pltpu.CompilerParams(vmem_limit_bytes=8 << 20),
+        cost_estimate=cost(0, 4 * sum(x.size for x in arrays)),
+    )(*arrays)
+
+
+def fan(messages):
+    got = [messages[0]]
+    for i in range(1, PARTS // 2):
+        got.append(exchange(messages[i], "frame", 2 * i))
+    return got
+
+
+def scattered(stacks):
+    own, other = stacks
+    got = exchange(other, "frame", 1)
+    message = jax.ShapeDtypeStruct(own.shape[1:], BF16)
+    return fan(small(pair_kernel, [message] * (PARTS // 2), own, got))
+
+
+def gathered(part):
+    parts = fan([part] * (PARTS // 2))
+    own = small(stack_kernel, jax.ShapeDtypeStruct((len(parts), *part.shape), BF16), *parts)
+    return own, exchange(own, "frame", 1)
 
 
 def over_groups(part):
@@ -363,7 +411,7 @@
         x.transpose(1, 0, 2) for x in (grad_out, saved_queries, saved_keys, saved_values)
     )
     array = jax.ShapeDtypeStruct(grad_out.shape, BF16)
-    message = jax.ShapeDtypeStruct((ROWS + 2, width), BF16)
+    stack = jax.ShapeDtypeStruct((PARTS // 2, ROWS + 2, width), BF16)
     smem = pl.BlockSpec(memory_space=pltpu.SMEM)
     vmem = pl.BlockSpec(memory_space=pltpu.VMEM)
     window = max(block[3] - block[2] for block in spans(width))
@@ -389,19 +437,24 @@
             cost_estimate=cost(0, 2 * size * len(sources)),
         )(*sources)
 
+    def halo(source):
+        return lax.ppermute(source, "frame", [(i + 1, i) for i in range(devices - 1)])
+
+    early = tokens * 1 // 2 // 8 * 8
+    following = [halo(grad_out[:early])]
     key = pl.pallas_call(
         key_kernel,
         in_specs=[smem, anywhere, anywhere],
-        out_specs=[vmem] * PARTS,
-        out_shape=[message] * PARTS,
+        out_specs=[vmem] * 2,
+        out_shape=[stack] * 2,
         scratch_shapes=[state, pltpu.VMEM((8, width), F32), ordered, held, held, pltpu.SemaphoreType.DMA((4,))],
         compiler_params=LARGE,
         cost_estimate=cost(size * 512, 2 * size),
     )
     state_messages = key(rank, saved_keys, saved_values)
-    following = lax.ppermute(grad_out, "frame", [(i + 1, i) for i in range(devices - 1)])
+    following.append(halo(grad_out[early:]))
     query_rows, grad_rows = relay(saved_queries, grad_out)
-    part = over_groups(added(spread_out(state_messages)))
+    part = over_groups(added(scattered(state_messages)))
     per_head = (frames * tokens, LANES)
     denominators = pl.pallas_call(
         denominator_kernel,
@@ -412,18 +465,18 @@
     inverse, spread = denominators(query_rows, part)
     query = pl.pallas_call(
         functools.partial(query_kernel, frames),
-        in_specs=[smem] + [vmem] * 4 + [anywhere],
-        out_shape=[merged] + [message] * PARTS,
-        scratch_shapes=[state, ordered, held, sems],
+        in_specs=[smem] + [vmem] * 4 + [anywhere] * 2,
+        out_shape=[merged] + [stack] * 2,
+        scratch_shapes=[state, ordered, held, pltpu.SemaphoreType.DMA((2, len(spans(width))))],
         compiler_params=PARAMS,
         cost_estimate=cost(size * 1024, 4 * size),
     )
-    numer, *grad_messages = query(rank, query_rows, grad_rows, conv_taps, spread, following)
-    states = spread_out([part] * PARTS)
-    grad_parts = spread_out(grad_messages)
+    numer, *grad_messages = query(rank, query_rows, grad_rows, conv_taps, spread, *following)
+    states = gathered(part)
+    grad_parts = scattered(grad_messages)
     side = pl.pallas_call(
         side_kernel,
-        in_specs=[smem] + [vmem] * (3 + PARTS),
+        in_specs=[smem] + [vmem] * 5,
         out_shape=[jax.ShapeDtypeStruct(per_head, BF16), jax.ShapeDtypeStruct((8, width), F32)],
         scratch_shapes=[state, ordered, wide],
         compiler_params=PARAMS,
@@ -432,7 +485,7 @@
     sides, total = side(rank, query_rows, numer, inverse, *states)
     query_grad = pl.pallas_call(
         functools.partial(query_grad_kernel, scale),
-        in_specs=[smem] + [vmem] * (3 + PARTS),
+        in_specs=[smem] + [vmem] * 5,
         out_specs=anywhere,
         out_shape=array,
         scratch_shapes=[state, ordered, across, held, sems],

time: 112 us -> 89.8 us (0.80)
  waiting for transfers between devices: 32.1 us -> 16.9 us
  Pallas kernels: 35.1 us -> 27.4 us
  local copies, waits for them, and re-layouts: 0.91 us -> 7.23 us
  starting transfers between devices: 32.7 us -> 26.9 us
    ppermute x27 -> x18, waiting for transfers between devices: 32.1 us -> 16.9 us  [exchange(): return lax.ppermute(block, axis, [(i, i ^ distance) for i in devices])]
    pallas_call x1 -> x4, Pallas kernels: 12.5 us -> 4.81 us  [the longest x1 4.43 us: shards(): query(rank, query_rows, grad_rows, conv_taps, spread, *following)]
    ppermute x27 -> x18, starting transfers between devices: 31.4 us -> 24.4 us  [exchange(): return lax.ppermute(block, axis, [(i, i ^ distance) for i in devices])]
    slice x0 -> x2, local copies, waits for them, and re-layouts: none -> 4.68 us  [the longest x1 3.09 us: shards(): following.append(halo(grad_out[early:]))]
    unnamed x12, local copies, waits for them, and re-layouts: 0.91 us -> 2.55 us
    ppermute x1 -> x2, starting transfers between devices: 1.29 us -> 2.56 us  [halo(): lax.ppermute(source, 'frame', [(i + 1, i) for i in range(devices - 1)])]
  transfers between devices with their start and end apart: 28 -> 20, of which waited for: 8 -> 5; matrix products, arithmetic and copies ran while one was open for 0% -> 2% of each run, Pallas kernels for 27% -> 25%
where the time goes in v4:
time: 89.8 us; the launch traced here: 89.5 us
  Pallas kernels  27.4 us (31%)
  starting transfers between devices  26.9 us (30%)
  waiting for transfers between devices  16.9 us (19%)
  blocking collectives  10.1 us (11%)
  local copies, waits for them, and re-layouts  7.23 us (8%)
  between operations  1.04 us (1%)
    ppermute x18, starting transfers between devices, exchange(): return lax.ppermute(block, axis, [(i, i ^ distance) for i in devices])  24.4 us
    ppermute x18, waiting for transfers between devices, exchange(): return lax.ppermute(block, axis, [(i, i ^ distance) for i in devices])  16.9 us
    all_gather x1, blocking collectives, shards(): lax.all_gather(part, 'frame', axis_index_groups=groups if len(groups) > 1...  10.1 us
    pallas_call x2, Pallas kernels, relay(): pl.pallas_call(relay_kernel, in_specs=[anywhere] * len(sources), out_spec...  5.85 us
    pallas_call x1, Pallas kernels, shards(): pl.pallas_call(functools.partial(key_grad_kernel, scale), in_specs=[vmem]...  4.91 us
    pallas_call x1, Pallas kernels, shards(): query(rank, query_rows, grad_rows, conv_taps, spread, *following)  4.43 us
    pallas_call x1, Pallas kernels, shards(): state_messages = key(rank, saved_keys, saved_values)  4.12 us
    pallas_call x1, Pallas kernels, shards(): grad_queries = query_grad(rank, query_rows, numer, sides, *states)  3.64 us
  transfers between devices with their start and end apart: 20, of which 5 were waited for; matrix products, arithmetic and copies ran while one was open for 2% of the time, Pallas kernels for 25%

profile of v4, /device:TPU:0, one launch (start us, length us, event | category | flops | bytes accessed | tf_op | source)
XLA Modules:
  0.0 89.5 jit_solution(16617139882028196449)
XLA Ops:
  0.6 3.1 %slice.9 = bf16[116,2,2240]{2,1,0:T(2,128)(2,1)} slice(bf16[220,2,2240]{2,1,0:T(2,128)(2,1)} %bitcast.9), slice={[104:220], [0:2], [0:2240]} | slice | bytes 2078720 | tf_op jit(solution)/shard_map/slice | solution.py:455
  3.7 1.3 %collective-permute-start.8 = (bf16[116,2,2240]{2,1,0:T(2,128)(2,1)}, bf16[116,2,2240]{2,1,0:T(2,128)(2,1)S(1)}, u32[]{:S(2)}, u32[]{:S(2)}) collective-permute-start(bf16[116,2,2240]{2,1,0:T(2,128)(2,1)} %slice.9), channel_id=1, source_target_pairs={{4,0},{8,4},{12,8},{16,12},{20,16},{24,20},{28,24},{5,1},{9,5},{13... | collective-permute-start | bytes 3118088 | tf_op jit(solution)/shard_map/ppermute | solution.py:441
  5.0 1.6 %slice.8 = bf16[104,2,2240]{2,1,0:T(2,128)(2,1)} slice(bf16[220,2,2240]{2,1,0:T(2,128)(2,1)S(1)} %bitcast.10), slice={[0:104], [0:2], [0:2240]} | slice | bytes 1863680 | tf_op jit(solution)/shard_map/slice | solution.py:444
  6.6 1.3 %collective-permute-start.7 = (bf16[104,2,2240]{2,1,0:T(2,128)(2,1)}, bf16[104,2,2240]{2,1,0:T(2,128)(2,1)}, u32[]{:S(2)}, u32[]{:S(2)}) collective-permute-start(bf16[104,2,2240]{2,1,0:T(2,128)(2,1)} %slice.8), channel_id=1, source_target_pairs={{4,0},{8,4},{12,8},{16,12},{20,16},{24,20},{28,24},{5,1},{9,5},{13... | collective-permute-start | bytes 2795528 | tf_op jit(solution)/shard_map/ppermute | solution.py:441
  7.9 4.1 %shard_map.77 = (bf16[4,16,2240]{2,1,0:T(8,128)(2,1)}, bf16[4,16,2240]{2,1,0:T(8,128)(2,1)}) custom-call(s32[1]{0:T(128)} %bitcast.rank_ref, bf16[220,2,2240]{2,1,0:T(2,128)(2,1)} %bitcast.12, bf16[220,2,2240]{2,1,0:T(2,128)(2,1)} %bitcast.14), custom_call_target="tpu_custom_call" | custom-call | flops 1009254400 | bytes 3942400 | tf_op jit(solution)/shard_map/pallas_call | solution.py:454
  12.1 1.8 %collective-permute-start = (bf16[4,16,2240]{2,1,0:T(8,128)(2,1)}, bf16[4,16,2240]{2,1,0:T(8,128)(2,1)S(1)}, u32[]{:S(2)}, u32[]{:S(2)}) collective-permute-start(bf16[4,16,2240]{2,1,0:T(8,128)(2,1)} %get-tuple-element.29), channel_id=1, source_target_pairs={{0,4},{4,0},{8,12},{12,8},{16,20},{20,16},{24,28},{28,24},{1,5},{5... | collective-permute-start | bytes 860168 | tf_op jit(solution)/shard_map/ppermute | solution.py:352
  13.9 1.4 %collective-permute-done.got_ref = bf16[4,16,2240]{2,1,0:T(8,128)(2,1)S(1)} collective-permute-done((bf16[4,16,2240]{2,1,0:T(8,128)(2,1)}, bf16[4,16,2240]{2,1,0:T(8,128)(2,1)S(1)}, u32[]{:S(2)}, u32[]{:S(2)}) %collective-permute-start) | collective-permute-done | bytes 286752 | tf_op jit(solution)/shard_map/ppermute | solution.py:352
  15.3 1.0 %copy-done.4 = bf16[4,16,2240]{2,1,0:T(8,128)(2,1)S(1)} copy-done((bf16[4,16,2240]{2,1,0:T(8,128)(2,1)S(1)}, bf16[4,16,2240]{2,1,0:T(8,128)(2,1)}, u32[]{:S(2)}) %copy-start.4) | copy-done | bytes 286744
  16.4 3.0 %collective-permute-start.1 = (bf16[16,2240]{1,0:T(8,128)(2,1)S(1)}, bf16[16,2240]{1,0:T(8,128)(2,1)S(1)}, u32[]{:S(2)}, u32[]{:S(2)}) collective-permute-start(bf16[16,2240]{1,0:T(8,128)(2,1)S(1)} %get-tuple-element.31), channel_id=1, source_target_pairs={{0,8},{4,12},{8,0},{12,4},{16,24},{20,28},{24,16},{28,20},{1,9},{5... | collective-permute-start | bytes 215048 | tf_op jit(solution)/shard_map/ppermute | solution.py:352
  19.5 2.4 %collective-permute-start.2 = (bf16[16,2240]{1,0:T(8,128)(2,1)S(1)}, bf16[16,2240]{1,0:T(8,128)(2,1)S(1)}, u32[]{:S(2)}, u32[]{:S(2)}) collective-permute-start(bf16[16,2240]{1,0:T(8,128)(2,1)S(1)} %get-tuple-element.32), channel_id=1, source_target_pairs={{0,16},{4,20},{8,24},{12,28},{16,0},{20,4},{24,8},{28,12},{1,17},{... | collective-permute-start | bytes 215048 | tf_op jit(solution)/shard_map/ppermute | solution.py:352
  22.4 12.1 %collective-permute-done.1.refs_1_ = bf16[16,2240]{1,0:T(8,128)(2,1)S(1)} collective-permute-done((bf16[16,2240]{1,0:T(8,128)(2,1)S(1)}, bf16[16,2240]{1,0:T(8,128)(2,1)S(1)}, u32[]{:S(2)}, u32[]{:S(2)}) %collective-permute-start.1) | collective-permute-done | bytes 71712 | tf_op jit(solution)/shard_map/ppermute | solution.py:352
  34.4 1.7 %collective-permute-done.3.refs_3_ = bf16[16,2240]{1,0:T(8,128)(2,1)S(1)} collective-permute-done((bf16[16,2240]{1,0:T(8,128)(2,1)S(1)}, bf16[16,2240]{1,0:T(8,128)(2,1)S(1)}, u32[]{:S(2)}, u32[]{:S(2)}) %collective-permute-start.3) | collective-permute-done | bytes 71712 | tf_op jit(solution)/shard_map/ppermute | solution.py:352
  36.2 3.7 %collective-permute-start.6 = (bf16[16,2240]{1,0:T(8,128)(2,1)S(1)}, bf16[16,2240]{1,0:T(8,128)(2,1)S(1)}, u32[]{:S(2)}, u32[]{:S(2)}) collective-permute-start(bf16[16,2240]{1,0:T(8,128)(2,1)S(1)} %shard_map.79.refs_0_), channel_id=1, source_target_pairs={{0,3},{1,2},{2,1},{3,0},{4,7},{5,6},{6,5},{7,4},{8,11},{9,10},{10,... | collective-permute-start | bytes 215048 | tf_op jit(solution)/shard_map/ppermute | solution.py:352
  39.9 0.8 collective-permute-start.4
  40.7 1.6 %copy-done.3 = bf16[2,220,2240]{2,0,1:T(2,128)(2,1)S(1)} copy-done((bf16[2,220,2240]{2,0,1:T(2,128)(2,1)S(1)}, bf16[2,220,2240]{2,0,1:T(2,128)(2,1)}, u32[]{:S(2)}) %copy-start.3) | copy-done | bytes 1971224
  42.3 2.8 %shard_map.76 = (bf16[440,2240]{1,0:T(8,128)(2,1)S(1)}, bf16[440,2240]{1,0:T(8,128)(2,1)S(1)}) custom-call(bf16[220,2,2240]{2,1,0:T(2,128)(2,1)S(1)} %bitcast.16, bf16[220,2,2240]{2,1,0:T(2,128)(2,1)S(1)} %bitcast.11), custom_call_target="tpu_custom_call" | custom-call | bytes 7884800 | tf_op jit(solution)/shard_map/pallas_call | solution.py:430
  45.2 1.1 %collective-permute-start.11 = (bf16[16,2240]{1,0:T(8,128)(2,1)S(1)}, bf16[16,2240]{1,0:T(8,128)(2,1)S(1)}, u32[]{:S(2)}, u32[]{:S(2)}) collective-permute-start(bf16[16,2240]{1,0:T(8,128)(2,1)S(1)} %shard_map.80.message_ref.refs_0_), channel_id=1, source_target_pairs={{0,24},{4,28},{8,16},{12,20},{16,8},{20,12},{24,0},{28,4},{1,25},{... | collective-permute-start | bytes 215048 | tf_op jit(solution)/shard_map/ppermute | solution.py:352
  46.4 2.3 %collective-permute-start.10 = (bf16[16,2240]{1,0:T(8,128)(2,1)S(1)}, bf16[16,2240]{1,0:T(8,128)(2,1)S(1)}, u32[]{:S(2)}, u32[]{:S(2)}) collective-permute-start(bf16[16,2240]{1,0:T(8,128)(2,1)S(1)} %shard_map.80.message_ref.refs_0_), channel_id=1, source_target_pairs={{0,16},{4,20},{8,24},{12,28},{16,0},{20,4},{24,8},{28,12},{1,17},{... | collective-permute-start | bytes 215048 | tf_op jit(solution)/shard_map/ppermute | solution.py:352
  48.8 0.8 shard_map.81
  49.7 4.4 %shard_map.82 = (bf16[440,2240]{1,0:T(8,128)(2,1)S(1)}, bf16[4,16,2240]{2,1,0:T(8,128)(2,1)S(1)}, bf16[4,16,2240]{2,1,0:T(8,128)(2,1)S(1)}) custom-call(s32[1]{0:T(128)} %bitcast.rank_ref, bf16[440,2240]{1,0:T(8,128)(2,1)S(1)} %get-tuple-element.26.queries_ref, bf16[440,2240]{1,0:T(8,128)(2,1)S(1)} %get-tuple-element.27.grad_ref, f32[3,2240]{1,0:T(4,128)S(1)} %copy-done.5, ...), custom_call_target="tpu_custom_call" | custom-call | flops 2018508800 | bytes 7884800 | tf_op jit(solution)/shard_map/pallas_call | solution.py:474
  54.2 0.5 collective-permute-start.12
  54.8 3.0 %shard_map.86 = (bf16[440,2240]{1,0:T(8,128)(2,1)S(1)}, bf16[440,2240]{1,0:T(8,128)(2,1)S(1)}) custom-call(bf16[220,2,2240]{2,1,0:T(2,128)(2,1)S(1)} %bitcast.13, bf16[220,2,2240]{2,1,0:T(2,128)(2,1)S(1)} %bitcast.15), custom_call_target="tpu_custom_call" | custom-call | bytes 7884800 | tf_op jit(solution)/shard_map/pallas_call | solution.py:430
  58.0 2.0 %collective-permute-start.14 = (bf16[16,2240]{1,0:T(8,128)(2,1)S(1)}, bf16[16,2240]{1,0:T(8,128)(2,1)S(1)}, u32[]{:S(2)}, u32[]{:S(2)}) collective-permute-start(bf16[16,2240]{1,0:T(8,128)(2,1)S(1)} %get-tuple-element.43), channel_id=1, source_target_pairs={{0,8},{4,12},{8,0},{12,4},{16,24},{20,28},{24,16},{28,20},{1,9},{5... | collective-permute-start | bytes 215048 | tf_op jit(solution)/shard_map/ppermute | solution.py:352
  60.0 1.6 %collective-permute-start.16 = (bf16[16,2240]{1,0:T(8,128)(2,1)S(1)}, bf16[16,2240]{1,0:T(8,128)(2,1)S(1)}, u32[]{:S(2)}, u32[]{:S(2)}) collective-permute-start(bf16[16,2240]{1,0:T(8,128)(2,1)S(1)} %get-tuple-element.45), channel_id=1, source_target_pairs={{0,24},{4,28},{8,16},{12,20},{16,8},{20,12},{24,0},{28,4},{1,25},{... | collective-permute-start | bytes 215048 | tf_op jit(solution)/shard_map/ppermute | solution.py:352
  61.6 3.0 %shard_map.84 = (bf16[440,128]{1,0:T(8,128)(2,1)S(1)}, f32[8,2240]{1,0:T(8,128)S(1)}) custom-call(s32[1]{0:T(128)} %bitcast.rank_ref, bf16[440,2240]{1,0:T(8,128)(2,1)S(1)} %get-tuple-element.26.queries_ref, bf16[440,2240]{1,0:T(8,128)(2,1)S(1)} %get-tuple-element.35.numer_ref, f32[440,128]{1,0:T(8,128)S(1)} %get-tuple-element.36.inverse_ref, ...), custom_call_target="tpu_custom_call" | custom-call | flops 1009254400 | bytes 3942400 | tf_op jit(solution)/shard_map/pallas_call | solution.py:485
  64.5 1.1 %collective-permute-done.15.refs_2_ = bf16[16,2240]{1,0:T(8,128)(2,1)S(1)} collective-permute-done((bf16[16,2240]{1,0:T(8,128)(2,1)S(1)}, bf16[16,2240]{1,0:T(8,128)(2,1)S(1)}, u32[]{:S(2)}, u32[]{:S(2)}) %collective-permute-start.15) | collective-permute-done | bytes 71712 | tf_op jit(solution)/shard_map/ppermute | solution.py:352
  65.7 3.1 %collective-permute-start.19 = (bf16[16,2240]{1,0:T(8,128)(2,1)S(1)}, bf16[16,2240]{1,0:T(8,128)(2,1)S(1)}, u32[]{:S(2)}, u32[]{:S(2)}) collective-permute-start(bf16[16,2240]{1,0:T(8,128)(2,1)S(1)} %shard_map.88.refs_0_), channel_id=1, source_target_pairs={{0,3},{1,2},{2,1},{3,0},{4,7},{5,6},{6,5},{7,4},{8,11},{9,10},{10,... | collective-permute-start | bytes 215048 | tf_op jit(solution)/shard_map/ppermute | solution.py:352
  68.8 1.3 %collective-permute-start.17 = (bf16[16,2240]{1,0:T(8,128)(2,1)S(1)}, bf16[16,2240]{1,0:T(8,128)(2,1)S(1)}, u32[]{:S(2)}, u32[]{:S(2)}) collective-permute-start(bf16[16,2240]{1,0:T(8,128)(2,1)S(1)} %shard_map.88.refs_0_), channel_id=1, source_target_pairs={{0,1},{1,0},{2,3},{3,2},{4,5},{5,4},{6,7},{7,6},{8,9},{9,8},{10,11... | collective-permute-start | bytes 215048 | tf_op jit(solution)/shard_map/ppermute | solution.py:352
  70.1 3.6 %shard_map.85 = bf16[220,2,2240]{2,1,0:T(2,128)(2,1)} custom-call(s32[1]{0:T(128)} %bitcast.rank_ref, bf16[440,2240]{1,0:T(8,128)(2,1)S(1)} %get-tuple-element.26.queries_ref, bf16[440,2240]{1,0:T(8,128)(2,1)S(1)} %get-tuple-element.35.numer_ref, bf16[440,128]{1,0:T(8,128)(2,1)S(1)} %get-tuple-element.37.sides_ref, ...), custom_call_target="tpu_custom_call" | custom-call | flops 1009254400 | bytes 5913600 | tf_op jit(solution)/shard_map/pallas_call | solution.py:495
  73.8 0.5 collective-permute-done.18.refs_2_
  74.4 10.1 %all-gather = bf16[128,2240]{1,0:T(8,128)(2,1)S(1)} all-gather(bf16[16,2240]{1,0:T(8,128)(2,1)S(1)} %shard_map.89), channel_id=2, replica_groups=mesh['frame'=8,'space'=4] {'frame'}, dimensions={0}, use_global_device_ids=true | all-gather | bytes 645120 | tf_op jit(solution)/shard_map/all_gather | solution.py:499
  84.5 4.9 %shard_map.90 = (bf16[220,2,2240]{2,1,0:T(2,128)(2,1)}, bf16[220,2,2240]{2,1,0:T(2,128)(2,1)}) custom-call(bf16[440,2240]{1,0:T(8,128)(2,1)S(1)} %get-tuple-element.38.keys_ref, bf16[440,2240]{1,0:T(8,128)(2,1)S(1)} %get-tuple-element.39.values_ref, bf16[8,16,2240]{2,1,0:T(8,128)(2,1)S(1)} %bitcast.17), custom_call_target="tpu_custom_call" | custom-call | flops 2018508800 | bytes 7884800 | tf_op jit(solution)/shard_map/pallas_call | solution.py:500
  (38 shorter events, 1.4 us)
Async XLA Ops:
  0.6 4.4 %copy-start = (bf16[2,220,2240]{2,0,1:T(2,128)(2,1)S(1)}, bf16[2,220,2240]{2,0,1:T(2,128)(2,1)}, u32[]{:S(2)}) copy-start(bf16[2,220,2240]{2,0,1:T(2,128)(2,1)} %param.5) | copy-start | bytes 5913604
  3.7 45.9 %collective-permute-start.8 = (bf16[116,2,2240]{2,1,0:T(2,128)(2,1)}, bf16[116,2,2240]{2,1,0:T(2,128)(2,1)S(1)}, u32[]{:S(2)}, u32[]{:S(2)}) collective-permute-start(bf16[116,2,2240]{2,1,0:T(2,128)(2,1)} %slice.9), channel_id=1, source_target_pairs={{4,0},{8,4},{12,8},{16,12},{20,16},{24,20},{28,24},{5,1},{9,5},{13... | collective-permute-start | bytes 3118088 | tf_op jit(solution)/shard_map/ppermute | solution.py:441
  6.6 43.0 %collective-permute-start.7 = (bf16[104,2,2240]{2,1,0:T(2,128)(2,1)}, bf16[104,2,2240]{2,1,0:T(2,128)(2,1)}, u32[]{:S(2)}, u32[]{:S(2)}) collective-permute-start(bf16[104,2,2240]{2,1,0:T(2,128)(2,1)} %slice.8), channel_id=1, source_target_pairs={{4,0},{8,4},{12,8},{16,12},{20,16},{24,20},{28,24},{5,1},{9,5},{13... | collective-permute-start | bytes 2795528 | tf_op jit(solution)/shard_map/ppermute | solution.py:441
  12.1 3.2 %collective-permute-start = (bf16[4,16,2240]{2,1,0:T(8,128)(2,1)}, bf16[4,16,2240]{2,1,0:T(8,128)(2,1)S(1)}, u32[]{:S(2)}, u32[]{:S(2)}) collective-permute-start(bf16[4,16,2240]{2,1,0:T(8,128)(2,1)} %get-tuple-element.29), channel_id=1, source_target_pairs={{0,4},{4,0},{8,12},{12,8},{16,20},{20,16},{24,28},{28,24},{1,5},{5... | collective-permute-start | bytes 860168 | tf_op jit(solution)/shard_map/ppermute | solution.py:352
  15.3 1.0 %copy-start.4 = (bf16[4,16,2240]{2,1,0:T(8,128)(2,1)S(1)}, bf16[4,16,2240]{2,1,0:T(8,128)(2,1)}, u32[]{:S(2)}) copy-start(bf16[4,16,2240]{2,1,0:T(8,128)(2,1)} %get-tuple-element.28.own_ref) | copy-start | bytes 860164
  16.4 18.0 %collective-permute-start.1 = (bf16[16,2240]{1,0:T(8,128)(2,1)S(1)}, bf16[16,2240]{1,0:T(8,128)(2,1)S(1)}, u32[]{:S(2)}, u32[]{:S(2)}) collective-permute-start(bf16[16,2240]{1,0:T(8,128)(2,1)S(1)} %get-tuple-element.31), channel_id=1, source_target_pairs={{0,8},{4,12},{8,0},{12,4},{16,24},{20,28},{24,16},{28,20},{1,9},{5... | collective-permute-start | bytes 215048 | tf_op jit(solution)/shard_map/ppermute | solution.py:352
  19.5 15.0 %collective-permute-start.2 = (bf16[16,2240]{1,0:T(8,128)(2,1)S(1)}, bf16[16,2240]{1,0:T(8,128)(2,1)S(1)}, u32[]{:S(2)}, u32[]{:S(2)}) collective-permute-start(bf16[16,2240]{1,0:T(8,128)(2,1)S(1)} %get-tuple-element.32), channel_id=1, source_target_pairs={{0,16},{4,20},{8,24},{12,28},{16,0},{20,4},{24,8},{28,12},{1,17},{... | collective-permute-start | bytes 215048 | tf_op jit(solution)/shard_map/ppermute | solution.py:352
  21.9 14.3 %collective-permute-start.3 = (bf16[16,2240]{1,0:T(8,128)(2,1)S(1)}, bf16[16,2240]{1,0:T(8,128)(2,1)S(1)}, u32[]{:S(2)}, u32[]{:S(2)}) collective-permute-start(bf16[16,2240]{1,0:T(8,128)(2,1)S(1)} %get-tuple-element.33), channel_id=1, source_target_pairs={{0,24},{4,28},{8,16},{12,20},{16,8},{20,12},{24,0},{28,4},{1,25},{... | collective-permute-start | bytes 215048 | tf_op jit(solution)/shard_map/ppermute | solution.py:352
  36.2 8.9 %collective-permute-start.6 = (bf16[16,2240]{1,0:T(8,128)(2,1)S(1)}, bf16[16,2240]{1,0:T(8,128)(2,1)S(1)}, u32[]{:S(2)}, u32[]{:S(2)}) collective-permute-start(bf16[16,2240]{1,0:T(8,128)(2,1)S(1)} %shard_map.79.refs_0_), channel_id=1, source_target_pairs={{0,3},{1,2},{2,1},{3,0},{4,7},{5,6},{6,5},{7,4},{8,11},{9,10},{10,... | collective-permute-start | bytes 215048 | tf_op jit(solution)/shard_map/ppermute | solution.py:352
  39.9 5.3 %collective-permute-start.5 = (bf16[16,2240]{1,0:T(8,128)(2,1)S(1)}, bf16[16,2240]{1,0:T(8,128)(2,1)S(1)}, u32[]{:S(2)}, u32[]{:S(2)}) collective-permute-start(bf16[16,2240]{1,0:T(8,128)(2,1)S(1)} %shard_map.79.refs_0_), channel_id=1, source_target_pairs={{0,2},{1,3},{2,0},{3,1},{4,6},{5,7},{6,4},{7,5},{8,10},{9,11},{10,... | collective-permute-start | bytes 215048 | tf_op jit(solution)/shard_map/ppermute | solution.py:352
  39.9 5.3 %collective-permute-start.4 = (bf16[16,2240]{1,0:T(8,128)(2,1)S(1)}, bf16[16,2240]{1,0:T(8,128)(2,1)S(1)}, u32[]{:S(2)}, u32[]{:S(2)}) collective-permute-start(bf16[16,2240]{1,0:T(8,128)(2,1)S(1)} %shard_map.79.refs_0_), channel_id=1, source_target_pairs={{0,1},{1,0},{2,3},{3,2},{4,5},{5,4},{6,7},{7,6},{8,9},{9,8},{10,11... | collective-permute-start | bytes 215048 | tf_op jit(solution)/shard_map/ppermute | solution.py:352
  40.7 1.6 %copy-start.3 = (bf16[2,220,2240]{2,0,1:T(2,128)(2,1)S(1)}, bf16[2,220,2240]{2,0,1:T(2,128)(2,1)}, u32[]{:S(2)}) copy-start(bf16[2,220,2240]{2,0,1:T(2,128)(2,1)} %param.7) | copy-start | bytes 5913604
  45.1 4.5 %copy-start.5 = (f32[3,2240]{1,0:T(4,128)S(1)}, f32[3,2240]{1,0:T(4,128)}, u32[]{:S(2)}) copy-start(f32[3,2240]{1,0:T(4,128)} %taps_ref.1) | copy-start | bytes 80644
  45.2 8.9 %collective-permute-start.11 = (bf16[16,2240]{1,0:T(8,128)(2,1)S(1)}, bf16[16,2240]{1,0:T(8,128)(2,1)S(1)}, u32[]{:S(2)}, u32[]{:S(2)}) collective-permute-start(bf16[16,2240]{1,0:T(8,128)(2,1)S(1)} %shard_map.80.message_ref.refs_0_), channel_id=1, source_target_pairs={{0,24},{4,28},{8,16},{12,20},{16,8},{20,12},{24,0},{28,4},{1,25},{... | collective-permute-start | bytes 215048 | tf_op jit(solution)/shard_map/ppermute | solution.py:352
  46.4 7.8 %collective-permute-start.10 = (bf16[16,2240]{1,0:T(8,128)(2,1)S(1)}, bf16[16,2240]{1,0:T(8,128)(2,1)S(1)}, u32[]{:S(2)}, u32[]{:S(2)}) collective-permute-start(bf16[16,2240]{1,0:T(8,128)(2,1)S(1)} %shard_map.80.message_ref.refs_0_), channel_id=1, source_target_pairs={{0,16},{4,20},{8,24},{12,28},{16,0},{20,4},{24,8},{28,12},{1,17},{... | collective-permute-start | bytes 215048 | tf_op jit(solution)/shard_map/ppermute | solution.py:352
  48.7 5.5 %collective-permute-start.9 = (bf16[16,2240]{1,0:T(8,128)(2,1)S(1)}, bf16[16,2240]{1,0:T(8,128)(2,1)S(1)}, u32[]{:S(2)}, u32[]{:S(2)}) collective-permute-start(bf16[16,2240]{1,0:T(8,128)(2,1)S(1)} %shard_map.80.message_ref.refs_0_), channel_id=1, source_target_pairs={{0,8},{4,12},{8,0},{12,4},{16,24},{20,28},{24,16},{28,20},{1,9},{5... | collective-permute-start | bytes 215048 | tf_op jit(solution)/shard_map/ppermute | solution.py:352
  49.6 5.2 %copy-start.1 = (bf16[2,220,2240]{2,0,1:T(2,128)(2,1)S(1)}, bf16[2,220,2240]{2,0,1:T(2,128)(2,1)}, u32[]{:S(2)}) copy-start(bf16[2,220,2240]{2,0,1:T(2,128)(2,1)} %param.8) | copy-start | bytes 5913604
  49.6 5.1 %copy-start.2 = (bf16[2,220,2240]{2,0,1:T(2,128)(2,1)S(1)}, bf16[2,220,2240]{2,0,1:T(2,128)(2,1)}, u32[]{:S(2)}) copy-start(bf16[2,220,2240]{2,0,1:T(2,128)(2,1)} %param.9) | copy-start | bytes 5913604
  54.1 3.7 %collective-permute-start.13 = (bf16[4,16,2240]{2,1,0:T(8,128)(2,1)S(1)}, bf16[4,16,2240]{2,1,0:T(8,128)(2,1)S(1)}, u32[]{:S(2)}, u32[]{:S(2)}) collective-permute-start(bf16[4,16,2240]{2,1,0:T(8,128)(2,1)S(1)} %get-tuple-element.41), channel_id=1, source_target_pairs={{0,4},{4,0},{8,12},{12,8},{16,20},{20,16},{24,28},{28,24},{1,5},{5... | collective-permute-start | bytes 860168 | tf_op jit(solution)/shard_map/ppermute | solution.py:352
  54.2 7.3 %collective-permute-start.12 = (bf16[4,16,2240]{2,1,0:T(8,128)(2,1)S(1)}, bf16[4,16,2240]{2,1,0:T(8,128)(2,1)S(1)}, u32[]{:S(2)}, u32[]{:S(2)}) collective-permute-start(bf16[4,16,2240]{2,1,0:T(8,128)(2,1)S(1)} %shard_map.83.refs_0_), channel_id=1, source_target_pairs={{0,4},{4,0},{8,12},{12,8},{16,20},{20,16},{24,28},{28,24},{1,5},{5... | collective-permute-start | bytes 860168 | tf_op jit(solution)/shard_map/ppermute | solution.py:352
  58.0 6.5 %collective-permute-start.14 = (bf16[16,2240]{1,0:T(8,128)(2,1)S(1)}, bf16[16,2240]{1,0:T(8,128)(2,1)S(1)}, u32[]{:S(2)}, u32[]{:S(2)}) collective-permute-start(bf16[16,2240]{1,0:T(8,128)(2,1)S(1)} %get-tuple-element.43), channel_id=1, source_target_pairs={{0,8},{4,12},{8,0},{12,4},{16,24},{20,28},{24,16},{28,20},{1,9},{5... | collective-permute-start | bytes 215048 | tf_op jit(solution)/shard_map/ppermute | solution.py:352
  60.0 5.6 %collective-permute-start.15 = (bf16[16,2240]{1,0:T(8,128)(2,1)S(1)}, bf16[16,2240]{1,0:T(8,128)(2,1)S(1)}, u32[]{:S(2)}, u32[]{:S(2)}) collective-permute-start(bf16[16,2240]{1,0:T(8,128)(2,1)S(1)} %get-tuple-element.44), channel_id=1, source_target_pairs={{0,16},{4,20},{8,24},{12,28},{16,0},{20,4},{24,8},{28,12},{1,17},{... | collective-permute-start | bytes 215048 | tf_op jit(solution)/shard_map/ppermute | solution.py:352
  60.0 5.6 %collective-permute-start.16 = (bf16[16,2240]{1,0:T(8,128)(2,1)S(1)}, bf16[16,2240]{1,0:T(8,128)(2,1)S(1)}, u32[]{:S(2)}, u32[]{:S(2)}) collective-permute-start(bf16[16,2240]{1,0:T(8,128)(2,1)S(1)} %get-tuple-element.45), channel_id=1, source_target_pairs={{0,24},{4,28},{8,16},{12,20},{16,8},{20,12},{24,0},{28,4},{1,25},{... | collective-permute-start | bytes 215048 | tf_op jit(solution)/shard_map/ppermute | solution.py:352
  65.7 8.1 %collective-permute-start.19 = (bf16[16,2240]{1,0:T(8,128)(2,1)S(1)}, bf16[16,2240]{1,0:T(8,128)(2,1)S(1)}, u32[]{:S(2)}, u32[]{:S(2)}) collective-permute-start(bf16[16,2240]{1,0:T(8,128)(2,1)S(1)} %shard_map.88.refs_0_), channel_id=1, source_target_pairs={{0,3},{1,2},{2,1},{3,0},{4,7},{5,6},{6,5},{7,4},{8,11},{9,10},{10,... | collective-permute-start | bytes 215048 | tf_op jit(solution)/shard_map/ppermute | solution.py:352
  68.8 5.5 %collective-permute-start.18 = (bf16[16,2240]{1,0:T(8,128)(2,1)S(1)}, bf16[16,2240]{1,0:T(8,128)(2,1)S(1)}, u32[]{:S(2)}, u32[]{:S(2)}) collective-permute-start(bf16[16,2240]{1,0:T(8,128)(2,1)S(1)} %shard_map.88.refs_0_), channel_id=1, source_target_pairs={{0,2},{1,3},{2,0},{3,1},{4,6},{5,7},{6,4},{7,5},{8,10},{9,11},{10,... | collective-permute-start | bytes 215048 | tf_op jit(solution)/shard_map/ppermute | solution.py:352
  68.8 5.5 %collective-permute-start.17 = (bf16[16,2240]{1,0:T(8,128)(2,1)S(1)}, bf16[16,2240]{1,0:T(8,128)(2,1)S(1)}, u32[]{:S(2)}, u32[]{:S(2)}) collective-permute-start(bf16[16,2240]{1,0:T(8,128)(2,1)S(1)} %shard_map.88.refs_0_), channel_id=1, source_target_pairs={{0,1},{1,0},{2,3},{3,2},{4,5},{5,4},{6,7},{7,6},{8,9},{9,8},{10,11... | collective-permute-start | bytes 215048 | tf_op jit(solution)/shard_map/ppermute | solution.py:352

commit v5 on v4

--- a/solution.py
+++ b/solution.py
@@ -18,7 +18,7 @@
 PARTS = E // ROWS
 COPY = 32
 F32, BF16 = jnp.float32, jnp.bfloat16
-LARGE = pltpu.CompilerParams(vmem_limit_bytes=60 << 20)
+LARGE = pltpu.CompilerParams(vmem_limit_bytes=57 << 20)
 PARAMS = pltpu.CompilerParams(vmem_limit_bytes=24 << 20)
 
 
@@ -315,13 +315,13 @@
     leaving.finish()
 
 
-def key_grad_kernel(scale, keys_ref, values_ref, messages_ref, key_out, value_out, *refs):
-    state, wide, across, key_held, value_held, key_sems, value_sems = refs
+def key_grad_kernel(scale, rank_ref, keys_ref, values_ref, own_ref, got_ref, key_out, value_out, *refs):
+    state, sorted_ref, wide, across, key_held, value_held, key_sems, value_sems = refs
     blocks = spans(keys_ref.shape[1])
-    load_state(messages_ref, state)
-    rows = messages_ref[0].astype(F32)
+    sort_messages(rank_ref[0], (own_ref, got_ref), sorted_ref, state)
+    rows = sorted_ref[0]
     for part in range(1, PARTS):
-        rows = rows + messages_ref[part].astype(F32)
+        rows = rows + sorted_ref[part]
     row = lax.broadcasted_iota(jnp.int32, rows.shape, 0)
     total = jnp.sum(jnp.where(row >= ROWS, rows, 0.0), 0, keepdims=True)
     key_leaving = Leaving(key_held, key_out, key_sems)
@@ -334,11 +334,11 @@
         grad = dot(values_ref[:, low:high], across[i, : stop - start, : high - low], (1, 1)) + total[:, start:stop]
         alive = keys_ref[:, start:stop].astype(F32) > 0
         grad = jnp.where(alive, grad * scale, 0.0).astype(BF16)
-        key_leaving.put(start, stop, grad, last_of(i, len(blocks), 2))
+        key_leaving.put(start, stop, grad, last_of(i, len(blocks), 1))
     for i, (start, stop, low, high, _) in enumerate(blocks):
         feat = jnp.maximum(keys_ref[:, low:high], 0)
         grad = dot(feat, wide[i, : high - low, : stop - start], (1, 0))
-        value_leaving.put(start, stop, (grad * scale).astype(BF16), last_of(i, len(blocks), 3))
+        value_leaving.put(start, stop, (grad * scale).astype(BF16), last_of(i, len(blocks), 2))
     key_leaving.finish()
     value_leaving.finish()
 
@@ -440,7 +440,7 @@
     def halo(source):
         return lax.ppermute(source, "frame", [(i + 1, i) for i in range(devices - 1)])
 
-    early = tokens * 1 // 2 // 8 * 8
+    early = tokens * 40 // 100 // 8 * 8
     following = [halo(grad_out[:early])]
     key = pl.pallas_call(
         key_kernel,
@@ -495,17 +495,16 @@
     grad_queries = query_grad(rank, query_rows, numer, sides, *states)
     key_rows, value_rows = relay(saved_keys, saved_values)
     part = over_groups(added(grad_parts, total))
-    groups = [list(range(i, i + PARTS)) for i in range(0, devices, PARTS)]
-    grads = lax.all_gather(part, "frame", axis_index_groups=groups if len(groups) > 1 else None)
+    grads = gathered(part)
     grad_keys, grad_values = pl.pallas_call(
         functools.partial(key_grad_kernel, scale),
-        in_specs=[vmem] * 3,
+        in_specs=[smem] + [vmem] * 4,
         out_specs=[anywhere] * 2,
         out_shape=[array, array],
-        scratch_shapes=[state, wide, across, held, held, sems, sems],
+        scratch_shapes=[state, ordered, wide, across, held, held, sems, sems],
         compiler_params=PARAMS,
         cost_estimate=cost(size * 1024, 4 * size),
-    )(key_rows, value_rows, grads)
+    )(rank, key_rows, value_rows, *grads)
     return tuple(x.transpose(1, 0, 2) for x in (grad_queries, grad_keys, grad_values))
 
 

time: 89.8 us -> 91.3 us (1.017)
  blocking collectives: 10.1 us -> 0 us
  waiting for transfers between devices: 16.9 us -> 26.9 us
  starting transfers between devices: 26.9 us -> 30.6 us
  local copies, waits for them, and re-layouts: 7.23 us -> 5.72 us
    all_gather x1 -> x0, blocking collectives: 10.1 us -> none  [shards(): lax.all_gather(part, 'frame', axis_index_groups=groups if len(groups) > 1...]
    ppermute x18 -> x22, waiting for transfers between devices: 16.9 us -> 26.9 us  [exchange(): return lax.ppermute(block, axis, [(i, i ^ distance) for i in devices])]
    ppermute x18 -> x22, starting transfers between devices: 24.4 us -> 28 us  [exchange(): return lax.ppermute(block, axis, [(i, i ^ distance) for i in devices])]
    unnamed x12, local copies, waits for them, and re-layouts: 2.55 us -> 0.99 us
  transfers between devices with their start and end apart: 20 -> 24, of which waited for: 5 -> 11; matrix products, arithmetic and copies ran while one was open for 2% -> 2% of each run, Pallas kernels for 25% -> 25%
where the time goes in v5:
time: 91.3 us; the launch traced here: 91.1 us
  starting transfers between devices  30.6 us (34%)
  Pallas kernels  26.9 us (29%)
  waiting for transfers between devices  26.9 us (29%)
  local copies, waits for them, and re-layouts  5.72 us (6%)
  between operations  1.07 us (1%)
    ppermute x22, starting transfers between devices, exchange(): return lax.ppermute(block, axis, [(i, i ^ distance) for i in devices])  28 us
    ppermute x22, waiting for transfers between devices, exchange(): return lax.ppermute(block, axis, [(i, i ^ distance) for i in devices])  26.9 us
    pallas_call x2, Pallas kernels, relay(): pl.pallas_call(relay_kernel, in_specs=[anywhere] * len(sources), out_spec...  5.9 us
    pallas_call x1, Pallas kernels, shards(): pl.pallas_call(functools.partial(key_grad_kernel, scale), in_specs=[smem]...  4.37 us
    pallas_call x1, Pallas kernels, shards(): query(rank, query_rows, grad_rows, conv_taps, spread, *following)  4.28 us
    pallas_call x1, Pallas kernels, shards(): state_messages = key(rank, saved_keys, saved_values)  4.27 us
    pallas_call x1, Pallas kernels, shards(): grad_queries = query_grad(rank, query_rows, numer, sides, *states)  3.64 us
    slice x1, local copies, waits for them, and re-layouts, shards(): following.append(halo(grad_out[early:]))  3.29 us
  transfers between devices with their start and end apart: 24, of which 11 were waited for; matrix products, arithmetic and copies ran while one was open for 2% of the time, Pallas kernels for 25%

profile of v5, /device:TPU:0, one launch (start us, length us, event | category | flops | bytes accessed | tf_op | source)
XLA Modules:
  0.0 91.1 jit_solution(14984787396369220870)
XLA Ops:
  0.6 3.3 %slice.9 = bf16[132,2,2240]{2,1,0:T(2,128)(2,1)} slice(bf16[220,2,2240]{2,1,0:T(2,128)(2,1)} %bitcast.8), slice={[88:220], [0:2], [0:2240]} | slice | bytes 2365440 | tf_op jit(solution)/shard_map/slice | solution.py:455
  3.9 1.3 %collective-permute-start.8 = (bf16[132,2,2240]{2,1,0:T(2,128)(2,1)}, bf16[132,2,2240]{2,1,0:T(2,128)(2,1)S(1)}, u32[]{:S(2)}, u32[]{:S(2)}) collective-permute-start(bf16[132,2,2240]{2,1,0:T(2,128)(2,1)} %slice.9), channel_id=1, source_target_pairs={{4,0},{8,4},{12,8},{16,12},{20,16},{24,20},{28,24},{5,1},{9,5},{13... | collective-permute-start | bytes 3548168 | tf_op jit(solution)/shard_map/ppermute | solution.py:441
  5.2 1.4 %slice.8 = bf16[88,2,2240]{2,1,0:T(2,128)(2,1)} slice(bf16[220,2,2240]{2,1,0:T(2,128)(2,1)S(1)} %bitcast.9), slice={[0:88], [0:2], [0:2240]} | slice | bytes 1576960 | tf_op jit(solution)/shard_map/slice | solution.py:444
  6.7 1.3 %collective-permute-start.7 = (bf16[88,2,2240]{2,1,0:T(2,128)(2,1)}, bf16[88,2,2240]{2,1,0:T(2,128)(2,1)}, u32[]{:S(2)}, u32[]{:S(2)}) collective-permute-start(bf16[88,2,2240]{2,1,0:T(2,128)(2,1)} %slice.8), channel_id=1, source_target_pairs={{4,0},{8,4},{12,8},{16,12},{20,16},{24,20},{28,24},{5,1},{9,5},{13... | collective-permute-start | bytes 2365448 | tf_op jit(solution)/shard_map/ppermute | solution.py:441
  8.0 4.3 %shard_map.77 = (bf16[4,16,2240]{2,1,0:T(8,128)(2,1)}, bf16[4,16,2240]{2,1,0:T(8,128)(2,1)}) custom-call(s32[1]{0:T(128)} %bitcast.rank_ref, bf16[220,2,2240]{2,1,0:T(2,128)(2,1)} %bitcast.11, bf16[220,2,2240]{2,1,0:T(2,128)(2,1)} %bitcast.13), custom_call_target="tpu_custom_call" | custom-call | flops 1009254400 | bytes 3942400 | tf_op jit(solution)/shard_map/pallas_call | solution.py:454
  12.3 1.8 %collective-permute-start = (bf16[4,16,2240]{2,1,0:T(8,128)(2,1)}, bf16[4,16,2240]{2,1,0:T(8,128)(2,1)S(1)}, u32[]{:S(2)}, u32[]{:S(2)}) collective-permute-start(bf16[4,16,2240]{2,1,0:T(8,128)(2,1)} %get-tuple-element.29), channel_id=1, source_target_pairs={{0,4},{4,0},{8,12},{12,8},{16,20},{20,16},{24,28},{28,24},{1,5},{5... | collective-permute-start | bytes 860168 | tf_op jit(solution)/shard_map/ppermute | solution.py:352
  14.1 1.4 %collective-permute-done.got_ref = bf16[4,16,2240]{2,1,0:T(8,128)(2,1)S(1)} collective-permute-done((bf16[4,16,2240]{2,1,0:T(8,128)(2,1)}, bf16[4,16,2240]{2,1,0:T(8,128)(2,1)S(1)}, u32[]{:S(2)}, u32[]{:S(2)}) %collective-permute-start) | collective-permute-done | bytes 286752 | tf_op jit(solution)/shard_map/ppermute | solution.py:352
  16.6 3.0 %collective-permute-start.1 = (bf16[16,2240]{1,0:T(8,128)(2,1)S(1)}, bf16[16,2240]{1,0:T(8,128)(2,1)S(1)}, u32[]{:S(2)}, u32[]{:S(2)}) collective-permute-start(bf16[16,2240]{1,0:T(8,128)(2,1)S(1)} %get-tuple-element.31), channel_id=1, source_target_pairs={{0,8},{4,12},{8,0},{12,4},{16,24},{20,28},{24,16},{28,20},{1,9},{5... | collective-permute-start | bytes 215048 | tf_op jit(solution)/shard_map/ppermute | solution.py:352
  19.7 2.4 %collective-permute-start.2 = (bf16[16,2240]{1,0:T(8,128)(2,1)S(1)}, bf16[16,2240]{1,0:T(8,128)(2,1)S(1)}, u32[]{:S(2)}, u32[]{:S(2)}) collective-permute-start(bf16[16,2240]{1,0:T(8,128)(2,1)S(1)} %get-tuple-element.32), channel_id=1, source_target_pairs={{0,16},{4,20},{8,24},{12,28},{16,0},{20,4},{24,8},{28,12},{1,17},{... | collective-permute-start | bytes 215048 | tf_op jit(solution)/shard_map/ppermute | solution.py:352
  22.6 12.1 %collective-permute-done.1.refs_1_ = bf16[16,2240]{1,0:T(8,128)(2,1)S(1)} collective-permute-done((bf16[16,2240]{1,0:T(8,128)(2,1)S(1)}, bf16[16,2240]{1,0:T(8,128)(2,1)S(1)}, u32[]{:S(2)}, u32[]{:S(2)}) %collective-permute-start.1) | collective-permute-done | bytes 71712 | tf_op jit(solution)/shard_map/ppermute | solution.py:352
  34.6 1.7 %collective-permute-done.3.refs_3_ = bf16[16,2240]{1,0:T(8,128)(2,1)S(1)} collective-permute-done((bf16[16,2240]{1,0:T(8,128)(2,1)S(1)}, bf16[16,2240]{1,0:T(8,128)(2,1)S(1)}, u32[]{:S(2)}, u32[]{:S(2)}) %collective-permute-start.3) | collective-permute-done | bytes 71712 | tf_op jit(solution)/shard_map/ppermute | solution.py:352
  36.4 3.7 %collective-permute-start.6 = (bf16[16,2240]{1,0:T(8,128)(2,1)S(1)}, bf16[16,2240]{1,0:T(8,128)(2,1)S(1)}, u32[]{:S(2)}, u32[]{:S(2)}) collective-permute-start(bf16[16,2240]{1,0:T(8,128)(2,1)S(1)} %shard_map.79.refs_0_), channel_id=1, source_target_pairs={{0,3},{1,2},{2,1},{3,0},{4,7},{5,6},{6,5},{7,4},{8,11},{9,10},{10,... | collective-permute-start | bytes 215048 | tf_op jit(solution)/shard_map/ppermute | solution.py:352
  40.9 2.8 %shard_map.76 = (bf16[440,2240]{1,0:T(8,128)(2,1)S(1)}, bf16[440,2240]{1,0:T(8,128)(2,1)S(1)}) custom-call(bf16[220,2,2240]{2,1,0:T(2,128)(2,1)S(1)} %bitcast.15, bf16[220,2,2240]{2,1,0:T(2,128)(2,1)S(1)} %bitcast.10), custom_call_target="tpu_custom_call" | custom-call | bytes 7884800 | tf_op jit(solution)/shard_map/pallas_call | solution.py:430
  43.8 1.6 %collective-permute-done.5.refs_2_ = bf16[16,2240]{1,0:T(8,128)(2,1)S(1)} collective-permute-done((bf16[16,2240]{1,0:T(8,128)(2,1)S(1)}, bf16[16,2240]{1,0:T(8,128)(2,1)S(1)}, u32[]{:S(2)}, u32[]{:S(2)}) %collective-permute-start.5) | collective-permute-done | bytes 71712 | tf_op jit(solution)/shard_map/ppermute | solution.py:352
  45.4 1.1 %collective-permute-start.11 = (bf16[16,2240]{1,0:T(8,128)(2,1)S(1)}, bf16[16,2240]{1,0:T(8,128)(2,1)S(1)}, u32[]{:S(2)}, u32[]{:S(2)}) collective-permute-start(bf16[16,2240]{1,0:T(8,128)(2,1)S(1)} %shard_map.80.message_ref.refs_0_), channel_id=1, source_target_pairs={{0,24},{4,28},{8,16},{12,20},{16,8},{20,12},{24,0},{28,4},{1,25},{... | collective-permute-start | bytes 215048 | tf_op jit(solution)/shard_map/ppermute | solution.py:352
  46.6 2.3 %collective-permute-start.10 = (bf16[16,2240]{1,0:T(8,128)(2,1)S(1)}, bf16[16,2240]{1,0:T(8,128)(2,1)S(1)}, u32[]{:S(2)}, u32[]{:S(2)}) collective-permute-start(bf16[16,2240]{1,0:T(8,128)(2,1)S(1)} %shard_map.80.message_ref.refs_0_), channel_id=1, source_target_pairs={{0,16},{4,20},{8,24},{12,28},{16,0},{20,4},{24,8},{28,12},{1,17},{... | collective-permute-start | bytes 215048 | tf_op jit(solution)/shard_map/ppermute | solution.py:352
  49.8 4.3 %shard_map.82 = (bf16[440,2240]{1,0:T(8,128)(2,1)S(1)}, bf16[4,16,2240]{2,1,0:T(8,128)(2,1)S(1)}, bf16[4,16,2240]{2,1,0:T(8,128)(2,1)S(1)}) custom-call(s32[1]{0:T(128)} %bitcast.rank_ref, bf16[440,2240]{1,0:T(8,128)(2,1)S(1)} %get-tuple-element.26.queries_ref, bf16[440,2240]{1,0:T(8,128)(2,1)S(1)} %get-tuple-element.27.grad_ref, f32[3,2240]{1,0:T(4,128)S(1)} %copy-done.5, ...), custom_call_target="tpu_custom_call" | custom-call | flops 2018508800 | bytes 7884800 | tf_op jit(solution)/shard_map/pallas_call | solution.py:474
  54.8 1.0 %collective-permute-done.13.got_ref = bf16[4,16,2240]{2,1,0:T(8,128)(2,1)S(1)} collective-permute-done((bf16[4,16,2240]{2,1,0:T(8,128)(2,1)S(1)}, bf16[4,16,2240]{2,1,0:T(8,128)(2,1)S(1)}, u32[]{:S(2)}, u32[]{:S(2)}) %collective-permute-start.13) | collective-permute-done | bytes 286752 | tf_op jit(solution)/shard_map/ppermute | solution.py:352
  55.9 2.0 %collective-permute-start.14 = (bf16[16,2240]{1,0:T(8,128)(2,1)S(1)}, bf16[16,2240]{1,0:T(8,128)(2,1)S(1)}, u32[]{:S(2)}, u32[]{:S(2)}) collective-permute-start(bf16[16,2240]{1,0:T(8,128)(2,1)S(1)} %get-tuple-element.43), channel_id=1, source_target_pairs={{0,8},{4,12},{8,0},{12,4},{16,24},{20,28},{24,16},{28,20},{1,9},{5... | collective-permute-start | bytes 215048 | tf_op jit(solution)/shard_map/ppermute | solution.py:352
  57.9 1.6 %collective-permute-start.16 = (bf16[16,2240]{1,0:T(8,128)(2,1)S(1)}, bf16[16,2240]{1,0:T(8,128)(2,1)S(1)}, u32[]{:S(2)}, u32[]{:S(2)}) collective-permute-start(bf16[16,2240]{1,0:T(8,128)(2,1)S(1)} %get-tuple-element.45), channel_id=1, source_target_pairs={{0,24},{4,28},{8,16},{12,20},{16,8},{20,12},{24,0},{28,4},{1,25},{... | collective-permute-start | bytes 215048 | tf_op jit(solution)/shard_map/ppermute | solution.py:352
  59.5 3.0 %shard_map.84 = (bf16[440,128]{1,0:T(8,128)(2,1)S(1)}, f32[8,2240]{1,0:T(8,128)S(1)}) custom-call(s32[1]{0:T(128)} %bitcast.rank_ref, bf16[440,2240]{1,0:T(8,128)(2,1)S(1)} %get-tuple-element.26.queries_ref, bf16[440,2240]{1,0:T(8,128)(2,1)S(1)} %get-tuple-element.35.numer_ref, f32[440,128]{1,0:T(8,128)S(1)} %get-tuple-element.36.inverse_ref, ...), custom_call_target="tpu_custom_call" | custom-call | flops 1009254400 | bytes 3942400 | tf_op jit(solution)/shard_map/pallas_call | solution.py:485
  62.5 1.2 %collective-permute-done.15.refs_2_ = bf16[16,2240]{1,0:T(8,128)(2,1)S(1)} collective-permute-done((bf16[16,2240]{1,0:T(8,128)(2,1)S(1)}, bf16[16,2240]{1,0:T(8,128)(2,1)S(1)}, u32[]{:S(2)}, u32[]{:S(2)}) %collective-permute-start.15) | collective-permute-done | bytes 71712 | tf_op jit(solution)/shard_map/ppermute | solution.py:352
  63.7 2.6 %collective-permute-start.19 = (bf16[16,2240]{1,0:T(8,128)(2,1)S(1)}, bf16[16,2240]{1,0:T(8,128)(2,1)S(1)}, u32[]{:S(2)}, u32[]{:S(2)}) collective-permute-start(bf16[16,2240]{1,0:T(8,128)(2,1)S(1)} %shard_map.88.refs_0_), channel_id=1, source_target_pairs={{0,3},{1,2},{2,1},{3,0},{4,7},{5,6},{6,5},{7,4},{8,11},{9,10},{10,... | collective-permute-start | bytes 215048 | tf_op jit(solution)/shard_map/ppermute | solution.py:352
  66.3 1.8 %collective-permute-start.17 = (bf16[16,2240]{1,0:T(8,128)(2,1)S(1)}, bf16[16,2240]{1,0:T(8,128)(2,1)S(1)}, u32[]{:S(2)}, u32[]{:S(2)}) collective-permute-start(bf16[16,2240]{1,0:T(8,128)(2,1)S(1)} %shard_map.88.refs_0_), channel_id=1, source_target_pairs={{0,1},{1,0},{2,3},{3,2},{4,5},{5,4},{6,7},{7,6},{8,9},{9,8},{10,11... | collective-permute-start | bytes 215048 | tf_op jit(solution)/shard_map/ppermute | solution.py:352
  68.2 2.5 %collective-permute-done.19.refs_3_ = bf16[16,2240]{1,0:T(8,128)(2,1)S(1)} collective-permute-done((bf16[16,2240]{1,0:T(8,128)(2,1)S(1)}, bf16[16,2240]{1,0:T(8,128)(2,1)S(1)}, u32[]{:S(2)}, u32[]{:S(2)}) %collective-permute-start.19) | collective-permute-done | bytes 71712 | tf_op jit(solution)/shard_map/ppermute | solution.py:352
  70.7 1.6 %collective-permute-done.18.refs_2_ = bf16[16,2240]{1,0:T(8,128)(2,1)S(1)} collective-permute-done((bf16[16,2240]{1,0:T(8,128)(2,1)S(1)}, bf16[16,2240]{1,0:T(8,128)(2,1)S(1)}, u32[]{:S(2)}, u32[]{:S(2)}) %collective-permute-start.18) | collective-permute-done | bytes 71712 | tf_op jit(solution)/shard_map/ppermute | solution.py:352
  72.4 1.6 %collective-permute-start.22 = (bf16[16,2240]{1,0:T(8,128)(2,1)S(1)}, bf16[16,2240]{1,0:T(8,128)(2,1)S(1)}, u32[]{:S(2)}, u32[]{:S(2)}) collective-permute-start(bf16[16,2240]{1,0:T(8,128)(2,1)S(1)} %shard_map.89.refs_0_), channel_id=1, source_target_pairs={{0,24},{4,28},{8,16},{12,20},{16,8},{20,12},{24,0},{28,4},{1,25},{... | collective-permute-start | bytes 215048 | tf_op jit(solution)/shard_map/ppermute | solution.py:352
  74.0 1.4 %collective-permute-start.21 = (bf16[16,2240]{1,0:T(8,128)(2,1)S(1)}, bf16[16,2240]{1,0:T(8,128)(2,1)S(1)}, u32[]{:S(2)}, u32[]{:S(2)}) collective-permute-start(bf16[16,2240]{1,0:T(8,128)(2,1)S(1)} %shard_map.89.refs_0_), channel_id=1, source_target_pairs={{0,16},{4,20},{8,24},{12,28},{16,0},{20,4},{24,8},{28,12},{1,17},{... | collective-permute-start | bytes 215048 | tf_op jit(solution)/shard_map/ppermute | solution.py:352
  75.9 2.5 %collective-permute-done.22.refs_3_ = bf16[16,2240]{1,0:T(8,128)(2,1)S(1)} collective-permute-done((bf16[16,2240]{1,0:T(8,128)(2,1)S(1)}, bf16[16,2240]{1,0:T(8,128)(2,1)S(1)}, u32[]{:S(2)}, u32[]{:S(2)}) %collective-permute-start.22) | collective-permute-done | bytes 71712 | tf_op jit(solution)/shard_map/ppermute | solution.py:352
  79.8 3.1 %shard_map.86 = (bf16[440,2240]{1,0:T(8,128)(2,1)S(1)}, bf16[440,2240]{1,0:T(8,128)(2,1)S(1)}) custom-call(bf16[220,2,2240]{2,1,0:T(2,128)(2,1)S(1)} %bitcast.12, bf16[220,2,2240]{2,1,0:T(2,128)(2,1)S(1)} %bitcast.14), custom_call_target="tpu_custom_call" | custom-call | bytes 7884800 | tf_op jit(solution)/shard_map/pallas_call | solution.py:430
  82.9 3.6 %shard_map.85 = bf16[220,2,2240]{2,1,0:T(2,128)(2,1)} custom-call(s32[1]{0:T(128)} %bitcast.rank_ref, bf16[440,2240]{1,0:T(8,128)(2,1)S(1)} %get-tuple-element.26.queries_ref, bf16[440,2240]{1,0:T(8,128)(2,1)S(1)} %get-tuple-element.35.numer_ref, bf16[440,128]{1,0:T(8,128)(2,1)S(1)} %get-tuple-element.37.sides_ref, ...), custom_call_target="tpu_custom_call" | custom-call | flops 1009254400 | bytes 5913600 | tf_op jit(solution)/shard_map/pallas_call | solution.py:495
  86.6 4.4 %shard_map.91 = (bf16[220,2,2240]{2,1,0:T(2,128)(2,1)}, bf16[220,2,2240]{2,1,0:T(2,128)(2,1)}) custom-call(s32[1]{0:T(128)} %bitcast.rank_ref, bf16[440,2240]{1,0:T(8,128)(2,1)S(1)} %get-tuple-element.38.keys_ref, bf16[440,2240]{1,0:T(8,128)(2,1)S(1)} %get-tuple-element.39.values_ref, bf16[4,16,2240]{2,1,0:T(8,128)(2,1)S(1)} %shard_map.90.own_ref, ...), custom_call_target="tpu_custom_call" | custom-call | flops 2018508800 | bytes 7884800 | tf_op jit(solution)/shard_map/pallas_call | solution.py:499
  (46 shorter events, 6.4 us)
Async XLA Ops:
  0.6 4.6 %copy-start = (bf16[2,220,2240]{2,0,1:T(2,128)(2,1)S(1)}, bf16[2,220,2240]{2,0,1:T(2,128)(2,1)}, u32[]{:S(2)}) copy-start(bf16[2,220,2240]{2,0,1:T(2,128)(2,1)} %param.5) | copy-start | bytes 5913604
  3.9 45.9 %collective-permute-start.8 = (bf16[132,2,2240]{2,1,0:T(2,128)(2,1)}, bf16[132,2,2240]{2,1,0:T(2,128)(2,1)S(1)}, u32[]{:S(2)}, u32[]{:S(2)}) collective-permute-start(bf16[132,2,2240]{2,1,0:T(2,128)(2,1)} %slice.9), channel_id=1, source_target_pairs={{4,0},{8,4},{12,8},{16,12},{20,16},{24,20},{28,24},{5,1},{9,5},{13... | collective-permute-start | bytes 3548168 | tf_op jit(solution)/shard_map/ppermute | solution.py:441
  6.7 43.1 %collective-permute-start.7 = (bf16[88,2,2240]{2,1,0:T(2,128)(2,1)}, bf16[88,2,2240]{2,1,0:T(2,128)(2,1)}, u32[]{:S(2)}, u32[]{:S(2)}) collective-permute-start(bf16[88,2,2240]{2,1,0:T(2,128)(2,1)} %slice.8), channel_id=1, source_target_pairs={{4,0},{8,4},{12,8},{16,12},{20,16},{24,20},{28,24},{5,1},{9,5},{13... | collective-permute-start | bytes 2365448 | tf_op jit(solution)/shard_map/ppermute | solution.py:441
  8.0 32.9 %copy-start.3 = (bf16[2,220,2240]{2,0,1:T(2,128)(2,1)S(1)}, bf16[2,220,2240]{2,0,1:T(2,128)(2,1)}, u32[]{:S(2)}) copy-start(bf16[2,220,2240]{2,0,1:T(2,128)(2,1)} %param.7) | copy-start | bytes 5913604
  12.3 3.2 %collective-permute-start = (bf16[4,16,2240]{2,1,0:T(8,128)(2,1)}, bf16[4,16,2240]{2,1,0:T(8,128)(2,1)S(1)}, u32[]{:S(2)}, u32[]{:S(2)}) collective-permute-start(bf16[4,16,2240]{2,1,0:T(8,128)(2,1)} %get-tuple-element.29), channel_id=1, source_target_pairs={{0,4},{4,0},{8,12},{12,8},{16,20},{20,16},{24,28},{28,24},{1,5},{5... | collective-permute-start | bytes 860168 | tf_op jit(solution)/shard_map/ppermute | solution.py:352
  15.5 1.0 %copy-start.4 = (bf16[4,16,2240]{2,1,0:T(8,128)(2,1)S(1)}, bf16[4,16,2240]{2,1,0:T(8,128)(2,1)}, u32[]{:S(2)}) copy-start(bf16[4,16,2240]{2,1,0:T(8,128)(2,1)} %get-tuple-element.28.own_ref) | copy-start | bytes 860164
  16.6 18.0 %collective-permute-start.1 = (bf16[16,2240]{1,0:T(8,128)(2,1)S(1)}, bf16[16,2240]{1,0:T(8,128)(2,1)S(1)}, u32[]{:S(2)}, u32[]{:S(2)}) collective-permute-start(bf16[16,2240]{1,0:T(8,128)(2,1)S(1)} %get-tuple-element.31), channel_id=1, source_target_pairs={{0,8},{4,12},{8,0},{12,4},{16,24},{20,28},{24,16},{28,20},{1,9},{5... | collective-permute-start | bytes 215048 | tf_op jit(solution)/shard_map/ppermute | solution.py:352
  19.7 15.0 %collective-permute-start.2 = (bf16[16,2240]{1,0:T(8,128)(2,1)S(1)}, bf16[16,2240]{1,0:T(8,128)(2,1)S(1)}, u32[]{:S(2)}, u32[]{:S(2)}) collective-permute-start(bf16[16,2240]{1,0:T(8,128)(2,1)S(1)} %get-tuple-element.32), channel_id=1, source_target_pairs={{0,16},{4,20},{8,24},{12,28},{16,0},{20,4},{24,8},{28,12},{1,17},{... | collective-permute-start | bytes 215048 | tf_op jit(solution)/shard_map/ppermute | solution.py:352
  22.1 14.3 %collective-permute-start.3 = (bf16[16,2240]{1,0:T(8,128)(2,1)S(1)}, bf16[16,2240]{1,0:T(8,128)(2,1)S(1)}, u32[]{:S(2)}, u32[]{:S(2)}) collective-permute-start(bf16[16,2240]{1,0:T(8,128)(2,1)S(1)} %get-tuple-element.33), channel_id=1, source_target_pairs={{0,24},{4,28},{8,16},{12,20},{16,8},{20,12},{24,0},{28,4},{1,25},{... | collective-permute-start | bytes 215048 | tf_op jit(solution)/shard_map/ppermute | solution.py:352
  36.4 7.3 %collective-permute-start.6 = (bf16[16,2240]{1,0:T(8,128)(2,1)S(1)}, bf16[16,2240]{1,0:T(8,128)(2,1)S(1)}, u32[]{:S(2)}, u32[]{:S(2)}) collective-permute-start(bf16[16,2240]{1,0:T(8,128)(2,1)S(1)} %shard_map.79.refs_0_), channel_id=1, source_target_pairs={{0,3},{1,2},{2,1},{3,0},{4,7},{5,6},{6,5},{7,4},{8,11},{9,10},{10,... | collective-permute-start | bytes 215048 | tf_op jit(solution)/shard_map/ppermute | solution.py:352
  40.1 5.3 %collective-permute-start.5 = (bf16[16,2240]{1,0:T(8,128)(2,1)S(1)}, bf16[16,2240]{1,0:T(8,128)(2,1)S(1)}, u32[]{:S(2)}, u32[]{:S(2)}) collective-permute-start(bf16[16,2240]{1,0:T(8,128)(2,1)S(1)} %shard_map.79.refs_0_), channel_id=1, source_target_pairs={{0,2},{1,3},{2,0},{3,1},{4,6},{5,7},{6,4},{7,5},{8,10},{9,11},{10,... | collective-permute-start | bytes 215048 | tf_op jit(solution)/shard_map/ppermute | solution.py:352
  40.1 5.3 %collective-permute-start.4 = (bf16[16,2240]{1,0:T(8,128)(2,1)S(1)}, bf16[16,2240]{1,0:T(8,128)(2,1)S(1)}, u32[]{:S(2)}, u32[]{:S(2)}) collective-permute-start(bf16[16,2240]{1,0:T(8,128)(2,1)S(1)} %shard_map.79.refs_0_), channel_id=1, source_target_pairs={{0,1},{1,0},{2,3},{3,2},{4,5},{5,4},{6,7},{7,6},{8,9},{9,8},{10,11... | collective-permute-start | bytes 215048 | tf_op jit(solution)/shard_map/ppermute | solution.py:352
  43.7 6.1 %copy-start.5 = (f32[3,2240]{1,0:T(4,128)S(1)}, f32[3,2240]{1,0:T(4,128)}, u32[]{:S(2)}) copy-start(f32[3,2240]{1,0:T(4,128)} %taps_ref.1) | copy-start | bytes 80644
  45.4 8.8 %collective-permute-start.11 = (bf16[16,2240]{1,0:T(8,128)(2,1)S(1)}, bf16[16,2240]{1,0:T(8,128)(2,1)S(1)}, u32[]{:S(2)}, u32[]{:S(2)}) collective-permute-start(bf16[16,2240]{1,0:T(8,128)(2,1)S(1)} %shard_map.80.message_ref.refs_0_), channel_id=1, source_target_pairs={{0,24},{4,28},{8,16},{12,20},{16,8},{20,12},{24,0},{28,4},{1,25},{... | collective-permute-start | bytes 215048 | tf_op jit(solution)/shard_map/ppermute | solution.py:352
  46.6 7.6 %collective-permute-start.10 = (bf16[16,2240]{1,0:T(8,128)(2,1)S(1)}, bf16[16,2240]{1,0:T(8,128)(2,1)S(1)}, u32[]{:S(2)}, u32[]{:S(2)}) collective-permute-start(bf16[16,2240]{1,0:T(8,128)(2,1)S(1)} %shard_map.80.message_ref.refs_0_), channel_id=1, source_target_pairs={{0,16},{4,20},{8,24},{12,28},{16,0},{20,4},{24,8},{28,12},{1,17},{... | collective-permute-start | bytes 215048 | tf_op jit(solution)/shard_map/ppermute | solution.py:352
  48.9 5.3 %collective-permute-start.9 = (bf16[16,2240]{1,0:T(8,128)(2,1)S(1)}, bf16[16,2240]{1,0:T(8,128)(2,1)S(1)}, u32[]{:S(2)}, u32[]{:S(2)}) collective-permute-start(bf16[16,2240]{1,0:T(8,128)(2,1)S(1)} %shard_map.80.message_ref.refs_0_), channel_id=1, source_target_pairs={{0,8},{4,12},{8,0},{12,4},{16,24},{20,28},{24,16},{28,20},{1,9},{5... | collective-permute-start | bytes 215048 | tf_op jit(solution)/shard_map/ppermute | solution.py:352
  54.1 1.6 %collective-permute-start.13 = (bf16[4,16,2240]{2,1,0:T(8,128)(2,1)S(1)}, bf16[4,16,2240]{2,1,0:T(8,128)(2,1)S(1)}, u32[]{:S(2)}, u32[]{:S(2)}) collective-permute-start(bf16[4,16,2240]{2,1,0:T(8,128)(2,1)S(1)} %get-tuple-element.41), channel_id=1, source_target_pairs={{0,4},{4,0},{8,12},{12,8},{16,20},{20,16},{24,28},{28,24},{1,5},{5... | collective-permute-start | bytes 860168 | tf_op jit(solution)/shard_map/ppermute | solution.py:352
  54.3 5.2 %collective-permute-start.12 = (bf16[4,16,2240]{2,1,0:T(8,128)(2,1)S(1)}, bf16[4,16,2240]{2,1,0:T(8,128)(2,1)S(1)}, u32[]{:S(2)}, u32[]{:S(2)}) collective-permute-start(bf16[4,16,2240]{2,1,0:T(8,128)(2,1)S(1)} %shard_map.83.refs_0_), channel_id=1, source_target_pairs={{0,4},{4,0},{8,12},{12,8},{16,20},{20,16},{24,28},{28,24},{1,5},{5... | collective-permute-start | bytes 860168 | tf_op jit(solution)/shard_map/ppermute | solution.py:352
  55.9 6.5 %collective-permute-start.14 = (bf16[16,2240]{1,0:T(8,128)(2,1)S(1)}, bf16[16,2240]{1,0:T(8,128)(2,1)S(1)}, u32[]{:S(2)}, u32[]{:S(2)}) collective-permute-start(bf16[16,2240]{1,0:T(8,128)(2,1)S(1)} %get-tuple-element.43), channel_id=1, source_target_pairs={{0,8},{4,12},{8,0},{12,4},{16,24},{20,28},{24,16},{28,20},{1,9},{5... | collective-permute-start | bytes 215048 | tf_op jit(solution)/shard_map/ppermute | solution.py:352
  57.9 5.7 %collective-permute-start.15 = (bf16[16,2240]{1,0:T(8,128)(2,1)S(1)}, bf16[16,2240]{1,0:T(8,128)(2,1)S(1)}, u32[]{:S(2)}, u32[]{:S(2)}) collective-permute-start(bf16[16,2240]{1,0:T(8,128)(2,1)S(1)} %get-tuple-element.44), channel_id=1, source_target_pairs={{0,16},{4,20},{8,24},{12,28},{16,0},{20,4},{24,8},{28,12},{1,17},{... | collective-permute-start | bytes 215048 | tf_op jit(solution)/shard_map/ppermute | solution.py:352
  57.9 5.7 %collective-permute-start.16 = (bf16[16,2240]{1,0:T(8,128)(2,1)S(1)}, bf16[16,2240]{1,0:T(8,128)(2,1)S(1)}, u32[]{:S(2)}, u32[]{:S(2)}) collective-permute-start(bf16[16,2240]{1,0:T(8,128)(2,1)S(1)} %get-tuple-element.45), channel_id=1, source_target_pairs={{0,24},{4,28},{8,16},{12,20},{16,8},{20,12},{24,0},{28,4},{1,25},{... | collective-permute-start | bytes 215048 | tf_op jit(solution)/shard_map/ppermute | solution.py:352
  59.5 20.3 %copy-start.1 = (bf16[2,220,2240]{2,0,1:T(2,128)(2,1)S(1)}, bf16[2,220,2240]{2,0,1:T(2,128)(2,1)}, u32[]{:S(2)}) copy-start(bf16[2,220,2240]{2,0,1:T(2,128)(2,1)} %param.8) | copy-start | bytes 5913604
  59.5 20.3 %copy-start.2 = (bf16[2,220,2240]{2,0,1:T(2,128)(2,1)S(1)}, bf16[2,220,2240]{2,0,1:T(2,128)(2,1)}, u32[]{:S(2)}) copy-start(bf16[2,220,2240]{2,0,1:T(2,128)(2,1)} %param.9) | copy-start | bytes 5913604
  63.7 7.0 %collective-permute-start.19 = (bf16[16,2240]{1,0:T(8,128)(2,1)S(1)}, bf16[16,2240]{1,0:T(8,128)(2,1)S(1)}, u32[]{:S(2)}, u32[]{:S(2)}) collective-permute-start(bf16[16,2240]{1,0:T(8,128)(2,1)S(1)} %shard_map.88.refs_0_), channel_id=1, source_target_pairs={{0,3},{1,2},{2,1},{3,0},{4,7},{5,6},{6,5},{7,4},{8,11},{9,10},{10,... | collective-permute-start | bytes 215048 | tf_op jit(solution)/shard_map/ppermute | solution.py:352
  66.3 6.0 %collective-permute-start.18 = (bf16[16,2240]{1,0:T(8,128)(2,1)S(1)}, bf16[16,2240]{1,0:T(8,128)(2,1)S(1)}, u32[]{:S(2)}, u32[]{:S(2)}) collective-permute-start(bf16[16,2240]{1,0:T(8,128)(2,1)S(1)} %shard_map.88.refs_0_), channel_id=1, source_target_pairs={{0,2},{1,3},{2,0},{3,1},{4,6},{5,7},{6,4},{7,5},{8,10},{9,11},{10,... | collective-permute-start | bytes 215048 | tf_op jit(solution)/shard_map/ppermute | solution.py:352
  66.3 6.0 %collective-permute-start.17 = (bf16[16,2240]{1,0:T(8,128)(2,1)S(1)}, bf16[16,2240]{1,0:T(8,128)(2,1)S(1)}, u32[]{:S(2)}, u32[]{:S(2)}) collective-permute-start(bf16[16,2240]{1,0:T(8,128)(2,1)S(1)} %shard_map.88.refs_0_), channel_id=1, source_target_pairs={{0,1},{1,0},{2,3},{3,2},{4,5},{5,4},{6,7},{7,6},{8,9},{9,8},{10,11... | collective-permute-start | bytes 215048 | tf_op jit(solution)/shard_map/ppermute | solution.py:352
  72.4 6.1 %collective-permute-start.22 = (bf16[16,2240]{1,0:T(8,128)(2,1)S(1)}, bf16[16,2240]{1,0:T(8,128)(2,1)S(1)}, u32[]{:S(2)}, u32[]{:S(2)}) collective-permute-start(bf16[16,2240]{1,0:T(8,128)(2,1)S(1)} %shard_map.89.refs_0_), channel_id=1, source_target_pairs={{0,24},{4,28},{8,16},{12,20},{16,8},{20,12},{24,0},{28,4},{1,25},{... | collective-permute-start | bytes 215048 | tf_op jit(solution)/shard_map/ppermute | solution.py:352
  74.0 4.8 %collective-permute-start.21 = (bf16[16,2240]{1,0:T(8,128)(2,1)S(1)}, bf16[16,2240]{1,0:T(8,128)(2,1)S(1)}, u32[]{:S(2)}, u32[]{:S(2)}) collective-permute-start(bf16[16,2240]{1,0:T(8,128)(2,1)S(1)} %shard_map.89.refs_0_), channel_id=1, source_target_pairs={{0,16},{4,20},{8,24},{12,28},{16,0},{20,4},{24,8},{28,12},{1,17},{... | collective-permute-start | bytes 215048 | tf_op jit(solution)/shard_map/ppermute | solution.py:352
  75.4 4.4 %collective-permute-start.20 = (bf16[16,2240]{1,0:T(8,128)(2,1)S(1)}, bf16[16,2240]{1,0:T(8,128)(2,1)S(1)}, u32[]{:S(2)}, u32[]{:S(2)}) collective-permute-start(bf16[16,2240]{1,0:T(8,128)(2,1)S(1)} %shard_map.89.refs_0_), channel_id=1, source_target_pairs={{0,8},{4,12},{8,0},{12,4},{16,24},{20,28},{24,16},{28,20},{1,9},{5... | collective-permute-start | bytes 215048 | tf_op jit(solution)/shard_map/ppermute | solution.py:352
  79.7 6.8 %collective-permute-start.23 = (bf16[4,16,2240]{2,1,0:T(8,128)(2,1)S(1)}, bf16[4,16,2240]{2,1,0:T(8,128)(2,1)S(1)}, u32[]{:S(2)}, u32[]{:S(2)}) collective-permute-start(bf16[4,16,2240]{2,1,0:T(8,128)(2,1)S(1)} %shard_map.90.own_ref), channel_id=1, source_target_pairs={{0,4},{4,0},{8,12},{12,8},{16,20},{20,16},{24,28},{28,24},{1,5},{5... | collective-permute-start | bytes 860168 | tf_op jit(solution)/shard_map/ppermute | solution.py:352

commit v6 on v5

--- a/solution.py
+++ b/solution.py
@@ -231,7 +231,7 @@
     taps = [taps[0:1] + 1.0, taps[1:2], taps[2:3]]
     state[...] = jnp.zeros_like(state)
     group = 8 if 8 % frames == 0 and rows % 8 == 0 else rows
-    cuts, arrivals = sorted({0, 1, min(4, len(blocks)), len(blocks)}), {}
+    cuts, arrivals = sorted({0, min(2, len(blocks)), len(blocks)}), {}
     for k, (begin, end) in enumerate(zip(cuts, cuts[1:])):
         columns, first = slice(blocks[begin][0], blocks[end - 1][1]), 0
         arrivals[begin] = []
@@ -311,7 +311,7 @@
         grad = dot(numer_ref[:, low:high], across[i, : stop - start, : high - low], (1, 1))
         grad += dot(sides_ref[...], tot, (1, 0))
         grad = jnp.where(queries_ref[:, start:stop].astype(F32) > 0, grad * scale, 0.0).astype(BF16)
-        leaving.put(start, stop, grad, last_of(i, len(blocks), 3))
+        leaving.put(start, stop, grad, last_of(i, len(blocks), 2))
     leaving.finish()
 
 
@@ -338,7 +338,7 @@
     for i, (start, stop, low, high, _) in enumerate(blocks):
         feat = jnp.maximum(keys_ref[:, low:high], 0)
         grad = dot(feat, wide[i, : high - low, : stop - start], (1, 0))
-        value_leaving.put(start, stop, (grad * scale).astype(BF16), last_of(i, len(blocks), 2))
+        value_leaving.put(start, stop, (grad * scale).astype(BF16), i in (len(blocks) * 2 // 3, len(blocks) - 1))
     key_leaving.finish()
     value_leaving.finish()
 

time: 91.3 us -> 90.9 us (level)
  transfers between devices with their start and end apart: 24 -> 24, of which waited for: 11 -> 11; matrix products, arithmetic and copies ran while one was open for 2% -> 2% of each run, Pallas kernels for 25% -> 24%
where the time goes in v6:
time: 90.9 us; the launch traced here: 90.6 us
  starting transfers between devices  30.6 us (34%)
  waiting for transfers between devices  26.9 us (30%)
  Pallas kernels  26.4 us (29%)
  local copies, waits for them, and re-layouts  5.72 us (6%)
  between operations  1.07 us (1%)
    ppermute x22, starting transfers between devices, exchange(): return lax.ppermute(block, axis, [(i, i ^ distance) for i in devices])  28 us
    ppermute x22, waiting for transfers between devices, exchange(): return lax.ppermute(block, axis, [(i, i ^ distance) for i in devices])  26.9 us
    pallas_call x2, Pallas kernels, relay(): pl.pallas_call(relay_kernel, in_specs=[anywhere] * len(sources), out_spec...  5.9 us
    pallas_call x1, Pallas kernels, shards(): pl.pallas_call(functools.partial(key_grad_kernel, scale), in_specs=[smem]...  4.33 us
    pallas_call x1, Pallas kernels, shards(): state_messages = key(rank, saved_keys, saved_values)  4.27 us
    pallas_call x1, Pallas kernels, shards(): query(rank, query_rows, grad_rows, conv_taps, spread, *following)  4.27 us
    slice x1, local copies, waits for them, and re-layouts, shards(): following.append(halo(grad_out[early:]))  3.29 us
    pallas_call x1, Pallas kernels, shards(): grad_queries = query_grad(rank, query_rows, numer, sides, *states)  3.21 us
  transfers between devices with their start and end apart: 24, of which 11 were waited for; matrix products, arithmetic and copies ran while one was open for 2% of the time, Pallas kernels for 24%

profile of v6, /device:TPU:0, one launch (start us, length us, event | category | flops | bytes accessed | tf_op | source)
XLA Modules:
  0.0 90.6 jit_solution(13941680106573215679)
XLA Ops:
  0.6 3.3 %slice.9 = bf16[132,2,2240]{2,1,0:T(2,128)(2,1)} slice(bf16[220,2,2240]{2,1,0:T(2,128)(2,1)} %bitcast.8), slice={[88:220], [0:2], [0:2240]} | slice | bytes 2365440 | tf_op jit(solution)/shard_map/slice | solution.py:455
  3.9 1.3 %collective-permute-start.8 = (bf16[132,2,2240]{2,1,0:T(2,128)(2,1)}, bf16[132,2,2240]{2,1,0:T(2,128)(2,1)S(1)}, u32[]{:S(2)}, u32[]{:S(2)}) collective-permute-start(bf16[132,2,2240]{2,1,0:T(2,128)(2,1)} %slice.9), channel_id=1, source_target_pairs={{4,0},{8,4},{12,8},{16,12},{20,16},{24,20},{28,24},{5,1},{9,5},{13... | collective-permute-start | bytes 3548168 | tf_op jit(solution)/shard_map/ppermute | solution.py:441
  5.2 1.4 %slice.8 = bf16[88,2,2240]{2,1,0:T(2,128)(2,1)} slice(bf16[220,2,2240]{2,1,0:T(2,128)(2,1)S(1)} %bitcast.9), slice={[0:88], [0:2], [0:2240]} | slice | bytes 1576960 | tf_op jit(solution)/shard_map/slice | solution.py:444
  6.7 1.3 %collective-permute-start.7 = (bf16[88,2,2240]{2,1,0:T(2,128)(2,1)}, bf16[88,2,2240]{2,1,0:T(2,128)(2,1)}, u32[]{:S(2)}, u32[]{:S(2)}) collective-permute-start(bf16[88,2,2240]{2,1,0:T(2,128)(2,1)} %slice.8), channel_id=1, source_target_pairs={{4,0},{8,4},{12,8},{16,12},{20,16},{24,20},{28,24},{5,1},{9,5},{13... | collective-permute-start | bytes 2365448 | tf_op jit(solution)/shard_map/ppermute | solution.py:441
  8.0 4.3 %shard_map.77 = (bf16[4,16,2240]{2,1,0:T(8,128)(2,1)}, bf16[4,16,2240]{2,1,0:T(8,128)(2,1)}) custom-call(s32[1]{0:T(128)} %bitcast.rank_ref, bf16[220,2,2240]{2,1,0:T(2,128)(2,1)} %bitcast.11, bf16[220,2,2240]{2,1,0:T(2,128)(2,1)} %bitcast.13), custom_call_target="tpu_custom_call" | custom-call | flops 1009254400 | bytes 3942400 | tf_op jit(solution)/shard_map/pallas_call | solution.py:454
  12.3 1.8 %collective-permute-start = (bf16[4,16,2240]{2,1,0:T(8,128)(2,1)}, bf16[4,16,2240]{2,1,0:T(8,128)(2,1)S(1)}, u32[]{:S(2)}, u32[]{:S(2)}) collective-permute-start(bf16[4,16,2240]{2,1,0:T(8,128)(2,1)} %get-tuple-element.29), channel_id=1, source_target_pairs={{0,4},{4,0},{8,12},{12,8},{16,20},{20,16},{24,28},{28,24},{1,5},{5... | collective-permute-start | bytes 860168 | tf_op jit(solution)/shard_map/ppermute | solution.py:352
  14.1 1.4 %collective-permute-done.got_ref = bf16[4,16,2240]{2,1,0:T(8,128)(2,1)S(1)} collective-permute-done((bf16[4,16,2240]{2,1,0:T(8,128)(2,1)}, bf16[4,16,2240]{2,1,0:T(8,128)(2,1)S(1)}, u32[]{:S(2)}, u32[]{:S(2)}) %collective-permute-start) | collective-permute-done | bytes 286752 | tf_op jit(solution)/shard_map/ppermute | solution.py:352
  16.6 3.0 %collective-permute-start.1 = (bf16[16,2240]{1,0:T(8,128)(2,1)S(1)}, bf16[16,2240]{1,0:T(8,128)(2,1)S(1)}, u32[]{:S(2)}, u32[]{:S(2)}) collective-permute-start(bf16[16,2240]{1,0:T(8,128)(2,1)S(1)} %get-tuple-element.31), channel_id=1, source_target_pairs={{0,8},{4,12},{8,0},{12,4},{16,24},{20,28},{24,16},{28,20},{1,9},{5... | collective-permute-start | bytes 215048 | tf_op jit(solution)/shard_map/ppermute | solution.py:352
  19.7 2.4 %collective-permute-start.2 = (bf16[16,2240]{1,0:T(8,128)(2,1)S(1)}, bf16[16,2240]{1,0:T(8,128)(2,1)S(1)}, u32[]{:S(2)}, u32[]{:S(2)}) collective-permute-start(bf16[16,2240]{1,0:T(8,128)(2,1)S(1)} %get-tuple-element.32), channel_id=1, source_target_pairs={{0,16},{4,20},{8,24},{12,28},{16,0},{20,4},{24,8},{28,12},{1,17},{... | collective-permute-start | bytes 215048 | tf_op jit(solution)/shard_map/ppermute | solution.py:352
  22.6 12.1 %collective-permute-done.1.refs_1_ = bf16[16,2240]{1,0:T(8,128)(2,1)S(1)} collective-permute-done((bf16[16,2240]{1,0:T(8,128)(2,1)S(1)}, bf16[16,2240]{1,0:T(8,128)(2,1)S(1)}, u32[]{:S(2)}, u32[]{:S(2)}) %collective-permute-start.1) | collective-permute-done | bytes 71712 | tf_op jit(solution)/shard_map/ppermute | solution.py:352
  34.6 1.7 %collective-permute-done.3.refs_3_ = bf16[16,2240]{1,0:T(8,128)(2,1)S(1)} collective-permute-done((bf16[16,2240]{1,0:T(8,128)(2,1)S(1)}, bf16[16,2240]{1,0:T(8,128)(2,1)S(1)}, u32[]{:S(2)}, u32[]{:S(2)}) %collective-permute-start.3) | collective-permute-done | bytes 71712 | tf_op jit(solution)/shard_map/ppermute | solution.py:352
  36.4 3.7 %collective-permute-start.6 = (bf16[16,2240]{1,0:T(8,128)(2,1)S(1)}, bf16[16,2240]{1,0:T(8,128)(2,1)S(1)}, u32[]{:S(2)}, u32[]{:S(2)}) collective-permute-start(bf16[16,2240]{1,0:T(8,128)(2,1)S(1)} %shard_map.79.refs_0_), channel_id=1, source_target_pairs={{0,3},{1,2},{2,1},{3,0},{4,7},{5,6},{6,5},{7,4},{8,11},{9,10},{10,... | collective-permute-start | bytes 215048 | tf_op jit(solution)/shard_map/ppermute | solution.py:352
  40.9 2.8 %shard_map.76 = (bf16[440,2240]{1,0:T(8,128)(2,1)S(1)}, bf16[440,2240]{1,0:T(8,128)(2,1)S(1)}) custom-call(bf16[220,2,2240]{2,1,0:T(2,128)(2,1)S(1)} %bitcast.15, bf16[220,2,2240]{2,1,0:T(2,128)(2,1)S(1)} %bitcast.10), custom_call_target="tpu_custom_call" | custom-call | bytes 7884800 | tf_op jit(solution)/shard_map/pallas_call | solution.py:430
  43.8 1.6 %collective-permute-done.5.refs_2_ = bf16[16,2240]{1,0:T(8,128)(2,1)S(1)} collective-permute-done((bf16[16,2240]{1,0:T(8,128)(2,1)S(1)}, bf16[16,2240]{1,0:T(8,128)(2,1)S(1)}, u32[]{:S(2)}, u32[]{:S(2)}) %collective-permute-start.5) | collective-permute-done | bytes 71712 | tf_op jit(solution)/shard_map/ppermute | solution.py:352
  45.4 1.1 %collective-permute-start.11 = (bf16[16,2240]{1,0:T(8,128)(2,1)S(1)}, bf16[16,2240]{1,0:T(8,128)(2,1)S(1)}, u32[]{:S(2)}, u32[]{:S(2)}) collective-permute-start(bf16[16,2240]{1,0:T(8,128)(2,1)S(1)} %shard_map.80.message_ref.refs_0_), channel_id=1, source_target_pairs={{0,24},{4,28},{8,16},{12,20},{16,8},{20,12},{24,0},{28,4},{1,25},{... | collective-permute-start | bytes 215048 | tf_op jit(solution)/shard_map/ppermute | solution.py:352
  46.6 2.3 %collective-permute-start.10 = (bf16[16,2240]{1,0:T(8,128)(2,1)S(1)}, bf16[16,2240]{1,0:T(8,128)(2,1)S(1)}, u32[]{:S(2)}, u32[]{:S(2)}) collective-permute-start(bf16[16,2240]{1,0:T(8,128)(2,1)S(1)} %shard_map.80.message_ref.refs_0_), channel_id=1, source_target_pairs={{0,16},{4,20},{8,24},{12,28},{16,0},{20,4},{24,8},{28,12},{1,17},{... | collective-permute-start | bytes 215048 | tf_op jit(solution)/shard_map/ppermute | solution.py:352
  49.8 4.3 %shard_map.82 = (bf16[440,2240]{1,0:T(8,128)(2,1)S(1)}, bf16[4,16,2240]{2,1,0:T(8,128)(2,1)S(1)}, bf16[4,16,2240]{2,1,0:T(8,128)(2,1)S(1)}) custom-call(s32[1]{0:T(128)} %bitcast.rank_ref, bf16[440,2240]{1,0:T(8,128)(2,1)S(1)} %get-tuple-element.26.queries_ref, bf16[440,2240]{1,0:T(8,128)(2,1)S(1)} %get-tuple-element.27.grad_ref, f32[3,2240]{1,0:T(4,128)S(1)} %copy-done.5, ...), custom_call_target="tpu_custom_call" | custom-call | flops 2018508800 | bytes 7884800 | tf_op jit(solution)/shard_map/pallas_call | solution.py:474
  54.8 1.0 %collective-permute-done.13.got_ref = bf16[4,16,2240]{2,1,0:T(8,128)(2,1)S(1)} collective-permute-done((bf16[4,16,2240]{2,1,0:T(8,128)(2,1)S(1)}, bf16[4,16,2240]{2,1,0:T(8,128)(2,1)S(1)}, u32[]{:S(2)}, u32[]{:S(2)}) %collective-permute-start.13) | collective-permute-done | bytes 286752 | tf_op jit(solution)/shard_map/ppermute | solution.py:352
  55.9 2.0 %collective-permute-start.14 = (bf16[16,2240]{1,0:T(8,128)(2,1)S(1)}, bf16[16,2240]{1,0:T(8,128)(2,1)S(1)}, u32[]{:S(2)}, u32[]{:S(2)}) collective-permute-start(bf16[16,2240]{1,0:T(8,128)(2,1)S(1)} %get-tuple-element.43), channel_id=1, source_target_pairs={{0,8},{4,12},{8,0},{12,4},{16,24},{20,28},{24,16},{28,20},{1,9},{5... | collective-permute-start | bytes 215048 | tf_op jit(solution)/shard_map/ppermute | solution.py:352
  57.9 1.6 %collective-permute-start.16 = (bf16[16,2240]{1,0:T(8,128)(2,1)S(1)}, bf16[16,2240]{1,0:T(8,128)(2,1)S(1)}, u32[]{:S(2)}, u32[]{:S(2)}) collective-permute-start(bf16[16,2240]{1,0:T(8,128)(2,1)S(1)} %get-tuple-element.45), channel_id=1, source_target_pairs={{0,24},{4,28},{8,16},{12,20},{16,8},{20,12},{24,0},{28,4},{1,25},{... | collective-permute-start | bytes 215048 | tf_op jit(solution)/shard_map/ppermute | solution.py:352
  59.5 3.0 %shard_map.84 = (bf16[440,128]{1,0:T(8,128)(2,1)S(1)}, f32[8,2240]{1,0:T(8,128)S(1)}) custom-call(s32[1]{0:T(128)} %bitcast.rank_ref, bf16[440,2240]{1,0:T(8,128)(2,1)S(1)} %get-tuple-element.26.queries_ref, bf16[440,2240]{1,0:T(8,128)(2,1)S(1)} %get-tuple-element.35.numer_ref, f32[440,128]{1,0:T(8,128)S(1)} %get-tuple-element.36.inverse_ref, ...), custom_call_target="tpu_custom_call" | custom-call | flops 1009254400 | bytes 3942400 | tf_op jit(solution)/shard_map/pallas_call | solution.py:485
  62.5 1.2 %collective-permute-done.15.refs_2_ = bf16[16,2240]{1,0:T(8,128)(2,1)S(1)} collective-permute-done((bf16[16,2240]{1,0:T(8,128)(2,1)S(1)}, bf16[16,2240]{1,0:T(8,128)(2,1)S(1)}, u32[]{:S(2)}, u32[]{:S(2)}) %collective-permute-start.15) | collective-permute-done | bytes 71712 | tf_op jit(solution)/shard_map/ppermute | solution.py:352
  63.7 2.6 %collective-permute-start.19 = (bf16[16,2240]{1,0:T(8,128)(2,1)S(1)}, bf16[16,2240]{1,0:T(8,128)(2,1)S(1)}, u32[]{:S(2)}, u32[]{:S(2)}) collective-permute-start(bf16[16,2240]{1,0:T(8,128)(2,1)S(1)} %shard_map.88.refs_0_), channel_id=1, source_target_pairs={{0,3},{1,2},{2,1},{3,0},{4,7},{5,6},{6,5},{7,4},{8,11},{9,10},{10,... | collective-permute-start | bytes 215048 | tf_op jit(solution)/shard_map/ppermute | solution.py:352
  66.3 1.8 %collective-permute-start.17 = (bf16[16,2240]{1,0:T(8,128)(2,1)S(1)}, bf16[16,2240]{1,0:T(8,128)(2,1)S(1)}, u32[]{:S(2)}, u32[]{:S(2)}) collective-permute-start(bf16[16,2240]{1,0:T(8,128)(2,1)S(1)} %shard_map.88.refs_0_), channel_id=1, source_target_pairs={{0,1},{1,0},{2,3},{3,2},{4,5},{5,4},{6,7},{7,6},{8,9},{9,8},{10,11... | collective-permute-start | bytes 215048 | tf_op jit(solution)/shard_map/ppermute | solution.py:352
  68.2 2.5 %collective-permute-done.19.refs_3_ = bf16[16,2240]{1,0:T(8,128)(2,1)S(1)} collective-permute-done((bf16[16,2240]{1,0:T(8,128)(2,1)S(1)}, bf16[16,2240]{1,0:T(8,128)(2,1)S(1)}, u32[]{:S(2)}, u32[]{:S(2)}) %collective-permute-start.19) | collective-permute-done | bytes 71712 | tf_op jit(solution)/shard_map/ppermute | solution.py:352
  70.7 1.6 %collective-permute-done.18.refs_2_ = bf16[16,2240]{1,0:T(8,128)(2,1)S(1)} collective-permute-done((bf16[16,2240]{1,0:T(8,128)(2,1)S(1)}, bf16[16,2240]{1,0:T(8,128)(2,1)S(1)}, u32[]{:S(2)}, u32[]{:S(2)}) %collective-permute-start.18) | collective-permute-done | bytes 71712 | tf_op jit(solution)/shard_map/ppermute | solution.py:352
  72.4 1.6 %collective-permute-start.22 = (bf16[16,2240]{1,0:T(8,128)(2,1)S(1)}, bf16[16,2240]{1,0:T(8,128)(2,1)S(1)}, u32[]{:S(2)}, u32[]{:S(2)}) collective-permute-start(bf16[16,2240]{1,0:T(8,128)(2,1)S(1)} %shard_map.89.refs_0_), channel_id=1, source_target_pairs={{0,24},{4,28},{8,16},{12,20},{16,8},{20,12},{24,0},{28,4},{1,25},{... | collective-permute-start | bytes 215048 | tf_op jit(solution)/shard_map/ppermute | solution.py:352
  74.0 1.4 %collective-permute-start.21 = (bf16[16,2240]{1,0:T(8,128)(2,1)S(1)}, bf16[16,2240]{1,0:T(8,128)(2,1)S(1)}, u32[]{:S(2)}, u32[]{:S(2)}) collective-permute-start(bf16[16,2240]{1,0:T(8,128)(2,1)S(1)} %shard_map.89.refs_0_), channel_id=1, source_target_pairs={{0,16},{4,20},{8,24},{12,28},{16,0},{20,4},{24,8},{28,12},{1,17},{... | collective-permute-start | bytes 215048 | tf_op jit(solution)/shard_map/ppermute | solution.py:352
  75.9 2.5 %collective-permute-done.22.refs_3_ = bf16[16,2240]{1,0:T(8,128)(2,1)S(1)} collective-permute-done((bf16[16,2240]{1,0:T(8,128)(2,1)S(1)}, bf16[16,2240]{1,0:T(8,128)(2,1)S(1)}, u32[]{:S(2)}, u32[]{:S(2)}) %collective-permute-start.22) | collective-permute-done | bytes 71712 | tf_op jit(solution)/shard_map/ppermute | solution.py:352
  79.8 3.1 %shard_map.86 = (bf16[440,2240]{1,0:T(8,128)(2,1)S(1)}, bf16[440,2240]{1,0:T(8,128)(2,1)S(1)}) custom-call(bf16[220,2,2240]{2,1,0:T(2,128)(2,1)S(1)} %bitcast.12, bf16[220,2,2240]{2,1,0:T(2,128)(2,1)S(1)} %bitcast.14), custom_call_target="tpu_custom_call" | custom-call | bytes 7884800 | tf_op jit(solution)/shard_map/pallas_call | solution.py:430
  82.9 3.2 %shard_map.85 = bf16[220,2,2240]{2,1,0:T(2,128)(2,1)} custom-call(s32[1]{0:T(128)} %bitcast.rank_ref, bf16[440,2240]{1,0:T(8,128)(2,1)S(1)} %get-tuple-element.26.queries_ref, bf16[440,2240]{1,0:T(8,128)(2,1)S(1)} %get-tuple-element.35.numer_ref, bf16[440,128]{1,0:T(8,128)(2,1)S(1)} %get-tuple-element.37.sides_ref, ...), custom_call_target="tpu_custom_call" | custom-call | flops 1009254400 | bytes 5913600 | tf_op jit(solution)/shard_map/pallas_call | solution.py:495
  86.1 4.3 %shard_map.91 = (bf16[220,2,2240]{2,1,0:T(2,128)(2,1)}, bf16[220,2,2240]{2,1,0:T(2,128)(2,1)}) custom-call(s32[1]{0:T(128)} %bitcast.rank_ref, bf16[440,2240]{1,0:T(8,128)(2,1)S(1)} %get-tuple-element.38.keys_ref, bf16[440,2240]{1,0:T(8,128)(2,1)S(1)} %get-tuple-element.39.values_ref, bf16[4,16,2240]{2,1,0:T(8,128)(2,1)S(1)} %shard_map.90.own_ref, ...), custom_call_target="tpu_custom_call" | custom-call | flops 2018508800 | bytes 7884800 | tf_op jit(solution)/shard_map/pallas_call | solution.py:499
  (46 shorter events, 6.4 us)
Async XLA Ops:
  0.6 4.6 %copy-start = (bf16[2,220,2240]{2,0,1:T(2,128)(2,1)S(1)}, bf16[2,220,2240]{2,0,1:T(2,128)(2,1)}, u32[]{:S(2)}) copy-start(bf16[2,220,2240]{2,0,1:T(2,128)(2,1)} %param.5) | copy-start | bytes 5913604
  3.9 45.9 %collective-permute-start.8 = (bf16[132,2,2240]{2,1,0:T(2,128)(2,1)}, bf16[132,2,2240]{2,1,0:T(2,128)(2,1)S(1)}, u32[]{:S(2)}, u32[]{:S(2)}) collective-permute-start(bf16[132,2,2240]{2,1,0:T(2,128)(2,1)} %slice.9), channel_id=1, source_target_pairs={{4,0},{8,4},{12,8},{16,12},{20,16},{24,20},{28,24},{5,1},{9,5},{13... | collective-permute-start | bytes 3548168 | tf_op jit(solution)/shard_map/ppermute | solution.py:441
  6.7 43.1 %collective-permute-start.7 = (bf16[88,2,2240]{2,1,0:T(2,128)(2,1)}, bf16[88,2,2240]{2,1,0:T(2,128)(2,1)}, u32[]{:S(2)}, u32[]{:S(2)}) collective-permute-start(bf16[88,2,2240]{2,1,0:T(2,128)(2,1)} %slice.8), channel_id=1, source_target_pairs={{4,0},{8,4},{12,8},{16,12},{20,16},{24,20},{28,24},{5,1},{9,5},{13... | collective-permute-start | bytes 2365448 | tf_op jit(solution)/shard_map/ppermute | solution.py:441
  8.0 32.9 %copy-start.3 = (bf16[2,220,2240]{2,0,1:T(2,128)(2,1)S(1)}, bf16[2,220,2240]{2,0,1:T(2,128)(2,1)}, u32[]{:S(2)}) copy-start(bf16[2,220,2240]{2,0,1:T(2,128)(2,1)} %param.7) | copy-start | bytes 5913604
  12.3 3.2 %collective-permute-start = (bf16[4,16,2240]{2,1,0:T(8,128)(2,1)}, bf16[4,16,2240]{2,1,0:T(8,128)(2,1)S(1)}, u32[]{:S(2)}, u32[]{:S(2)}) collective-permute-start(bf16[4,16,2240]{2,1,0:T(8,128)(2,1)} %get-tuple-element.29), channel_id=1, source_target_pairs={{0,4},{4,0},{8,12},{12,8},{16,20},{20,16},{24,28},{28,24},{1,5},{5... | collective-permute-start | bytes 860168 | tf_op jit(solution)/shard_map/ppermute | solution.py:352
  15.5 1.0 %copy-start.4 = (bf16[4,16,2240]{2,1,0:T(8,128)(2,1)S(1)}, bf16[4,16,2240]{2,1,0:T(8,128)(2,1)}, u32[]{:S(2)}) copy-start(bf16[4,16,2240]{2,1,0:T(8,128)(2,1)} %get-tuple-element.28.own_ref) | copy-start | bytes 860164
  16.6 18.0 %collective-permute-start.1 = (bf16[16,2240]{1,0:T(8,128)(2,1)S(1)}, bf16[16,2240]{1,0:T(8,128)(2,1)S(1)}, u32[]{:S(2)}, u32[]{:S(2)}) collective-permute-start(bf16[16,2240]{1,0:T(8,128)(2,1)S(1)} %get-tuple-element.31), channel_id=1, source_target_pairs={{0,8},{4,12},{8,0},{12,4},{16,24},{20,28},{24,16},{28,20},{1,9},{5... | collective-permute-start | bytes 215048 | tf_op jit(solution)/shard_map/ppermute | solution.py:352
  19.7 15.0 %collective-permute-start.2 = (bf16[16,2240]{1,0:T(8,128)(2,1)S(1)}, bf16[16,2240]{1,0:T(8,128)(2,1)S(1)}, u32[]{:S(2)}, u32[]{:S(2)}) collective-permute-start(bf16[16,2240]{1,0:T(8,128)(2,1)S(1)} %get-tuple-element.32), channel_id=1, source_target_pairs={{0,16},{4,20},{8,24},{12,28},{16,0},{20,4},{24,8},{28,12},{1,17},{... | collective-permute-start | bytes 215048 | tf_op jit(solution)/shard_map/ppermute | solution.py:352
  22.1 14.3 %collective-permute-start.3 = (bf16[16,2240]{1,0:T(8,128)(2,1)S(1)}, bf16[16,2240]{1,0:T(8,128)(2,1)S(1)}, u32[]{:S(2)}, u32[]{:S(2)}) collective-permute-start(bf16[16,2240]{1,0:T(8,128)(2,1)S(1)} %get-tuple-element.33), channel_id=1, source_target_pairs={{0,24},{4,28},{8,16},{12,20},{16,8},{20,12},{24,0},{28,4},{1,25},{... | collective-permute-start | bytes 215048 | tf_op jit(solution)/shard_map/ppermute | solution.py:352
  36.4 7.3 %collective-permute-start.6 = (bf16[16,2240]{1,0:T(8,128)(2,1)S(1)}, bf16[16,2240]{1,0:T(8,128)(2,1)S(1)}, u32[]{:S(2)}, u32[]{:S(2)}) collective-permute-start(bf16[16,2240]{1,0:T(8,128)(2,1)S(1)} %shard_map.79.refs_0_), channel_id=1, source_target_pairs={{0,3},{1,2},{2,1},{3,0},{4,7},{5,6},{6,5},{7,4},{8,11},{9,10},{10,... | collective-permute-start | bytes 215048 | tf_op jit(solution)/shard_map/ppermute | solution.py:352
  40.1 5.3 %collective-permute-start.5 = (bf16[16,2240]{1,0:T(8,128)(2,1)S(1)}, bf16[16,2240]{1,0:T(8,128)(2,1)S(1)}, u32[]{:S(2)}, u32[]{:S(2)}) collective-permute-start(bf16[16,2240]{1,0:T(8,128)(2,1)S(1)} %shard_map.79.refs_0_), channel_id=1, source_target_pairs={{0,2},{1,3},{2,0},{3,1},{4,6},{5,7},{6,4},{7,5},{8,10},{9,11},{10,... | collective-permute-start | bytes 215048 | tf_op jit(solution)/shard_map/ppermute | solution.py:352
  40.1 5.3 %collective-permute-start.4 = (bf16[16,2240]{1,0:T(8,128)(2,1)S(1)}, bf16[16,2240]{1,0:T(8,128)(2,1)S(1)}, u32[]{:S(2)}, u32[]{:S(2)}) collective-permute-start(bf16[16,2240]{1,0:T(8,128)(2,1)S(1)} %shard_map.79.refs_0_), channel_id=1, source_target_pairs={{0,1},{1,0},{2,3},{3,2},{4,5},{5,4},{6,7},{7,6},{8,9},{9,8},{10,11... | collective-permute-start | bytes 215048 | tf_op jit(solution)/shard_map/ppermute | solution.py:352
  43.7 6.1 %copy-start.5 = (f32[3,2240]{1,0:T(4,128)S(1)}, f32[3,2240]{1,0:T(4,128)}, u32[]{:S(2)}) copy-start(f32[3,2240]{1,0:T(4,128)} %taps_ref.1) | copy-start | bytes 80644
  45.4 8.7 %collective-permute-start.11 = (bf16[16,2240]{1,0:T(8,128)(2,1)S(1)}, bf16[16,2240]{1,0:T(8,128)(2,1)S(1)}, u32[]{:S(2)}, u32[]{:S(2)}) collective-permute-start(bf16[16,2240]{1,0:T(8,128)(2,1)S(1)} %shard_map.80.message_ref.refs_0_), channel_id=1, source_target_pairs={{0,24},{4,28},{8,16},{12,20},{16,8},{20,12},{24,0},{28,4},{1,25},{... | collective-permute-start | bytes 215048 | tf_op jit(solution)/shard_map/ppermute | solution.py:352
  46.6 7.6 %collective-permute-start.10 = (bf16[16,2240]{1,0:T(8,128)(2,1)S(1)}, bf16[16,2240]{1,0:T(8,128)(2,1)S(1)}, u32[]{:S(2)}, u32[]{:S(2)}) collective-permute-start(bf16[16,2240]{1,0:T(8,128)(2,1)S(1)} %shard_map.80.message_ref.refs_0_), channel_id=1, source_target_pairs={{0,16},{4,20},{8,24},{12,28},{16,0},{20,4},{24,8},{28,12},{1,17},{... | collective-permute-start | bytes 215048 | tf_op jit(solution)/shard_map/ppermute | solution.py:352
  48.9 5.3 %collective-permute-start.9 = (bf16[16,2240]{1,0:T(8,128)(2,1)S(1)}, bf16[16,2240]{1,0:T(8,128)(2,1)S(1)}, u32[]{:S(2)}, u32[]{:S(2)}) collective-permute-start(bf16[16,2240]{1,0:T(8,128)(2,1)S(1)} %shard_map.80.message_ref.refs_0_), channel_id=1, source_target_pairs={{0,8},{4,12},{8,0},{12,4},{16,24},{20,28},{24,16},{28,20},{1,9},{5... | collective-permute-start | bytes 215048 | tf_op jit(solution)/shard_map/ppermute | solution.py:352
  54.1 1.6 %collective-permute-start.13 = (bf16[4,16,2240]{2,1,0:T(8,128)(2,1)S(1)}, bf16[4,16,2240]{2,1,0:T(8,128)(2,1)S(1)}, u32[]{:S(2)}, u32[]{:S(2)}) collective-permute-start(bf16[4,16,2240]{2,1,0:T(8,128)(2,1)S(1)} %get-tuple-element.41), channel_id=1, source_target_pairs={{0,4},{4,0},{8,12},{12,8},{16,20},{20,16},{24,28},{28,24},{1,5},{5... | collective-permute-start | bytes 860168 | tf_op jit(solution)/shard_map/ppermute | solution.py:352
  54.2 5.2 %collective-permute-start.12 = (bf16[4,16,2240]{2,1,0:T(8,128)(2,1)S(1)}, bf16[4,16,2240]{2,1,0:T(8,128)(2,1)S(1)}, u32[]{:S(2)}, u32[]{:S(2)}) collective-permute-start(bf16[4,16,2240]{2,1,0:T(8,128)(2,1)S(1)} %shard_map.83.refs_0_), channel_id=1, source_target_pairs={{0,4},{4,0},{8,12},{12,8},{16,20},{20,16},{24,28},{28,24},{1,5},{5... | collective-permute-start | bytes 860168 | tf_op jit(solution)/shard_map/ppermute | solution.py:352
  55.9 6.5 %collective-permute-start.14 = (bf16[16,2240]{1,0:T(8,128)(2,1)S(1)}, bf16[16,2240]{1,0:T(8,128)(2,1)S(1)}, u32[]{:S(2)}, u32[]{:S(2)}) collective-permute-start(bf16[16,2240]{1,0:T(8,128)(2,1)S(1)} %get-tuple-element.43), channel_id=1, source_target_pairs={{0,8},{4,12},{8,0},{12,4},{16,24},{20,28},{24,16},{28,20},{1,9},{5... | collective-permute-start | bytes 215048 | tf_op jit(solution)/shard_map/ppermute | solution.py:352
  57.9 5.7 %collective-permute-start.15 = (bf16[16,2240]{1,0:T(8,128)(2,1)S(1)}, bf16[16,2240]{1,0:T(8,128)(2,1)S(1)}, u32[]{:S(2)}, u32[]{:S(2)}) collective-permute-start(bf16[16,2240]{1,0:T(8,128)(2,1)S(1)} %get-tuple-element.44), channel_id=1, source_target_pairs={{0,16},{4,20},{8,24},{12,28},{16,0},{20,4},{24,8},{28,12},{1,17},{... | collective-permute-start | bytes 215048 | tf_op jit(solution)/shard_map/ppermute | solution.py:352
  57.9 5.7 %collective-permute-start.16 = (bf16[16,2240]{1,0:T(8,128)(2,1)S(1)}, bf16[16,2240]{1,0:T(8,128)(2,1)S(1)}, u32[]{:S(2)}, u32[]{:S(2)}) collective-permute-start(bf16[16,2240]{1,0:T(8,128)(2,1)S(1)} %get-tuple-element.45), channel_id=1, source_target_pairs={{0,24},{4,28},{8,16},{12,20},{16,8},{20,12},{24,0},{28,4},{1,25},{... | collective-permute-start | bytes 215048 | tf_op jit(solution)/shard_map/ppermute | solution.py:352
  59.5 20.3 %copy-start.1 = (bf16[2,220,2240]{2,0,1:T(2,128)(2,1)S(1)}, bf16[2,220,2240]{2,0,1:T(2,128)(2,1)}, u32[]{:S(2)}) copy-start(bf16[2,220,2240]{2,0,1:T(2,128)(2,1)} %param.8) | copy-start | bytes 5913604
  59.5 20.3 %copy-start.2 = (bf16[2,220,2240]{2,0,1:T(2,128)(2,1)S(1)}, bf16[2,220,2240]{2,0,1:T(2,128)(2,1)}, u32[]{:S(2)}) copy-start(bf16[2,220,2240]{2,0,1:T(2,128)(2,1)} %param.9) | copy-start | bytes 5913604
  63.7 7.0 %collective-permute-start.19 = (bf16[16,2240]{1,0:T(8,128)(2,1)S(1)}, bf16[16,2240]{1,0:T(8,128)(2,1)S(1)}, u32[]{:S(2)}, u32[]{:S(2)}) collective-permute-start(bf16[16,2240]{1,0:T(8,128)(2,1)S(1)} %shard_map.88.refs_0_), channel_id=1, source_target_pairs={{0,3},{1,2},{2,1},{3,0},{4,7},{5,6},{6,5},{7,4},{8,11},{9,10},{10,... | collective-permute-start | bytes 215048 | tf_op jit(solution)/shard_map/ppermute | solution.py:352
  66.3 6.0 %collective-permute-start.18 = (bf16[16,2240]{1,0:T(8,128)(2,1)S(1)}, bf16[16,2240]{1,0:T(8,128)(2,1)S(1)}, u32[]{:S(2)}, u32[]{:S(2)}) collective-permute-start(bf16[16,2240]{1,0:T(8,128)(2,1)S(1)} %shard_map.88.refs_0_), channel_id=1, source_target_pairs={{0,2},{1,3},{2,0},{3,1},{4,6},{5,7},{6,4},{7,5},{8,10},{9,11},{10,... | collective-permute-start | bytes 215048 | tf_op jit(solution)/shard_map/ppermute | solution.py:352
  66.3 6.0 %collective-permute-start.17 = (bf16[16,2240]{1,0:T(8,128)(2,1)S(1)}, bf16[16,2240]{1,0:T(8,128)(2,1)S(1)}, u32[]{:S(2)}, u32[]{:S(2)}) collective-permute-start(bf16[16,2240]{1,0:T(8,128)(2,1)S(1)} %shard_map.88.refs_0_), channel_id=1, source_target_pairs={{0,1},{1,0},{2,3},{3,2},{4,5},{5,4},{6,7},{7,6},{8,9},{9,8},{10,11... | collective-permute-start | bytes 215048 | tf_op jit(solution)/shard_map/ppermute | solution.py:352
  72.4 6.1 %collective-permute-start.22 = (bf16[16,2240]{1,0:T(8,128)(2,1)S(1)}, bf16[16,2240]{1,0:T(8,128)(2,1)S(1)}, u32[]{:S(2)}, u32[]{:S(2)}) collective-permute-start(bf16[16,2240]{1,0:T(8,128)(2,1)S(1)} %shard_map.89.refs_0_), channel_id=1, source_target_pairs={{0,24},{4,28},{8,16},{12,20},{16,8},{20,12},{24,0},{28,4},{1,25},{... | collective-permute-start | bytes 215048 | tf_op jit(solution)/shard_map/ppermute | solution.py:352
  74.0 4.8 %collective-permute-start.21 = (bf16[16,2240]{1,0:T(8,128)(2,1)S(1)}, bf16[16,2240]{1,0:T(8,128)(2,1)S(1)}, u32[]{:S(2)}, u32[]{:S(2)}) collective-permute-start(bf16[16,2240]{1,0:T(8,128)(2,1)S(1)} %shard_map.89.refs_0_), channel_id=1, source_target_pairs={{0,16},{4,20},{8,24},{12,28},{16,0},{20,4},{24,8},{28,12},{1,17},{... | collective-permute-start | bytes 215048 | tf_op jit(solution)/shard_map/ppermute | solution.py:352
  75.4 4.4 %collective-permute-start.20 = (bf16[16,2240]{1,0:T(8,128)(2,1)S(1)}, bf16[16,2240]{1,0:T(8,128)(2,1)S(1)}, u32[]{:S(2)}, u32[]{:S(2)}) collective-permute-start(bf16[16,2240]{1,0:T(8,128)(2,1)S(1)} %shard_map.89.refs_0_), channel_id=1, source_target_pairs={{0,8},{4,12},{8,0},{12,4},{16,24},{20,28},{24,16},{28,20},{1,9},{5... | collective-permute-start | bytes 215048 | tf_op jit(solution)/shard_map/ppermute | solution.py:352
  79.7 6.4 %collective-permute-start.23 = (bf16[4,16,2240]{2,1,0:T(8,128)(2,1)S(1)}, bf16[4,16,2240]{2,1,0:T(8,128)(2,1)S(1)}, u32[]{:S(2)}, u32[]{:S(2)}) collective-permute-start(bf16[4,16,2240]{2,1,0:T(8,128)(2,1)S(1)} %shard_map.90.own_ref), channel_id=1, source_target_pairs={{0,4},{4,0},{8,12},{12,8},{16,20},{20,16},{24,28},{28,24},{1,5},{5... | collective-permute-start | bytes 860168 | tf_op jit(solution)/shard_map/ppermute | solution.py:352
